TPU v7x, 256 devices: a whole 4x4x8 slice. The times are simulated.
256 devices in a mesh: bl: 32 (over z, x), ch: 8 (over y, core).
Axes of the slice: x: 4, y: 4, z: 8, core: 2. Of those that a mesh axis runs over, the one named last changes fastest.
Arguments:
- visibility: float32 [2, 2048, 64, 128], P(None, 'bl', 'ch'), may hold values from -3 to 3
- coordinates: float32 [2, 2048, 128], P(None, 'bl'), may hold values from -10 to 10
- freq_ratio: float32 [64], P('ch'), may hold values from 0.75 to 1.25
- aterms: float32 [512, 2048], P('bl'), may hold values from -4 to 4
- stations: int32 [2048, 2], P('bl'), may hold values from 0 to 511
- sub_tile: int32 [2048], P('bl'), may hold values from 0 to 31, as said below
- offsets: int32 [2048, 2], P('bl'), may hold values from 0 to 224
- tile_of_slot: int32 [32], replicated, may hold values from 0 to 31, each once
Outputs:
- grid_tiles: float32 [32, 256, 4, 256], P('bl', 'ch')
Inputs may be any that keep to these rules, and one draw needn't show every extreme that they name: `sub_tile`: within the rows of one device of bl no tile number appears more than 8 times, and one tile number, common to all devices, appears exactly 8 times in the rows of every device. `tile_of_slot`: each tile number appears once.
All inputs are finite; a program needn't handle non-finite values.
Results may differ from a plain program's by a relative error of at most 0.000098.
Values sent between devices are 32-bit elements; how exact they have to be, the bound alone decides.
No kernel may reach another device: no remote copies, remote signals or barrier semaphores. Data moves between devices by JAX's collectives and lax.ppermute only.
A program may use at most 128 MiB of HBM per device.

v0:
```python
import functools
import math

import jax
import jax.numpy as jnp
import numpy as np
from jax import lax
from jax.experimental import pallas as pl
from jax.experimental.pallas import tpu as pltpu
from jax.sharding import PartitionSpec as P

SUB = 32
TILE = 256
F32 = jnp.float32
BF16 = jnp.bfloat16
VM = pl.BlockSpec(memory_space=pltpu.VMEM)
SM = pl.BlockSpec(memory_space=pltpu.SMEM)

INV, TILES, ST0, ST1, OFF0, OFF1, OWN, ME = 0, 64, 128, 192, 256, 320, 384, 416

SIN = [(-1.0) ** k / math.factorial(2 * k + 1) for k in range(7)]
COS = [(-1.0) ** k / math.factorial(2 * k) for k in range(7)]


def poly(coefs, x2):
    r = jnp.full_like(x2, coefs[-1])
    for k in coefs[-2::-1]:
        r = r * x2 + k
    return r


def split(x):
    hi = x.astype(BF16)
    return hi, (x - hi.astype(F32)).astype(BF16)


def np_split(x):
    x = np.asarray(x, np.float64)
    hi = x.astype(np.float32).astype(BF16)
    lo = (x - hi.astype(np.float64)).astype(np.float32).astype(BF16)
    return hi, lo


def constants():
    pix = np.concatenate([16 + np.arange(16), 15 - np.arange(16)])
    m1 = np.zeros((2, 2, 2, 16, 2, 2, 32))
    m2 = np.zeros_like(m1)
    for b in range(32):
        n, sign = (b - 16, 1.0) if b >= 16 else (15 - b, -1.0)
        for k in range(2):
            for part in range(2):
                m1[k, part, 0, n, 0, k, b] = 1.0
                m1[k, part, 1, n, 1, k, b] = sign
                m2[k, part, 1, n, 0, k, b] = -sign
                m2[k, part, 0, n, 1, k, b] = 1.0
    to_image = np.concatenate([m1.reshape(128, 128), m2.reshape(128, 128)], 0)
    fold = np.zeros((2, 128, 128))
    for lane in range(128):
        for g in range(4):
            fold[0, lane, g * 32 + lane % 32] = 1.0
            fold[1, lane, g * 32 + lane % 32] = -1.0 if g < 2 else 1.0
    centred = np.arange(32) - 16
    four = np.exp(-2j * np.pi * centred[:, None] * centred[None, :] / 32) / 32
    left = np.concatenate([four.real[:, pix], four.imag[:, pix]], 1)
    lh, ll = np_split(left)
    left3 = np.concatenate([lh, ll, lh], 1)
    d = np.zeros((2, 2, 32, 2, 2, 32))
    for k in range(2):
        d[0, k, :, k, 0, :] = four.real.T
        d[1, k, :, k, 0, :] = -four.imag.T
        d[0, k, :, k, 1, :] = four.imag.T
        d[1, k, :, k, 1, :] = four.real.T
    dh, dl = np_split(d.reshape(128, 128))
    right3 = np.concatenate([dh, dl, dh], 0)
    line = np.sin(np.pi * (np.arange(32) + 0.5) / 32)
    taper = (line[:, None] * line[None, :]).reshape(8, 128).astype(np.float32)
    return (
        to_image.astype(BF16),
        fold.astype(BF16),
        left3.astype(BF16),
        right3.astype(BF16),
        taper,
    )


def pack_kernel(ints, freq, vis, coord, aterms, *outs):
    chunks, uv, shared = outs[:8], outs[8], outs[9]
    own = outs[10]
    me = ints[ME]
    y = me // 2
    core = me % 2
    row = lax.broadcasted_iota(jnp.int32, (8, 128), 0)
    lane = lax.broadcasted_iota(jnp.int32, (8, 128), 1)
    freqs = jnp.zeros((8, 128), F32)
    for k in range(8):
        freqs = jnp.where(row == k, freq[k], freqs)
    for q in range(8):
        to = ((y + q // 2) % 4) * 2 + (core + q % 2) % 2
        for j in range(8):
            s = ints[INV + 8 * j + to]
            chunks[q][j] = vis[0, s]
            chunks[q][8 + j] = vis[1, s]
        chunks[q][16] = freqs
    for n in range(32):
        own[ints[OWN + n]] = n
    blank = jnp.zeros((8, 128), F32)
    re = aterms[:, pl.ds(pl.multiple_of(me * 128, 128), 128)]
    im = aterms[:, pl.ds(pl.multiple_of(1024 + me * 128, 128), 128)]
    for b in range(32):
        shared[b, 0:16, :] = re
        shared[b, 16:32, :] = im
        shared[b, 32:40, :] = blank
    for j in range(8):
        s = ints[INV + 8 * j + me]
        for d in range(2):
            uv[d, pl.ds(j, 1), :] = coord[d, pl.ds(s, 1), :]
        spot = jnp.where(lane == 0, ints[OFF0 + s], jnp.where(lane == 1, ints[OFF1 + s], 0))
        shared[own[ints[TILES + s]], 32:40, :] = spot.astype(F32)


def image_kernel(count, first, uv, *refs):
    vis = refs[:count]
    refs = refs[count:]
    if not first:
        before = refs[0]
        refs = refs[1:]
    out, xu, xv, vp, lk, rk = refs
    for n in range(count):
        vref = vis[n]
        f = vref[16]
        weight = 4.0 * (f - 1.0)
        step = f * (math.pi / SUB)
        for s in range(8):
            base = []
            for d, table in ((0, xu), (1, xv)):
                phi = uv[d, pl.ds(s, 1), :] * step
                x2 = phi * phi
                zr = poly(COS, x2)
                zi = phi * poly(SIN, x2)
                wr = zr * zr - zi * zi
                wi = 2.0 * zr * zi
                cr, ci = zr, zi
                for m in range(16):
                    table[s, pl.ds(m * 8, 8), :] = cr
                    table[s, pl.ds((16 + m) * 8, 8), :] = ci
                    if m < 15:
                        cr, ci = cr * wr - ci * wi, cr * wi + ci * wr
                base.append((zr, zi))
            (ar, ai), (br, bi) = base
            pr = ar * br - ai * bi
            pi = ar * bi + ai * br
            vr = vref[s]
            vi = vref[8 + s]
            vp[s, 0] = vr * pr + vi * pi
            vp[s, 1] = vi * pr - vr * pi
        for s in range(8):
            for c in range(8):
                xs = xu[s, pl.ds(c, 32, stride=8), :]
                ys = xv[s, pl.ds(c, 32, stride=8), :]
                vr = vp[s, 0, pl.ds(c, 1), :]
                vi = vp[s, 1, pl.ds(c, 1), :]
                lh, ll = split(jnp.concatenate([xs * vr, xs * vi], 0))
                lk[s % 2, :, pl.ds(c * 256, 128)] = lh
                lk[s % 2, :, pl.ds(c * 256 + 128, 128)] = ll
                yh, yl = split(ys)
                wh, wl = split(ys * weight[c : c + 1])
                r4 = jnp.concatenate([yh, yl, wh, wl], 0)
                rk[s % 2, :, pl.ds(c * 256, 128)] = r4
                rk[s % 2, :, pl.ds(c * 256 + 128, 128)] = r4
            o = lax.dot_general(
                lk[s % 2], rk[s % 2], (((1,), (1,)), ((), ())), preferred_element_type=F32
            )
            if n == 0:
                out[s] = o if first else before[s] + o
            else:
                out[s] += o


def images(uv, chunks, before=None):
    count = len(chunks)
    first = before is None
    args = [uv, *chunks] + ([] if first else [before])
    return pl.pallas_call(
        functools.partial(image_kernel, count, first),
        out_shape=jax.ShapeDtypeStruct((8, 64, 128), F32),
        in_specs=[VM] * len(args),
        out_specs=VM,
        scratch_shapes=[
            pltpu.VMEM((8, 256, 128), F32),
            pltpu.VMEM((8, 256, 128), F32),
            pltpu.VMEM((8, 2, 8, 128), F32),
            pltpu.VMEM((2, 64, 2048), BF16),
            pltpu.VMEM((2, 128, 2048), BF16),
        ],
        cost_estimate=pl.CostEstimate(
            flops=count * 60_000_000, bytes_accessed=count * 100_000, transcendentals=0
        ),
        name=f"image{count}",
    )(*args)


def pair_kernel(ints, table, taper, out):
    me = ints[ME]
    g = taper[pl.ds(me, 1), :]
    for to in range(8):
        for j in range(8):
            s = ints[INV + 8 * j + to]
            p = ints[ST0 + s]
            q = ints[ST1 + s]
            pr = table[p // 16, pl.ds(p % 16, 1), :]
            pi = table[p // 16, pl.ds(16 + p % 16, 1), :]
            qr = table[q // 16, pl.ds(q % 16, 1), :]
            qi = table[q // 16, pl.ds(16 + q % 16, 1), :]
            out[to, pl.ds(j, 1), :] = (pr * qr + pi * qi) * g
            out[to, pl.ds(8 + j, 1), :] = (pi * qr - pr * qi) * g


def finish_kernel(ints, acc, pair, to_image, fold, left3, right3, out, own):
    me = ints[ME]
    for n in range(32):
        own[ints[OWN + n]] = n
    blank = jnp.zeros((32, 128), F32)
    for b in range(32):
        out[b] = blank
    row = lax.broadcasted_iota(jnp.int32, (8, 128), 0)
    group = lax.broadcasted_iota(jnp.int32, (8, 128), 1) // 32
    low = group == row % 4
    high = group == 3 - row % 4
    spread = [[], []]
    halves = []
    for s in range(8):
        for r in range(2):
            rows = [jnp.broadcast_to(pair[c, pl.ds(8 * r + s, 1), :], (8, 128)) for c in range(8)]
            for c in (4, 6):
                spread[r].append(jnp.where(low, jnp.where(row < 4, rows[c], rows[c + 1]), 0.0))
            for c in (3, 1):
                spread[r].append(jnp.where(high, jnp.where(row < 4, rows[c], rows[c - 1]), 0.0))
        g = acc[s]
        rc, rs, ic, js = g[0:16], g[16:32], g[32:48], g[48:64]
        real = jnp.concatenate([rc - js, rc + js], 0)
        imag = jnp.concatenate([ic + rs, ic - rs], 0)
        halves.append(jnp.concatenate([real, imag], 1))
    stack = jnp.concatenate(halves, 0)
    sh, sl = split(stack)
    img = jnp.dot(sh, to_image[...], preferred_element_type=F32) + jnp.dot(
        sl, to_image[...], preferred_element_type=F32
    )

    def unfold(r):
        h, l = split(jnp.concatenate(spread[r], 0))
        return jnp.dot(h, fold[r], preferred_element_type=F32) + jnp.dot(
            l, fold[r], preferred_element_type=F32
        )

    weighted = img * unfold(0) + pltpu.roll(img, 64, 1) * unfold(1)
    sign = jnp.where(lax.broadcasted_iota(jnp.int32, (256, 128), 1) < 64, -1.0, 1.0)
    turned = pltpu.roll(weighted, 64, 1) * sign
    wh, wl = split(weighted)
    th, tl = split(turned)

    def lanes(x):
        return jnp.concatenate([x[32 * s : 32 * s + 32] for s in range(8)], 1)

    wh, wl, th, tl = lanes(wh), lanes(wl), lanes(th), lanes(tl)
    rhs = jnp.concatenate([wh, th, wh, th, wl, tl], 0)
    half = jnp.dot(left3[...], rhs, preferred_element_type=F32)
    half = jnp.concatenate([half[:, 128 * s : 128 * s + 128] for s in range(8)], 0)
    hh, hl = split(half)
    full = jnp.dot(
        jnp.concatenate([hh, hh, hl], 1), right3[...], preferred_element_type=F32
    )
    for s in range(8):
        out[own[ints[TILES + ints[INV + 8 * s + me]]]] = full[32 * s : 32 * s + 32]


def place_kernel(spots, me_ref, arrived, keep, give, acc):
    lane = lax.broadcasted_iota(jnp.int32, (32, 128), 1)
    me = me_ref[0]
    y = me // 2
    core = me % 2
    acc[...] = jnp.zeros_like(acc)

    def one(i, unused):
        r = spots[2 * i]
        c = spots[2 * i + 1]
        tile = arrived[i]
        near = (lane >= c) & (lane < c + 32)
        far = (lane + 128 >= c) & (lane + 128 < c + 32)
        for m in range(4):
            moved = pltpu.roll(tile, (c - 32 * m + 128) % 128, 1)
            for half, mask in ((0, near), (1, far)):
                at = (2 * m + half, pl.ds(r, 32), slice(None))
                acc[at] = acc[at] + jnp.where(mask, moved, 0.0)
        return unused

    lax.fori_loop(0, 32, one, 0)
    for d in range(4):
        block = ((y + d) % 4) * 2
        for k in range(8):
            keep[d, k] = acc[k, pl.ds(pl.multiple_of((block + core) * 32, 32), 32), :]
            give[d, k] = acc[k, pl.ds(pl.multiple_of((block + 1 - core) * 32, 32), 32), :]


def merge_kernel(keep, got, *outs):
    for d in range(4):
        outs[d][...] = keep[d] + got[d]


def last_kernel(a, b, c, d, out):
    for m in range(4):
        for half in range(2):
            k = 2 * m + half
            out[0, :, m, 128 * half : 128 * half + 128] = (a[k] + b[k]) + (c[k] + d[k])


def shift(x, dy, dc):
    pairs = [(i, ((i // 2 + dy) % 4) * 2 + (i + dc) % 2) for i in range(8)]
    return lax.ppermute(x, "ch", pairs)


def local(visibility, coordinates, freq_ratio, aterms, stations, sub_tile, offsets, tile_of_slot):
    to_image, fold, left3, right3, taper = constants()
    me = lax.axis_index("ch").astype(jnp.int32)
    order = jnp.arange(64, dtype=jnp.int32)
    key = sub_tile * 64 + order
    pos = jnp.sum((key[None, :] < key[:, None]).astype(jnp.int32), axis=1)
    inv = jnp.sum(jnp.where(pos[None, :] == order[:, None], order[None, :], 0), axis=1)
    ints = jnp.concatenate(
        [
            inv,
            sub_tile,
            stations[:, 0],
            stations[:, 1],
            offsets[:, 0],
            offsets[:, 1],
            tile_of_slot,
            me[None],
        ]
    )
    packed = pl.pallas_call(
        pack_kernel,
        out_shape=[jax.ShapeDtypeStruct((17, 8, 128), F32)] * 8
        + [jax.ShapeDtypeStruct((2, 8, 128), F32), jax.ShapeDtypeStruct((32, 40, 128), F32)],
        in_specs=[SM, SM, VM, VM, VM],
        out_specs=[VM] * 10,
        scratch_shapes=[pltpu.SMEM((32,), jnp.int32)],
        name="pack",
    )(ints, freq_ratio, visibility, coordinates, aterms)
    chunks, uv, shared = packed[:8], packed[8], packed[9]
    moved = [shift(chunks[q], q // 2, q % 2) for q in range(1, 8)]
    table = lax.all_to_all(shared.reshape(32, 40 * 128), "bl", 0, 0, tiled=True)
    table = table.reshape(32, 40, 128)
    acc = images(uv, [chunks[0]])
    acc = images(uv, [moved[0]], acc)
    acc = images(uv, [moved[1], moved[2], moved[5], moved[6]], acc)
    pair = pl.pallas_call(
        pair_kernel,
        out_shape=jax.ShapeDtypeStruct((8, 16, 128), F32),
        in_specs=[SM, VM, VM],
        out_specs=VM,
        name="pair",
    )(ints, table, taper)
    pair = lax.all_to_all(pair.reshape(8, 2048), "ch", 0, 0, tiled=True).reshape(8, 16, 128)
    acc = images(uv, [moved[3], moved[4]], acc)
    outgoing = pl.pallas_call(
        finish_kernel,
        out_shape=jax.ShapeDtypeStruct((32, 32, 128), F32),
        in_specs=[SM] + [VM] * 6,
        out_specs=VM,
        scratch_shapes=[pltpu.SMEM((32,), jnp.int32)],
        name="finish",
    )(ints, acc, pair, to_image, fold, left3, right3)
    arrived = lax.all_to_all(outgoing.reshape(32, 4096), "bl", 0, 0, tiled=True)
    arrived = arrived.reshape(32, 32, 128)
    spots = table[:, 32, 0:2].reshape(64).astype(jnp.int32)
    half = jax.ShapeDtypeStruct((4, 8, 32, 128), F32)
    keep, give = pl.pallas_call(
        place_kernel,
        out_shape=[half, half],
        in_specs=[SM, SM, VM],
        out_specs=[VM, VM],
        scratch_shapes=[pltpu.VMEM((8, TILE, 128), F32)],
        name="place",
    )(spots, me[None], arrived)
    got = shift(give, 0, 1)
    block = jax.ShapeDtypeStruct((8, 32, 128), F32)
    sums = pl.pallas_call(
        merge_kernel,
        out_shape=[block] * 4,
        in_specs=[VM, VM],
        out_specs=[VM] * 4,
        name="merge",
    )(keep, got)
    parts = [sums[0]] + [shift(sums[d], d, 0) for d in range(1, 4)]
    return pl.pallas_call(
        last_kernel,
        out_shape=jax.ShapeDtypeStruct((1, 32, 4, TILE), F32),
        in_specs=[VM] * 4,
        out_specs=VM,
        name="last",
    )(*parts)


def solution(mesh):
    placed = (
        P(None, "bl", "ch", None),
        P(None, "bl", None),
        P("ch"),
        P("bl", None),
        P("bl", None),
        P("bl"),
        P("bl", None),
        P(),
    )
    return jax.shard_map(
        local, mesh=mesh, in_specs=placed, out_specs=P("bl", "ch", None, None), check_vma=False
    )
```

profile of v0, /device:TPU:1, one launch (start us, length us, event | category | flops | bytes accessed | tf_op | source)
XLA Modules:
  0.0 122.8 jit_solution(14199729653026796896)
XLA Ops:
  2.2 0.7 concatenate.3.ints
  2.9 2.3 %pack.1 = (f32[17,8,128]{2,1,0:T(8,128)}, f32[17,8,128]{2,1,0:T(8,128)}, f32[17,8,128]{2,1,0:T(8,128)}, f32[17,8,128]{2,1,0:T(8,128)}, f32[17,8,128]{2,1,0:T(8,1...) custom-call(s32[417]{0:T(512)} %concatenate.3.ints, ...), custom_call_target="tpu_custom_call" | custom-call | tf_op jit(solution)/shard_map/pack/pallas_call | solution.py:340
  5.2 12.0 %all-to-all-start = ((f32[32,1,5120]{2,1,0:T(1,128)}), f32[32,1,5120]{2,1,0:T(1,128)S(1)}, u32[]{:S(2)}, u32[]{:S(2)}) async-start(f32[32,1,5120]{2,1,0:T(1,128)} %bitcast.19), calls=%async_computation | async-start | bytes 1310720 | tf_op jit(solution)/shard_map/all_to_all | solution.py:351
  17.2 1.0 collective-permute-start.6
  18.3 1.3 %collective-permute-start.2 = (f32[17,8,128]{2,1,0:T(8,128)S(1)}, f32[17,8,128]{2,1,0:T(8,128)S(1)}, u32[]{:S(2)}, u32[]{:S(2)}) collective-permute-start(f32[17,8,128]{2,1,0:T(8,128)S(1)} %copy-done.23), channel_id=1, source_target_pairs={{0,2},{1,3},{2,4},{3,5},{4,6},{5,7},{6,0},{7,1},{8,10},{9,11},{10,... | collective-permute-start | bytes 208904 | tf_op jit(solution)/shard_map/ppermute | solution.py:318
  19.6 1.6 %collective-permute-start.3 = (f32[17,8,128]{2,1,0:T(8,128)S(1)}, f32[17,8,128]{2,1,0:T(8,128)S(1)}, u32[]{:S(2)}, u32[]{:S(2)}) collective-permute-start(f32[17,8,128]{2,1,0:T(8,128)S(1)} %copy-done.18), channel_id=1, source_target_pairs={{0,3},{1,2},{2,5},{3,4},{4,7},{5,6},{6,1},{7,0},{8,11},{9,10},{10,... | collective-permute-start | bytes 208904 | tf_op jit(solution)/shard_map/ppermute | solution.py:318
  21.2 1.4 %collective-permute-start.4 = (f32[17,8,128]{2,1,0:T(8,128)S(1)}, f32[17,8,128]{2,1,0:T(8,128)S(1)}, u32[]{:S(2)}, u32[]{:S(2)}) collective-permute-start(f32[17,8,128]{2,1,0:T(8,128)S(1)} %copy-done.17), channel_id=1, source_target_pairs={{0,6},{1,7},{2,0},{3,1},{4,2},{5,3},{6,4},{7,5},{8,14},{9,15},{10,... | collective-permute-start | bytes 208904 | tf_op jit(solution)/shard_map/ppermute | solution.py:318
  23.2 1.6 %collective-permute-start = (f32[17,8,128]{2,1,0:T(8,128)S(1)}, f32[17,8,128]{2,1,0:T(8,128)S(1)}, u32[]{:S(2)}, u32[]{:S(2)}) collective-permute-start(f32[17,8,128]{2,1,0:T(8,128)S(1)} %copy-done.15), channel_id=1, source_target_pairs={{0,4},{1,5},{2,6},{3,7},{4,0},{5,1},{6,2},{7,3},{8,12},{9,13},{10,... | collective-permute-start | bytes 208904 | tf_op jit(solution)/shard_map/ppermute | solution.py:318
  24.8 1.6 %collective-permute-start.1 = (f32[17,8,128]{2,1,0:T(8,128)S(1)}, f32[17,8,128]{2,1,0:T(8,128)S(1)}, u32[]{:S(2)}, u32[]{:S(2)}) collective-permute-start(f32[17,8,128]{2,1,0:T(8,128)S(1)} %copy-done.14), channel_id=1, source_target_pairs={{0,5},{1,4},{2,7},{3,6},{4,1},{5,0},{6,3},{7,2},{8,13},{9,12},{10,... | collective-permute-start | bytes 208904 | tf_op jit(solution)/shard_map/ppermute | solution.py:318
  26.4 9.5 %all-to-all-done = f32[32,1,5120]{2,1,0:T(1,128)S(1)} async-done(((f32[32,1,5120]{2,1,0:T(1,128)}), f32[32,1,5120]{2,1,0:T(1,128)S(1)}, u32[]{:S(2)}, u32[]{:S(2)}) %all-to-all-start) | async-done | bytes 655392 | tf_op jit(solution)/shard_map/all_to_all | solution.py:351
  35.9 0.8 copy-done
  36.8 2.6 %pair.1 = f32[8,16,128]{2,1,0:T(8,128)} custom-call(s32[417]{0:T(512)} %concatenate.3.ints, f32[32,40,128]{2,1,0:T(8,128)} %bitcast.15, f32[8,128]{1,0:T(8,128)} %constant.18.clone.taper), custom_call_target="tpu_custom_call" | custom-call | tf_op jit(solution)/shard_map/pair/pallas_call | solution.py:356
  39.3 7.0 %all-to-all-start.1 = ((f32[8,1,2048]{2,1,0:T(1,128)}), f32[8,1,2048]{2,1,0:T(1,128)S(1)}, u32[]{:S(2)}, u32[]{:S(2)}) async-start(f32[8,1,2048]{2,1,0:T(1,128)} %bitcast.21), calls=%async_computation.1 | async-start | bytes 131072 | tf_op jit(solution)/shard_map/all_to_all | solution.py:363
  46.3 4.0 %image1.2.refs_1_ = f32[8,64,128]{2,1,0:T(8,128)} custom-call(f32[2,8,128]{2,1,0:T(8,128)} %get-tuple-element.22.uv, f32[17,8,128]{2,1,0:T(8,128)} %get-tuple-element.30.refs_0_), custom_call_target="tpu_custom_call" | custom-call | flops 60000000 | bytes 100000 | tf_op jit(solution)/shard_map/image1/pallas_call | solution.py:183
  50.3 4.2 %image1.3.refs_4_ = f32[8,64,128]{2,1,0:T(8,128)} custom-call(f32[2,8,128]{2,1,0:T(8,128)} %get-tuple-element.22.uv, f32[17,8,128]{2,1,0:T(8,128)} %copy-done.7, f32[8,64,128]{2,1,0:T(8,128)} %image1.2.refs_1_), custom_call_target="tpu_custom_call" | custom-call | flops 60000000 | bytes 100000 | tf_op jit(solution)/shard_map/image1/pallas_call | solution.py:183
  55.7 9.8 %image4.1.refs_2_ = f32[8,64,128]{2,1,0:T(8,128)} custom-call(f32[2,8,128]{2,1,0:T(8,128)} %get-tuple-element.22.uv, f32[17,8,128]{2,1,0:T(8,128)} %copy-done.19, f32[17,8,128]{2,1,0:T(8,128)} %copy-done.20, f32[17,8,128]{2,1,0:T(8,128)} %copy-done.21, f32[17,8,128]{2,1,0:T(8,128)} %copy-done.22, f32[8,64,128]{2,1,0:T(8,128)} %image1.3.refs_4_), custom_call_target="tpu_custom_call" | custom-call | flops 240000000 | bytes 400000 | tf_op jit(solution)/shard_map/image4/pallas_call | solution.py:183
  66.8 6.2 %image2.1.acc = f32[8,64,128]{2,1,0:T(8,128)} custom-call(f32[2,8,128]{2,1,0:T(8,128)} %get-tuple-element.22.uv, f32[17,8,128]{2,1,0:T(8,128)} %copy-done.8, f32[17,8,128]{2,1,0:T(8,128)} %copy-done.9, f32[8,64,128]{2,1,0:T(8,128)} %image4.1.refs_2_), custom_call_target="tpu_custom_call" | custom-call | flops 120000000 | bytes 200000 | tf_op jit(solution)/shard_map/image2/pallas_call | solution.py:183
  73.7 2.6 %finish.1 = f32[32,32,128]{2,1,0:T(8,128)} custom-call(s32[417]{0:T(512)} %concatenate.3.ints, f32[8,64,128]{2,1,0:T(8,128)} %image2.1.acc, f32[8,16,128]{2,1,0:T(8,128)} %bitcast.20, bf16[256,128]{1,0:T(8,128)(2,1)} %constant.19.clone.to_image, bf16[2,128,128]{2,1,0:T(8,128)(2,1)} %constant.20.clone.fold, bf16[32,192]{1,0:T(8,128)(2,1)} %constant.21.clone.left3, ...), custom_call_target="tpu_custom_call" | custom-call | tf_op jit(solution)/shard_map/finish/pallas_call | solution.py:365
  76.3 4.7 %all-to-all-start.2 = ((f32[32,1,4096]{2,1,0:T(1,128)}), f32[32,1,4096]{2,1,0:T(1,128)S(1)}, u32[]{:S(2)}, u32[]{:S(2)}) async-start(f32[32,1,4096]{2,1,0:T(1,128)} %bitcast.18), calls=%async_computation.2 | async-start | bytes 1048576 | tf_op jit(solution)/shard_map/all_to_all | solution.py:373
  81.0 1.0 fusion
  82.6 15.1 %all-to-all-done.2 = f32[32,1,4096]{2,1,0:T(1,128)S(1)} async-done(((f32[32,1,4096]{2,1,0:T(1,128)}), f32[32,1,4096]{2,1,0:T(1,128)S(1)}, u32[]{:S(2)}, u32[]{:S(2)}) %all-to-all-start.2) | async-done | bytes 524320 | tf_op jit(solution)/shard_map/all_to_all | solution.py:373
  97.7 0.8 copy-done.1
  98.5 4.9 %place.1 = (f32[4,8,32,128]{3,2,1,0:T(8,128)}, f32[4,8,32,128]{3,2,1,0:T(8,128)}) custom-call(s32[64]{0:T(128)} %convert_element_type.10.spots, s32[1]{0:T(128)} %bitcast.4.me_ref, f32[32,32,128]{2,1,0:T(8,128)} %bitcast.17), custom_call_target="tpu_custom_call" | custom-call | tf_op jit(solution)/shard_map/place/pallas_call | solution.py:377
  103.5 2.0 %collective-permute-start.7 = (f32[4,8,32,128]{3,2,1,0:T(8,128)}, f32[4,8,32,128]{3,2,1,0:T(8,128)S(1)}, u32[]{:S(2)}, u32[]{:S(2)}) collective-permute-start(f32[4,8,32,128]{3,2,1,0:T(8,128)} %get-tuple-element.32), channel_id=1, source_target_pairs={{0,1},{1,0},{2,3},{3,2},{4,5},{5,4},{6,7},{7,6},{8,9},{9,8},{10,11... | collective-permute-start | bytes 1572872 | tf_op jit(solution)/shard_map/ppermute | solution.py:318
  105.5 1.7 %collective-permute-done.7.got = f32[4,8,32,128]{3,2,1,0:T(8,128)S(1)} collective-permute-done((f32[4,8,32,128]{3,2,1,0:T(8,128)}, f32[4,8,32,128]{3,2,1,0:T(8,128)S(1)}, u32[]{:S(2)}, u32[]{:S(2)}) %collective-permute-start.7) | collective-permute-done | bytes 524320 | tf_op jit(solution)/shard_map/ppermute | solution.py:318
  107.3 0.8 copy-done.2
  108.1 2.0 %merge.1 = (f32[8,32,128]{2,1,0:T(8,128)}, f32[8,32,128]{2,1,0:T(8,128)}, f32[8,32,128]{2,1,0:T(8,128)}, f32[8,32,128]{2,1,0:T(8,128)}) custom-call(f32[4,8,32,128]{3,2,1,0:T(8,128)} %get-tuple-element.31.keep, f32[4,8,32,128]{3,2,1,0:T(8,128)} %copy-done.2), custom_call_target="tpu_custom_call" | custom-call | tf_op jit(solution)/shard_map/merge/pallas_call | solution.py:387
  110.1 2.6 %collective-permute-start.10 = (f32[8,32,128]{2,1,0:T(8,128)}, f32[8,32,128]{2,1,0:T(8,128)S(1)}, u32[]{:S(2)}, u32[]{:S(2)}) collective-permute-start(f32[8,32,128]{2,1,0:T(8,128)} %get-tuple-element.36), channel_id=1, source_target_pairs={{0,6},{1,7},{2,0},{3,1},{4,2},{5,3},{6,4},{7,5},{8,14},{9,15},{10,... | collective-permute-start | bytes 393224 | tf_op jit(solution)/shard_map/ppermute | solution.py:318
  112.6 1.7 %collective-permute-start.9 = (f32[8,32,128]{2,1,0:T(8,128)}, f32[8,32,128]{2,1,0:T(8,128)S(1)}, u32[]{:S(2)}, u32[]{:S(2)}) collective-permute-start(f32[8,32,128]{2,1,0:T(8,128)} %get-tuple-element.35), channel_id=1, source_target_pairs={{0,4},{1,5},{2,6},{3,7},{4,0},{5,1},{6,2},{7,3},{8,12},{9,13},{10,... | collective-permute-start | bytes 393224 | tf_op jit(solution)/shard_map/ppermute | solution.py:318
  114.4 1.0 collective-permute-done.10.d
  115.4 4.3 %collective-permute-done.8.b = f32[8,32,128]{2,1,0:T(8,128)S(1)} collective-permute-done((f32[8,32,128]{2,1,0:T(8,128)}, f32[8,32,128]{2,1,0:T(8,128)S(1)}, u32[]{:S(2)}, u32[]{:S(2)}) %collective-permute-start.8) | collective-permute-done | bytes 131104 | tf_op jit(solution)/shard_map/ppermute | solution.py:318
  121.0 1.8 %last.1 = f32[1,32,4,256]{3,2,1,0:T(4,128)} custom-call(f32[8,32,128]{2,1,0:T(8,128)} %get-tuple-element.33.a, f32[8,32,128]{2,1,0:T(8,128)} %copy-done.5, f32[8,32,128]{2,1,0:T(8,128)} %copy-done.6, f32[8,32,128]{2,1,0:T(8,128)} %copy-done.4), custom_call_target="tpu_custom_call" | custom-call | tf_op jit(solution)/shard_map/last/pallas_call | solution.py:395
  (63 shorter events, 7.8 us)
Async XLA Ops:
  0.0 0.7 copy-start.12
  0.7 0.7 copy-start.11
  0.8 0.7 copy-start.10
  1.5 0.7 copy-start.13
  5.2 12.1 %copy-start.24 = (f32[17,8,128]{2,1,0:T(8,128)S(1)}, f32[17,8,128]{2,1,0:T(8,128)}, u32[]{:S(2)}) copy-start(f32[17,8,128]{2,1,0:T(8,128)} %get-tuple-element.29) | copy-start | bytes 208900
  5.2 13.1 %copy-start.23 = (f32[17,8,128]{2,1,0:T(8,128)S(1)}, f32[17,8,128]{2,1,0:T(8,128)}, u32[]{:S(2)}) copy-start(f32[17,8,128]{2,1,0:T(8,128)} %get-tuple-element.25) | copy-start | bytes 208900
  5.2 14.4 %copy-start.18 = (f32[17,8,128]{2,1,0:T(8,128)S(1)}, f32[17,8,128]{2,1,0:T(8,128)}, u32[]{:S(2)}) copy-start(f32[17,8,128]{2,1,0:T(8,128)} %get-tuple-element.26) | copy-start | bytes 208900
  5.2 16.0 %copy-start.17 = (f32[17,8,128]{2,1,0:T(8,128)S(1)}, f32[17,8,128]{2,1,0:T(8,128)}, u32[]{:S(2)}) copy-start(f32[17,8,128]{2,1,0:T(8,128)} %get-tuple-element.27) | copy-start | bytes 208900
  5.2 17.3 %copy-start.16 = (f32[17,8,128]{2,1,0:T(8,128)S(1)}, f32[17,8,128]{2,1,0:T(8,128)}, u32[]{:S(2)}) copy-start(f32[17,8,128]{2,1,0:T(8,128)} %get-tuple-element.28) | copy-start | bytes 208900
  5.2 17.9 %copy-start.15 = (f32[17,8,128]{2,1,0:T(8,128)S(1)}, f32[17,8,128]{2,1,0:T(8,128)}, u32[]{:S(2)}) copy-start(f32[17,8,128]{2,1,0:T(8,128)} %get-tuple-element.23) | copy-start | bytes 208900
  5.2 19.6 %copy-start.14 = (f32[17,8,128]{2,1,0:T(8,128)S(1)}, f32[17,8,128]{2,1,0:T(8,128)}, u32[]{:S(2)}) copy-start(f32[17,8,128]{2,1,0:T(8,128)} %get-tuple-element.24) | copy-start | bytes 208900
  5.2 30.7 %all-to-all-start = ((f32[32,1,5120]{2,1,0:T(1,128)}), f32[32,1,5120]{2,1,0:T(1,128)S(1)}, u32[]{:S(2)}, u32[]{:S(2)}) async-start(f32[32,1,5120]{2,1,0:T(1,128)} %bitcast.19), calls=%async_computation | async-start | bytes 1310720 | tf_op jit(solution)/shard_map/all_to_all | solution.py:351
  17.2 5.9 %collective-permute-start.6 = (f32[17,8,128]{2,1,0:T(8,128)S(1)}, f32[17,8,128]{2,1,0:T(8,128)S(1)}, u32[]{:S(2)}, u32[]{:S(2)}) collective-permute-start(f32[17,8,128]{2,1,0:T(8,128)S(1)} %copy-done.24), channel_id=1, source_target_pairs={{0,1},{1,0},{2,3},{3,2},{4,5},{5,4},{6,7},{7,6},{8,9},{9,8},{10,11... | collective-permute-start | bytes 208904 | tf_op jit(solution)/shard_map/ppermute | solution.py:318
  18.3 6.5 %collective-permute-start.2 = (f32[17,8,128]{2,1,0:T(8,128)S(1)}, f32[17,8,128]{2,1,0:T(8,128)S(1)}, u32[]{:S(2)}, u32[]{:S(2)}) collective-permute-start(f32[17,8,128]{2,1,0:T(8,128)S(1)} %copy-done.23), channel_id=1, source_target_pairs={{0,2},{1,3},{2,4},{3,5},{4,6},{5,7},{6,0},{7,1},{8,10},{9,11},{10,... | collective-permute-start | bytes 208904 | tf_op jit(solution)/shard_map/ppermute | solution.py:318
  19.6 34.8 %collective-permute-start.3 = (f32[17,8,128]{2,1,0:T(8,128)S(1)}, f32[17,8,128]{2,1,0:T(8,128)S(1)}, u32[]{:S(2)}, u32[]{:S(2)}) collective-permute-start(f32[17,8,128]{2,1,0:T(8,128)S(1)} %copy-done.18), channel_id=1, source_target_pairs={{0,3},{1,2},{2,5},{3,4},{4,7},{5,6},{6,1},{7,0},{8,11},{9,10},{10,... | collective-permute-start | bytes 208904 | tf_op jit(solution)/shard_map/ppermute | solution.py:318
  21.2 33.3 %collective-permute-start.4 = (f32[17,8,128]{2,1,0:T(8,128)S(1)}, f32[17,8,128]{2,1,0:T(8,128)S(1)}, u32[]{:S(2)}, u32[]{:S(2)}) collective-permute-start(f32[17,8,128]{2,1,0:T(8,128)S(1)} %copy-done.17), channel_id=1, source_target_pairs={{0,6},{1,7},{2,0},{3,1},{4,2},{5,3},{6,4},{7,5},{8,14},{9,15},{10,... | collective-permute-start | bytes 208904 | tf_op jit(solution)/shard_map/ppermute | solution.py:318
  22.5 31.9 %collective-permute-start.5 = (f32[17,8,128]{2,1,0:T(8,128)S(1)}, f32[17,8,128]{2,1,0:T(8,128)S(1)}, u32[]{:S(2)}, u32[]{:S(2)}) collective-permute-start(f32[17,8,128]{2,1,0:T(8,128)S(1)} %copy-done.16), channel_id=1, source_target_pairs={{0,7},{1,6},{2,1},{3,0},{4,3},{5,2},{6,5},{7,4},{8,15},{9,14},{10,... | collective-permute-start | bytes 208904 | tf_op jit(solution)/shard_map/ppermute | solution.py:318
  23.1 16.2 %copy-start.7 = (f32[17,8,128]{2,1,0:T(8,128)}, f32[17,8,128]{2,1,0:T(8,128)S(1)}, u32[]{:S(2)}) copy-start(f32[17,8,128]{2,1,0:T(8,128)S(1)} %collective-permute-done.6.refs_0_) | copy-start | bytes 208900
  23.2 42.4 %collective-permute-start = (f32[17,8,128]{2,1,0:T(8,128)S(1)}, f32[17,8,128]{2,1,0:T(8,128)S(1)}, u32[]{:S(2)}, u32[]{:S(2)}) collective-permute-start(f32[17,8,128]{2,1,0:T(8,128)S(1)} %copy-done.15), channel_id=1, source_target_pairs={{0,4},{1,5},{2,6},{3,7},{4,0},{5,1},{6,2},{7,3},{8,12},{9,13},{10,... | collective-permute-start | bytes 208904 | tf_op jit(solution)/shard_map/ppermute | solution.py:318
  24.8 14.5 %copy-start.19 = (f32[17,8,128]{2,1,0:T(8,128)}, f32[17,8,128]{2,1,0:T(8,128)S(1)}, u32[]{:S(2)}) copy-start(f32[17,8,128]{2,1,0:T(8,128)S(1)} %collective-permute-done.2.refs_0_) | copy-start | bytes 208900
  24.8 40.7 %collective-permute-start.1 = (f32[17,8,128]{2,1,0:T(8,128)S(1)}, f32[17,8,128]{2,1,0:T(8,128)S(1)}, u32[]{:S(2)}, u32[]{:S(2)}) collective-permute-start(f32[17,8,128]{2,1,0:T(8,128)S(1)} %copy-done.14), channel_id=1, source_target_pairs={{0,5},{1,4},{2,7},{3,6},{4,1},{5,0},{6,3},{7,2},{8,13},{9,12},{10,... | collective-permute-start | bytes 208904 | tf_op jit(solution)/shard_map/ppermute | solution.py:318
  35.9 0.8 copy-start
  39.3 33.7 %all-to-all-start.1 = ((f32[8,1,2048]{2,1,0:T(1,128)}), f32[8,1,2048]{2,1,0:T(1,128)S(1)}, u32[]{:S(2)}, u32[]{:S(2)}) async-start(f32[8,1,2048]{2,1,0:T(1,128)} %bitcast.21), calls=%async_computation.1 | async-start | bytes 131072 | tf_op jit(solution)/shard_map/all_to_all | solution.py:363
  76.3 21.4 %all-to-all-start.2 = ((f32[32,1,4096]{2,1,0:T(1,128)}), f32[32,1,4096]{2,1,0:T(1,128)S(1)}, u32[]{:S(2)}, u32[]{:S(2)}) async-start(f32[32,1,4096]{2,1,0:T(1,128)} %bitcast.18), calls=%async_computation.2 | async-start | bytes 1048576 | tf_op jit(solution)/shard_map/all_to_all | solution.py:373
  97.7 0.8 copy-start.1
  103.5 3.8 %collective-permute-start.7 = (f32[4,8,32,128]{3,2,1,0:T(8,128)}, f32[4,8,32,128]{3,2,1,0:T(8,128)S(1)}, u32[]{:S(2)}, u32[]{:S(2)}) collective-permute-start(f32[4,8,32,128]{3,2,1,0:T(8,128)} %get-tuple-element.32), channel_id=1, source_target_pairs={{0,1},{1,0},{2,3},{3,2},{4,5},{5,4},{6,7},{7,6},{8,9},{9,8},{10,11... | collective-permute-start | bytes 1572872 | tf_op jit(solution)/shard_map/ppermute | solution.py:318
  107.3 0.8 copy-start.2
  110.1 5.4 %collective-permute-start.10 = (f32[8,32,128]{2,1,0:T(8,128)}, f32[8,32,128]{2,1,0:T(8,128)S(1)}, u32[]{:S(2)}, u32[]{:S(2)}) collective-permute-start(f32[8,32,128]{2,1,0:T(8,128)} %get-tuple-element.36), channel_id=1, source_target_pairs={{0,6},{1,7},{2,0},{3,1},{4,2},{5,3},{6,4},{7,5},{8,14},{9,15},{10,... | collective-permute-start | bytes 393224 | tf_op jit(solution)/shard_map/ppermute | solution.py:318
  112.6 7.1 %collective-permute-start.8 = (f32[8,32,128]{2,1,0:T(8,128)}, f32[8,32,128]{2,1,0:T(8,128)S(1)}, u32[]{:S(2)}, u32[]{:S(2)}) collective-permute-start(f32[8,32,128]{2,1,0:T(8,128)} %get-tuple-element.34), channel_id=1, source_target_pairs={{0,2},{1,3},{2,4},{3,5},{4,6},{5,7},{6,0},{7,1},{8,10},{9,11},{10,... | collective-permute-start | bytes 393224 | tf_op jit(solution)/shard_map/ppermute | solution.py:318
  112.6 7.7 %collective-permute-start.9 = (f32[8,32,128]{2,1,0:T(8,128)}, f32[8,32,128]{2,1,0:T(8,128)S(1)}, u32[]{:S(2)}, u32[]{:S(2)}) collective-permute-start(f32[8,32,128]{2,1,0:T(8,128)} %get-tuple-element.35), channel_id=1, source_target_pairs={{0,4},{1,5},{2,6},{3,7},{4,0},{5,1},{6,2},{7,3},{8,12},{9,13},{10,... | collective-permute-start | bytes 393224 | tf_op jit(solution)/shard_map/ppermute | solution.py:318
  115.4 4.9 %copy-start.4 = (f32[8,32,128]{2,1,0:T(8,128)}, f32[8,32,128]{2,1,0:T(8,128)S(1)}, u32[]{:S(2)}) copy-start(f32[8,32,128]{2,1,0:T(8,128)S(1)} %collective-permute-done.10.d) | copy-start | bytes 393220
  120.3 0.7 copy-start.6
  (7 other events, 4.4 us)
where the time goes:
time: 124 us; the launch traced here: 123 us
  Pallas kernels  40.5 us (33%)
  starting transfers between devices  39.2 us (32%)
  waiting for transfers between devices  32.4 us (26%)
  local copies, waits for them, and re-layouts  9.44 us (8%)
  other arithmetic  1.24 us (1%)
    pallas_call x4, Pallas kernels, images(): pl.pallas_call(functools.partial(image_kernel, count, first), out_shape=j...  24.2 us
    ppermute x11, starting transfers between devices, shift(): return lax.ppermute(x, 'ch', pairs)  15.5 us
    all_to_all x1, waiting for transfers between devices, local(): arrived = lax.all_to_all(outgoing.reshape(32, 4096), 'bl', 0, 0, tiled=True)  15.1 us
    all_to_all x1, starting transfers between devices, local(): table = lax.all_to_all(shared.reshape(32, 40 * 128), 'bl', 0, 0, tiled=True)  12 us
    all_to_all x1, waiting for transfers between devices, local(): table = lax.all_to_all(shared.reshape(32, 40 * 128), 'bl', 0, 0, tiled=True)  9.5 us
    unnamed x50, local copies, waits for them, and re-layouts  8.14 us
    ppermute x11, waiting for transfers between devices, shift(): return lax.ppermute(x, 'ch', pairs)  7.71 us
    all_to_all x1, starting transfers between devices, local(): lax.all_to_all(pair.reshape(8, 2048), 'ch', 0, 0, tiled=True)  6.96 us
  transfers between devices with their start and end apart: 14, of which 6 were waited for; matrix products, arithmetic and copies ran while one was open for 1% of the time, Pallas kernels for 22%

commit v1 on v0

--- a/solution.py
+++ b/solution.py
@@ -15,8 +15,6 @@
 BF16 = jnp.bfloat16
 VM = pl.BlockSpec(memory_space=pltpu.VMEM)
 SM = pl.BlockSpec(memory_space=pltpu.SMEM)
-
-INV, TILES, ST0, ST1, OFF0, OFF1, OWN, ME = 0, 64, 128, 192, 256, 320, 384, 416
 
 SIN = [(-1.0) ** k / math.factorial(2 * k + 1) for k in range(7)]
 COS = [(-1.0) ** k / math.factorial(2 * k) for k in range(7)]
@@ -49,10 +47,10 @@
         n, sign = (b - 16, 1.0) if b >= 16 else (15 - b, -1.0)
         for k in range(2):
             for part in range(2):
-                m1[k, part, 0, n, 0, k, b] = 1.0
-                m1[k, part, 1, n, 1, k, b] = sign
-                m2[k, part, 1, n, 0, k, b] = -sign
-                m2[k, part, 0, n, 1, k, b] = 1.0
+                m1[part, k, 0, n, 0, k, b] = 1.0
+                m1[part, k, 1, n, 1, k, b] = sign
+                m2[part, k, 1, n, 0, k, b] = -sign
+                m2[part, k, 0, n, 1, k, b] = 1.0
     to_image = np.concatenate([m1.reshape(128, 128), m2.reshape(128, 128)], 0)
     fold = np.zeros((2, 128, 128))
     for lane in range(128):
@@ -83,48 +81,59 @@
     )
 
 
-def pack_kernel(ints, freq, vis, coord, aterms, *outs):
-    chunks, uv, shared = outs[:8], outs[8], outs[9]
-    own = outs[10]
-    me = ints[ME]
-    y = me // 2
-    core = me % 2
+def owners(slots, own):
+    for n in range(32):
+        own[slots[n]] = n
+
+
+def share_kernel(me_ref, inv, tiles, offs, slots, aterms, shared, own):
+    me = me_ref[0]
+    owners(slots, own)
+    lane = lax.broadcasted_iota(jnp.int32, (1, 128), 1)
+    re = aterms[:, pl.ds(pl.multiple_of(me * 128, 128), 128)]
+    im = aterms[:, pl.ds(pl.multiple_of(1024 + me * 128, 128), 128)]
+    blank = jnp.zeros((1, 128), F32)
+    for b in range(32):
+        shared[33 * b : 33 * b + 16, :] = re
+        shared[33 * b + 16 : 33 * b + 32, :] = im
+        shared[33 * b + 32 : 33 * b + 33, :] = blank
+    for j in range(8):
+        s = inv[8 * j + me]
+        spot = jnp.where(lane == 0, offs[0, s], jnp.where(lane == 1, offs[1, s], 0))
+        shared[pl.ds(33 * own[tiles[s]] + 32, 1), :] = spot.astype(F32)
+
+
+def pack_kernel(me_ref, inv, freq, vis, coord, *outs):
+    uv = outs[5]
+    me = me_ref[0]
+    y = me >> 1
+    core = me & 1
     row = lax.broadcasted_iota(jnp.int32, (8, 128), 0)
-    lane = lax.broadcasted_iota(jnp.int32, (8, 128), 1)
     freqs = jnp.zeros((8, 128), F32)
     for k in range(8):
         freqs = jnp.where(row == k, freq[k], freqs)
+    places = [outs[0], outs[1]] + [outs[1 + d].at[e] for d in range(1, 4) for e in range(2)]
     for q in range(8):
-        to = ((y + q // 2) % 4) * 2 + (core + q % 2) % 2
+        to = (((y + q // 2) & 3) << 1) + ((core + q % 2) & 1)
         for j in range(8):
-            s = ints[INV + 8 * j + to]
-            chunks[q][j] = vis[0, s]
-            chunks[q][8 + j] = vis[1, s]
-        chunks[q][16] = freqs
-    for n in range(32):
-        own[ints[OWN + n]] = n
-    blank = jnp.zeros((8, 128), F32)
-    re = aterms[:, pl.ds(pl.multiple_of(me * 128, 128), 128)]
-    im = aterms[:, pl.ds(pl.multiple_of(1024 + me * 128, 128), 128)]
-    for b in range(32):
-        shared[b, 0:16, :] = re
-        shared[b, 16:32, :] = im
-        shared[b, 32:40, :] = blank
+            s = inv[8 * j + to]
+            places[q][j] = vis[0, s]
+            places[q][8 + j] = vis[1, s]
+        places[q][16] = freqs
     for j in range(8):
-        s = ints[INV + 8 * j + me]
+        s = inv[8 * j + me]
         for d in range(2):
             uv[d, pl.ds(j, 1), :] = coord[d, pl.ds(s, 1), :]
-        spot = jnp.where(lane == 0, ints[OFF0 + s], jnp.where(lane == 1, ints[OFF1 + s], 0))
-        shared[own[ints[TILES + s]], 32:40, :] = spot.astype(F32)
-
-
-def image_kernel(count, first, uv, *refs):
-    vis = refs[:count]
+
+
+def image_kernel(picks, first, uv, *refs):
+    count = len(picks)
+    vis = [r if p is None else r.at[p] for p, r in zip(picks, refs)]
     refs = refs[count:]
     if not first:
         before = refs[0]
         refs = refs[1:]
-    out, xu, xv, vp, lk, rk = refs
+    out, xu, xv, vp = refs
     for n in range(count):
         vref = vis[n]
         f = vref[16]
@@ -154,34 +163,39 @@
             vp[s, 0] = vr * pr + vi * pi
             vp[s, 1] = vi * pr - vr * pi
         for s in range(8):
+            lefts, rights = [], []
             for c in range(8):
                 xs = xu[s, pl.ds(c, 32, stride=8), :]
                 ys = xv[s, pl.ds(c, 32, stride=8), :]
                 vr = vp[s, 0, pl.ds(c, 1), :]
                 vi = vp[s, 1, pl.ds(c, 1), :]
-                lh, ll = split(jnp.concatenate([xs * vr, xs * vi], 0))
-                lk[s % 2, :, pl.ds(c * 256, 128)] = lh
-                lk[s % 2, :, pl.ds(c * 256 + 128, 128)] = ll
-                yh, yl = split(ys)
-                wh, wl = split(ys * weight[c : c + 1])
-                r4 = jnp.concatenate([yh, yl, wh, wl], 0)
-                rk[s % 2, :, pl.ds(c * 256, 128)] = r4
-                rk[s % 2, :, pl.ds(c * 256 + 128, 128)] = r4
+                lefts.append(jnp.concatenate(split(jnp.concatenate([xs * vr, xs * vi], 0)), 0))
+                both = jnp.concatenate([ys, ys * weight[c : c + 1]], 0)
+                rights.append(jnp.concatenate(split(both), 0))
             o = lax.dot_general(
-                lk[s % 2], rk[s % 2], (((1,), (1,)), ((), ())), preferred_element_type=F32
+                jnp.concatenate(lefts, 1),
+                jnp.concatenate(rights, 1),
+                (((1,), (1,)), ((), ())),
+                preferred_element_type=F32,
             )
+            o = o[:64] + o[64:]
             if n == 0:
                 out[s] = o if first else before[s] + o
             else:
                 out[s] += o
 
 
+def grant(mib):
+    return pltpu.CompilerParams(vmem_limit_bytes=mib << 20)
+
+
 def images(uv, chunks, before=None):
+    picks = tuple(p for _, p in chunks)
     count = len(chunks)
     first = before is None
-    args = [uv, *chunks] + ([] if first else [before])
+    args = [uv] + [c for c, _ in chunks] + ([] if first else [before])
     return pl.pallas_call(
-        functools.partial(image_kernel, count, first),
+        functools.partial(image_kernel, picks, first),
         out_shape=jax.ShapeDtypeStruct((8, 64, 128), F32),
         in_specs=[VM] * len(args),
         out_specs=VM,
@@ -189,36 +203,35 @@
             pltpu.VMEM((8, 256, 128), F32),
             pltpu.VMEM((8, 256, 128), F32),
             pltpu.VMEM((8, 2, 8, 128), F32),
-            pltpu.VMEM((2, 64, 2048), BF16),
-            pltpu.VMEM((2, 128, 2048), BF16),
         ],
+        compiler_params=grant(16),
         cost_estimate=pl.CostEstimate(
-            flops=count * 60_000_000, bytes_accessed=count * 100_000, transcendentals=0
+            flops=count * 200_000_000, bytes_accessed=count * 100_000, transcendentals=0
         ),
         name=f"image{count}",
     )(*args)
 
 
-def pair_kernel(ints, table, taper, out):
-    me = ints[ME]
-    g = taper[pl.ds(me, 1), :]
+def pair_kernel(me_ref, inv, stations, table, taper, out):
+    g = taper[pl.ds(me_ref[0], 1), :]
     for to in range(8):
         for j in range(8):
-            s = ints[INV + 8 * j + to]
-            p = ints[ST0 + s]
-            q = ints[ST1 + s]
-            pr = table[p // 16, pl.ds(p % 16, 1), :]
-            pi = table[p // 16, pl.ds(16 + p % 16, 1), :]
-            qr = table[q // 16, pl.ds(q % 16, 1), :]
-            qi = table[q // 16, pl.ds(16 + q % 16, 1), :]
+            s = inv[8 * j + to]
+            p = stations[0, s]
+            q = stations[1, s]
+            p = p + 17 * (p >> 4)
+            q = q + 17 * (q >> 4)
+            pr = table[pl.ds(p, 1), :]
+            pi = table[pl.ds(p + 16, 1), :]
+            qr = table[pl.ds(q, 1), :]
+            qi = table[pl.ds(q + 16, 1), :]
             out[to, pl.ds(j, 1), :] = (pr * qr + pi * qi) * g
             out[to, pl.ds(8 + j, 1), :] = (pi * qr - pr * qi) * g
 
 
-def finish_kernel(ints, acc, pair, to_image, fold, left3, right3, out, own):
-    me = ints[ME]
-    for n in range(32):
-        own[ints[OWN + n]] = n
+def finish_kernel(me_ref, inv, tiles, slots, acc, pair, to_image, fold, left3, right3, out, own):
+    me = me_ref[0]
+    owners(slots, own)
     blank = jnp.zeros((32, 128), F32)
     for b in range(32):
         out[b] = blank
@@ -270,32 +283,40 @@
         jnp.concatenate([hh, hh, hl], 1), right3[...], preferred_element_type=F32
     )
     for s in range(8):
-        out[own[ints[TILES + ints[INV + 8 * s + me]]]] = full[32 * s : 32 * s + 32]
-
-
-def place_kernel(spots, me_ref, arrived, keep, give, acc):
+        out[own[tiles[inv[8 * s + me]]]] = full[32 * s : 32 * s + 32]
+
+
+def place_kernel(me_ref, spots, arrived, keep, give, acc):
     lane = lax.broadcasted_iota(jnp.int32, (32, 128), 1)
     me = me_ref[0]
-    y = me // 2
-    core = me % 2
+    y = me >> 1
+    core = me & 1
     acc[...] = jnp.zeros_like(acc)
 
     def one(i, unused):
         r = spots[2 * i]
         c = spots[2 * i + 1]
+        half = c >> 7
+        c = c & 127
         tile = arrived[i]
         near = (lane >= c) & (lane < c + 32)
-        far = (lane + 128 >= c) & (lane + 128 < c + 32)
+        moved = [pltpu.roll(tile, (c - 32 * m) & 127, 1) for m in range(4)]
         for m in range(4):
-            moved = pltpu.roll(tile, (c - 32 * m + 128) % 128, 1)
-            for half, mask in ((0, near), (1, far)):
-                at = (2 * m + half, pl.ds(r, 32), slice(None))
-                acc[at] = acc[at] + jnp.where(mask, moved, 0.0)
+            at = (2 * m + half, pl.ds(r, 32), slice(None))
+            acc[at] = acc[at] + jnp.where(near, moved[m], 0.0)
+
+        @pl.when(c > 96)
+        def _():
+            far = lane < c - 96
+            for m in range(4):
+                at = (2 * m + 1, pl.ds(r, 32), slice(None))
+                acc[at] = acc[at] + jnp.where(far, moved[m], 0.0)
+
         return unused
 
     lax.fori_loop(0, 32, one, 0)
     for d in range(4):
-        block = ((y + d) % 4) * 2
+        block = ((y + d) & 3) << 1
         for k in range(8):
             keep[d, k] = acc[k, pl.ds(pl.multiple_of((block + core) * 32, 32), 32), :]
             give[d, k] = acc[k, pl.ds(pl.multiple_of((block + 1 - core) * 32, 32), 32), :]
@@ -321,58 +342,65 @@
 def local(visibility, coordinates, freq_ratio, aterms, stations, sub_tile, offsets, tile_of_slot):
     to_image, fold, left3, right3, taper = constants()
     me = lax.axis_index("ch").astype(jnp.int32)
+    me = me[None]
     order = jnp.arange(64, dtype=jnp.int32)
     key = sub_tile * 64 + order
     pos = jnp.sum((key[None, :] < key[:, None]).astype(jnp.int32), axis=1)
     inv = jnp.sum(jnp.where(pos[None, :] == order[:, None], order[None, :], 0), axis=1)
-    ints = jnp.concatenate(
-        [
-            inv,
-            sub_tile,
-            stations[:, 0],
-            stations[:, 1],
-            offsets[:, 0],
-            offsets[:, 1],
-            tile_of_slot,
-            me[None],
-        ]
-    )
-    packed = pl.pallas_call(
+    stations = stations.T
+    offsets = offsets.T
+    own = pltpu.SMEM((32,), jnp.int32)
+    shared = pl.pallas_call(
+        share_kernel,
+        out_shape=jax.ShapeDtypeStruct((33 * 32, 128), F32),
+        in_specs=[SM] * 5 + [VM],
+        out_specs=VM,
+        scratch_shapes=[own],
+        compiler_params=grant(4),
+        name="share",
+    )(me, inv, sub_tile, offsets, tile_of_slot, aterms)
+    inv, shared = lax.optimization_barrier((inv, shared))
+    table = lax.all_to_all(shared.reshape(32, 33 * 128), "bl", 0, 0, tiled=True)
+    table = table.reshape(33 * 32, 128)
+    chunk = jax.ShapeDtypeStruct((17, 8, 128), F32)
+    double = jax.ShapeDtypeStruct((2, 17, 8, 128), F32)
+    mine, near, *far, uv = pl.pallas_call(
         pack_kernel,
-        out_shape=[jax.ShapeDtypeStruct((17, 8, 128), F32)] * 8
-        + [jax.ShapeDtypeStruct((2, 8, 128), F32), jax.ShapeDtypeStruct((32, 40, 128), F32)],
-        in_specs=[SM, SM, VM, VM, VM],
-        out_specs=[VM] * 10,
-        scratch_shapes=[pltpu.SMEM((32,), jnp.int32)],
+        out_shape=[chunk, chunk, double, double, double, jax.ShapeDtypeStruct((2, 8, 128), F32)],
+        in_specs=[SM, SM, SM, VM, VM],
+        out_specs=[VM] * 6,
+        compiler_params=grant(8),
         name="pack",
-    )(ints, freq_ratio, visibility, coordinates, aterms)
-    chunks, uv, shared = packed[:8], packed[8], packed[9]
-    moved = [shift(chunks[q], q // 2, q % 2) for q in range(1, 8)]
-    table = lax.all_to_all(shared.reshape(32, 40 * 128), "bl", 0, 0, tiled=True)
-    table = table.reshape(32, 40, 128)
-    acc = images(uv, [chunks[0]])
-    acc = images(uv, [moved[0]], acc)
-    acc = images(uv, [moved[1], moved[2], moved[5], moved[6]], acc)
+    )(me, inv, freq_ratio, visibility, coordinates)
+    near = shift(near, 0, 1)
+    direct = [shift(far[d - 1], d, 0) for d in range(1, 4)]
+    acc = images(uv, [(mine, None), (near, None)])
+    acc, *direct = lax.optimization_barrier((acc, *direct))
+    swapped = [shift(x, 0, 1) for x in direct]
+    acc = images(uv, [(direct[0], 0), (direct[2], 0)], acc)
+    acc = images(uv, [(swapped[0], 1), (swapped[2], 1), (direct[1], 0), (swapped[1], 1)], acc)
+    acc, table = lax.optimization_barrier((acc, table))
     pair = pl.pallas_call(
         pair_kernel,
         out_shape=jax.ShapeDtypeStruct((8, 16, 128), F32),
-        in_specs=[SM, VM, VM],
+        in_specs=[SM, SM, SM, VM, VM],
         out_specs=VM,
+        compiler_params=grant(4),
         name="pair",
-    )(ints, table, taper)
+    )(me, inv, stations, table, taper)
     pair = lax.all_to_all(pair.reshape(8, 2048), "ch", 0, 0, tiled=True).reshape(8, 16, 128)
-    acc = images(uv, [moved[3], moved[4]], acc)
     outgoing = pl.pallas_call(
         finish_kernel,
         out_shape=jax.ShapeDtypeStruct((32, 32, 128), F32),
-        in_specs=[SM] + [VM] * 6,
+        in_specs=[SM] * 4 + [VM] * 6,
         out_specs=VM,
-        scratch_shapes=[pltpu.SMEM((32,), jnp.int32)],
+        scratch_shapes=[own],
+        compiler_params=grant(12),
         name="finish",
-    )(ints, acc, pair, to_image, fold, left3, right3)
+    )(me, inv, sub_tile, tile_of_slot, acc, pair, to_image, fold, left3, right3)
     arrived = lax.all_to_all(outgoing.reshape(32, 4096), "bl", 0, 0, tiled=True)
     arrived = arrived.reshape(32, 32, 128)
-    spots = table[:, 32, 0:2].reshape(64).astype(jnp.int32)
+    spots = table[32::33, 0:2].reshape(64).astype(jnp.int32)
     half = jax.ShapeDtypeStruct((4, 8, 32, 128), F32)
     keep, give = pl.pallas_call(
         place_kernel,
@@ -380,8 +408,9 @@
         in_specs=[SM, SM, VM],
         out_specs=[VM, VM],
         scratch_shapes=[pltpu.VMEM((8, TILE, 128), F32)],
+        compiler_params=grant(8),
         name="place",
-    )(spots, me[None], arrived)
+    )(me, spots, arrived)
     got = shift(give, 0, 1)
     block = jax.ShapeDtypeStruct((8, 32, 128), F32)
     sums = pl.pallas_call(
@@ -389,6 +418,7 @@
         out_shape=[block] * 4,
         in_specs=[VM, VM],
         out_specs=[VM] * 4,
+        compiler_params=grant(6),
         name="merge",
     )(keep, got)
     parts = [sums[0]] + [shift(sums[d], d, 0) for d in range(1, 4)]
@@ -397,6 +427,7 @@
         out_shape=jax.ShapeDtypeStruct((1, 32, 4, TILE), F32),
         in_specs=[VM] * 4,
         out_specs=VM,
+        compiler_params=grant(4),
         name="last",
     )(*parts)
 

time: 124 us -> 92.1 us (0.74)
  Pallas kernels: 40.5 us -> 19.2 us
  blocking collectives: 0 us -> 8.73 us
  waiting for transfers between devices: 32.4 us -> 24.6 us
  local copies, waits for them, and re-layouts: 9.44 us -> 3.07 us
  starting transfers between devices: 39.2 us -> 35.5 us
    pallas_call x5, Pallas kernels: 26.5 us -> 12 us  [the longest x3 9.9 us: images(): pl.pallas_call(functools.partial(image_kernel, picks, first), out_shape=j...]
    all_to_all x2 -> x1, waiting for transfers between devices: 9.5 us -> 0.01 us  [local(): table = lax.all_to_all(shared.reshape(32, 33 * 128), 'bl', 0, 0, tiled=True)]
    all_to_all x0 -> x1, blocking collectives: none -> 8.73 us  [local(): lax.all_to_all(pair.reshape(8, 2048), 'ch', 0, 0, tiled=True)]
    all_to_all x2 -> x1, starting transfers between devices: 19 us -> 12 us  [local(): table = lax.all_to_all(shared.reshape(32, 33 * 128), 'bl', 0, 0, tiled=True)]
    unnamed x50 -> x26, local copies, waits for them, and re-layouts: 8.14 us -> 2.95 us
    all_to_all x1, starting transfers between devices: 4.71 us -> 9.22 us  [local(): arrived = lax.all_to_all(outgoing.reshape(32, 4096), 'bl', 0, 0, tiled=True)]
    pallas_call x1, Pallas kernels: 2 us -> 0.07 us  [local(): pl.pallas_call(merge_kernel, out_shape=[block] * 4, in_specs=[VM, VM], ou...]
    pallas_call x1, Pallas kernels: 2.55 us -> 0.84 us  [local(): pl.pallas_call(pair_kernel, out_shape=jax.ShapeDtypeStruct((8, 16, 128),...]
  transfers between devices with their start and end apart: 14 -> 13, of which waited for: 6 -> 6; matrix products, arithmetic and copies ran while one was open for 1% -> 0% of each run, Pallas kernels for 22% -> 11%
where the time goes in v1:
time: 92.1 us; the launch traced here: 91.7 us
  starting transfers between devices  35.5 us (39%)
  waiting for transfers between devices  24.6 us (27%)
  Pallas kernels  19.2 us (21%)
  blocking collectives  8.73 us (9%)
  local copies, waits for them, and re-layouts  3.07 us (3%)
    all_to_all x1, waiting for transfers between devices, local(): arrived = lax.all_to_all(outgoing.reshape(32, 4096), 'bl', 0, 0, tiled=True)  15.9 us
    ppermute x11, starting transfers between devices, shift(): return lax.ppermute(x, 'ch', pairs)  14.3 us
    all_to_all x1, starting transfers between devices, local(): table = lax.all_to_all(shared.reshape(32, 33 * 128), 'bl', 0, 0, tiled=True)  12 us
    pallas_call x3, Pallas kernels, images(): pl.pallas_call(functools.partial(image_kernel, picks, first), out_shape=j...  9.9 us
    all_to_all x1, starting transfers between devices, local(): arrived = lax.all_to_all(outgoing.reshape(32, 4096), 'bl', 0, 0, tiled=True)  9.22 us
    ppermute x11, waiting for transfers between devices, shift(): return lax.ppermute(x, 'ch', pairs)  8.75 us
    all_to_all x1, blocking collectives, local(): lax.all_to_all(pair.reshape(8, 2048), 'ch', 0, 0, tiled=True)  8.73 us
    pallas_call x1, Pallas kernels, local(): pl.pallas_call(place_kernel, out_shape=[half, half], in_specs=[SM, SM, VM...  3.51 us
  transfers between devices with their start and end apart: 13, of which 6 were waited for; matrix products, arithmetic and copies ran while one was open for 0% of the time, Pallas kernels for 11%

profile of v1, /device:TPU:1, one launch (start us, length us, event | category | flops | bytes accessed | tf_op | source)
XLA Modules:
  0.0 91.7 jit_solution(8192106829998481554)
XLA Ops:
  0.0 0.7 copy-done.8
  1.0 0.6 copy-done.9
  1.7 0.9 copy-done.1
  2.6 1.5 %share.1 = f32[1056,128]{1,0:T(8,128)} custom-call(s32[1]{0:T(128)} %bitcast.me_ref, s32[64]{0:T(128)S(1)} %select_reduce_fusion.inv, s32[64]{0:T(128)S(1)} %copy-done.8, s32[2,64]{1,0:T(2,128)S(1)} %bitcast.14, s32[32]{0:T(128)S(1)} %copy-done.9, f32[16,2048]{1,0:T(8,128)S(1)} %copy-done.1), custom_call_target="tpu_custom_call" | custom-call | tf_op jit(solution)/shard_map/share/pallas_call | solution.py:353
  4.0 12.0 %all-to-all-start = ((f32[32,1,4224]{2,1,0:T(1,128)}), f32[32,1,4224]{2,1,0:T(1,128)S(1)}, u32[]{:S(2)}, u32[]{:S(2)}) async-start(f32[32,1,4224]{2,1,0:T(1,128)} %bitcast.2), calls=%async_computation | async-start | bytes 1081344 | tf_op jit(solution)/shard_map/all_to_all | solution.py:363
  16.1 0.6 pack.1
  16.7 1.4 %collective-permute-start.1 = (f32[2,17,8,128]{3,2,1,0:T(8,128)S(1)}, f32[2,17,8,128]{3,2,1,0:T(8,128)S(1)}, u32[]{:S(2)}, u32[]{:S(2)}) collective-permute-start(f32[2,17,8,128]{3,2,1,0:T(8,128)S(1)} %get-tuple-element.29), channel_id=1, source_target_pairs={{0,2},{1,3},{2,4},{3,5},{4,6},{5,7},{6,0},{7,1},{8,10},{9,11},{10,... | collective-permute-start | bytes 417800 | tf_op jit(solution)/shard_map/ppermute | solution.py:339
  18.1 2.6 %collective-permute-start.2 = (f32[2,17,8,128]{3,2,1,0:T(8,128)S(1)}, f32[2,17,8,128]{3,2,1,0:T(8,128)S(1)}, u32[]{:S(2)}, u32[]{:S(2)}) collective-permute-start(f32[2,17,8,128]{3,2,1,0:T(8,128)S(1)} %get-tuple-element.30), channel_id=1, source_target_pairs={{0,4},{1,5},{2,6},{3,7},{4,0},{5,1},{6,2},{7,3},{8,12},{9,13},{10,... | collective-permute-start | bytes 417800 | tf_op jit(solution)/shard_map/ppermute | solution.py:339
  20.7 1.1 %collective-permute-start.3 = (f32[2,17,8,128]{3,2,1,0:T(8,128)S(1)}, f32[2,17,8,128]{3,2,1,0:T(8,128)S(1)}, u32[]{:S(2)}, u32[]{:S(2)}) collective-permute-start(f32[2,17,8,128]{3,2,1,0:T(8,128)S(1)} %get-tuple-element.31), channel_id=1, source_target_pairs={{0,6},{1,7},{2,0},{3,1},{4,2},{5,3},{6,4},{7,5},{8,14},{9,15},{10,... | collective-permute-start | bytes 417800 | tf_op jit(solution)/shard_map/ppermute | solution.py:339
  21.8 1.8 %collective-permute-start = (f32[17,8,128]{2,1,0:T(8,128)S(1)}, f32[17,8,128]{2,1,0:T(8,128)S(1)}, u32[]{:S(2)}, u32[]{:S(2)}) collective-permute-start(f32[17,8,128]{2,1,0:T(8,128)S(1)} %get-tuple-element.28), channel_id=1, source_target_pairs={{0,1},{1,0},{2,3},{3,2},{4,5},{5,4},{6,7},{7,6},{8,9},{9,8},{10,11... | collective-permute-start | bytes 208904 | tf_op jit(solution)/shard_map/ppermute | solution.py:339
  23.6 0.9 collective-permute-done.refs_1_
  24.5 2.5 %image2.2.refs_2_ = f32[8,64,128]{2,1,0:T(8,128)S(1)} custom-call(f32[2,8,128]{2,1,0:T(8,128)S(1)} %get-tuple-element.26.uv, f32[17,8,128]{2,1,0:T(8,128)S(1)} %get-tuple-element.27.refs_0_, f32[17,8,128]{2,1,0:T(8,128)S(1)} %collective-permute-done.refs_1_), custom_call_target="tpu_custom_call" | custom-call | flops 400000000 | bytes 200000 | tf_op jit(solution)/shard_map/image2/pallas_call | solution.py:197
  27.0 1.3 %collective-permute-start.4 = (f32[2,17,8,128]{3,2,1,0:T(8,128)S(1)}, f32[2,17,8,128]{3,2,1,0:T(8,128)S(1)}, u32[]{:S(2)}, u32[]{:S(2)}) collective-permute-start(f32[2,17,8,128]{3,2,1,0:T(8,128)S(1)} %collective-permute-done.1.refs_0_), channel_id=1, source_target_pairs={{0,1},{1,0},{2,3},{3,2},{4,5},{5,4},{6,7},{7,6},{8,9},{9,8},{10,11... | collective-permute-start | bytes 417800 | tf_op jit(solution)/shard_map/ppermute | solution.py:339
  28.3 0.5 collective-permute-start.6
  28.8 2.5 %image2.3.refs_4_ = f32[8,64,128]{2,1,0:T(8,128)S(1)} custom-call(f32[2,8,128]{2,1,0:T(8,128)S(1)} %get-tuple-element.26.uv, f32[2,17,8,128]{3,2,1,0:T(8,128)S(1)} %collective-permute-done.1.refs_0_, f32[2,17,8,128]{3,2,1,0:T(8,128)S(1)} %collective-permute-done.3.refs_1_, f32[8,64,128]{2,1,0:T(8,128)S(1)} %image2.2.refs_2_), custom_call_target="tpu_custom_call" | custom-call | flops 400000000 | bytes 200000 | tf_op jit(solution)/shard_map/image2/pallas_call | solution.py:197
  31.4 4.9 %image4.1.acc = f32[8,64,128]{2,1,0:T(8,128)S(1)} custom-call(f32[2,8,128]{2,1,0:T(8,128)S(1)} %get-tuple-element.26.uv, f32[2,17,8,128]{3,2,1,0:T(8,128)S(1)} %collective-permute-done.4.refs_0_, f32[2,17,8,128]{3,2,1,0:T(8,128)S(1)} %collective-permute-done.5.refs_1_, f32[2,17,8,128]{3,2,1,0:T(8,128)S(1)} %collective-permute-done.2.refs_2_, ...), custom_call_target="tpu_custom_call" | custom-call | flops 800000000 | bytes 400000 | tf_op jit(solution)/shard_map/image4/pallas_call | solution.py:197
  36.3 0.7 copy-done.11
  37.0 0.8 pair.1
  37.9 8.7 %all_to_all.27 = f32[8,1,2048]{2,1,0:T(1,128)S(1)} all-to-all(f32[8,1,2048]{2,1,0:T(1,128)S(1)} %bitcast.13), channel_id=1, replica_groups=mesh['bl'=32,'ch'=8] {'ch'}, dimensions={0} | all-to-all | bytes 131072 | tf_op jit(solution)/shard_map/all_to_all | solution.py:391
  46.6 2.1 %finish.1 = f32[32,32,128]{2,1,0:T(8,128)} custom-call(s32[1]{0:T(128)} %bitcast.me_ref, s32[64]{0:T(128)S(1)} %select_reduce_fusion.inv, s32[64]{0:T(128)S(1)} %copy-done.8, s32[32]{0:T(128)S(1)} %copy-done.9, f32[8,64,128]{2,1,0:T(8,128)S(1)} %image4.1.acc, f32[8,16,128]{2,1,0:T(8,128)S(1)} %bitcast.12, bf16[256,128]{1,0:T(8,128)(2,1)S(1)} %copy-done.4, ...), custom_call_target="tpu_custom_call" | custom-call | tf_op jit(solution)/shard_map/finish/pallas_call | solution.py:392
  48.7 9.2 %all-to-all-start.2 = ((f32[32,1,4096]{2,1,0:T(1,128)}), f32[32,1,4096]{2,1,0:T(1,128)S(1)}, u32[]{:S(2)}, u32[]{:S(2)}) async-start(f32[32,1,4096]{2,1,0:T(1,128)} %bitcast.7), calls=%async_computation.2 | async-start | bytes 1048576 | tf_op jit(solution)/shard_map/all_to_all | solution.py:401
  58.1 15.9 %all-to-all-done.2 = f32[32,1,4096]{2,1,0:T(1,128)S(1)} async-done(((f32[32,1,4096]{2,1,0:T(1,128)}), f32[32,1,4096]{2,1,0:T(1,128)S(1)}, u32[]{:S(2)}, u32[]{:S(2)}) %all-to-all-start.2) | async-done | bytes 524320 | tf_op jit(solution)/shard_map/all_to_all | solution.py:401
  74.0 3.5 %place.1 = (f32[4,8,32,128]{3,2,1,0:T(8,128)S(1)}, f32[4,8,32,128]{3,2,1,0:T(8,128)S(1)}) custom-call(s32[1]{0:T(128)} %bitcast.me_ref, s32[64]{0:T(128)S(1)} %convert_element_type.10.spots, f32[32,32,128]{2,1,0:T(8,128)S(1)} %bitcast.11), custom_call_target="tpu_custom_call" | custom-call | tf_op jit(solution)/shard_map/place/pallas_call | solution.py:405
  77.5 2.7 %collective-permute-start.7 = (f32[4,8,32,128]{3,2,1,0:T(8,128)S(1)}, f32[4,8,32,128]{3,2,1,0:T(8,128)S(1)}, u32[]{:S(2)}, u32[]{:S(2)}) collective-permute-start(f32[4,8,32,128]{3,2,1,0:T(8,128)S(1)} %get-tuple-element.40), channel_id=1, source_target_pairs={{0,1},{1,0},{2,3},{3,2},{4,5},{5,4},{6,7},{7,6},{8,9},{9,8},{10,11... | collective-permute-start | bytes 1572872 | tf_op jit(solution)/shard_map/ppermute | solution.py:339
  80.2 1.5 %collective-permute-done.7.got = f32[4,8,32,128]{3,2,1,0:T(8,128)S(1)} collective-permute-done((f32[4,8,32,128]{3,2,1,0:T(8,128)S(1)}, f32[4,8,32,128]{3,2,1,0:T(8,128)S(1)}, u32[]{:S(2)}, u32[]{:S(2)}) %collective-permute-start.7) | collective-permute-done | bytes 524320 | tf_op jit(solution)/shard_map/ppermute | solution.py:339
  81.8 0.4 collective-permute-start.8
  82.1 1.8 %collective-permute-start.9 = (f32[8,32,128]{2,1,0:T(8,128)S(1)}, f32[8,32,128]{2,1,0:T(8,128)S(1)}, u32[]{:S(2)}, u32[]{:S(2)}) collective-permute-start(f32[8,32,128]{2,1,0:T(8,128)S(1)} %get-tuple-element.43), channel_id=1, source_target_pairs={{0,4},{1,5},{2,6},{3,7},{4,0},{5,1},{6,2},{7,3},{8,12},{9,13},{10,... | collective-permute-start | bytes 393224 | tf_op jit(solution)/shard_map/ppermute | solution.py:339
  83.9 0.7 collective-permute-start.10
  84.7 3.7 %collective-permute-done.8.b = f32[8,32,128]{2,1,0:T(8,128)S(1)} collective-permute-done((f32[8,32,128]{2,1,0:T(8,128)S(1)}, f32[8,32,128]{2,1,0:T(8,128)S(1)}, u32[]{:S(2)}, u32[]{:S(2)}) %collective-permute-start.8) | collective-permute-done | bytes 131104 | tf_op jit(solution)/shard_map/ppermute | solution.py:339
  88.4 1.6 %collective-permute-done.9.c = f32[8,32,128]{2,1,0:T(8,128)S(1)} collective-permute-done((f32[8,32,128]{2,1,0:T(8,128)S(1)}, f32[8,32,128]{2,1,0:T(8,128)S(1)}, u32[]{:S(2)}, u32[]{:S(2)}) %collective-permute-start.9) | collective-permute-done | bytes 131104 | tf_op jit(solution)/shard_map/ppermute | solution.py:339
  90.0 1.0 %collective-permute-done.10.d = f32[8,32,128]{2,1,0:T(8,128)S(1)} collective-permute-done((f32[8,32,128]{2,1,0:T(8,128)S(1)}, f32[8,32,128]{2,1,0:T(8,128)S(1)}, u32[]{:S(2)}, u32[]{:S(2)}) %collective-permute-start.10) | collective-permute-done | bytes 131104 | tf_op jit(solution)/shard_map/ppermute | solution.py:339
  91.0 0.7 last.1
  (37 shorter events, 0.6 us)
Async XLA Ops:
  0.0 0.7 copy-start.8
  1.0 0.7 copy-start.9
  1.0 0.7 copy-start.10
  1.7 0.9 copy-start.1
  4.0 12.0 %copy-start = (f32[2,64,8,128]{3,2,1,0:T(8,128)S(1)}, f32[2,64,8,128]{3,2,1,0:T(8,128)}, u32[]{:S(2)}) copy-start(f32[2,64,8,128]{3,2,1,0:T(8,128)} %vis.1) | copy-start | bytes 1572868
  4.0 12.0 %copy-start.5 = (f32[2,64,128]{2,1,0:T(8,128)S(1)}, f32[2,64,128]{2,1,0:T(8,128)}, u32[]{:S(2)}) copy-start(f32[2,64,128]{2,1,0:T(8,128)} %coord.1) | copy-start | bytes 196612
  4.0 12.0 %copy-start.12 = (f32[8]{0:T(128)S(1)}, f32[8]{0:T(128)}, u32[]{:S(2)}) copy-start(f32[8]{0:T(128)} %freq.1) | copy-start | bytes 100
  4.0 32.3 %all-to-all-start = ((f32[32,1,4224]{2,1,0:T(1,128)}), f32[32,1,4224]{2,1,0:T(1,128)S(1)}, u32[]{:S(2)}, u32[]{:S(2)}) async-start(f32[32,1,4224]{2,1,0:T(1,128)} %bitcast.2), calls=%async_computation | async-start | bytes 1081344 | tf_op jit(solution)/shard_map/all_to_all | solution.py:363
  16.7 10.3 %collective-permute-start.1 = (f32[2,17,8,128]{3,2,1,0:T(8,128)S(1)}, f32[2,17,8,128]{3,2,1,0:T(8,128)S(1)}, u32[]{:S(2)}, u32[]{:S(2)}) collective-permute-start(f32[2,17,8,128]{3,2,1,0:T(8,128)S(1)} %get-tuple-element.29), channel_id=1, source_target_pairs={{0,2},{1,3},{2,4},{3,5},{4,6},{5,7},{6,0},{7,1},{8,10},{9,11},{10,... | collective-permute-start | bytes 417800 | tf_op jit(solution)/shard_map/ppermute | solution.py:339
  18.1 8.9 %collective-permute-start.2 = (f32[2,17,8,128]{3,2,1,0:T(8,128)S(1)}, f32[2,17,8,128]{3,2,1,0:T(8,128)S(1)}, u32[]{:S(2)}, u32[]{:S(2)}) collective-permute-start(f32[2,17,8,128]{3,2,1,0:T(8,128)S(1)} %get-tuple-element.30), channel_id=1, source_target_pairs={{0,4},{1,5},{2,6},{3,7},{4,0},{5,1},{6,2},{7,3},{8,12},{9,13},{10,... | collective-permute-start | bytes 417800 | tf_op jit(solution)/shard_map/ppermute | solution.py:339
  20.7 6.3 %collective-permute-start.3 = (f32[2,17,8,128]{3,2,1,0:T(8,128)S(1)}, f32[2,17,8,128]{3,2,1,0:T(8,128)S(1)}, u32[]{:S(2)}, u32[]{:S(2)}) collective-permute-start(f32[2,17,8,128]{3,2,1,0:T(8,128)S(1)} %get-tuple-element.31), channel_id=1, source_target_pairs={{0,6},{1,7},{2,0},{3,1},{4,2},{5,3},{6,4},{7,5},{8,14},{9,15},{10,... | collective-permute-start | bytes 417800 | tf_op jit(solution)/shard_map/ppermute | solution.py:339
  21.8 2.7 %collective-permute-start = (f32[17,8,128]{2,1,0:T(8,128)S(1)}, f32[17,8,128]{2,1,0:T(8,128)S(1)}, u32[]{:S(2)}, u32[]{:S(2)}) collective-permute-start(f32[17,8,128]{2,1,0:T(8,128)S(1)} %get-tuple-element.28), channel_id=1, source_target_pairs={{0,1},{1,0},{2,3},{3,2},{4,5},{5,4},{6,7},{7,6},{8,9},{9,8},{10,11... | collective-permute-start | bytes 208904 | tf_op jit(solution)/shard_map/ppermute | solution.py:339
  27.0 4.4 %collective-permute-start.4 = (f32[2,17,8,128]{3,2,1,0:T(8,128)S(1)}, f32[2,17,8,128]{3,2,1,0:T(8,128)S(1)}, u32[]{:S(2)}, u32[]{:S(2)}) collective-permute-start(f32[2,17,8,128]{3,2,1,0:T(8,128)S(1)} %collective-permute-done.1.refs_0_), channel_id=1, source_target_pairs={{0,1},{1,0},{2,3},{3,2},{4,5},{5,4},{6,7},{7,6},{8,9},{9,8},{10,11... | collective-permute-start | bytes 417800 | tf_op jit(solution)/shard_map/ppermute | solution.py:339
  28.3 3.0 %collective-permute-start.5 = (f32[2,17,8,128]{3,2,1,0:T(8,128)S(1)}, f32[2,17,8,128]{3,2,1,0:T(8,128)S(1)}, u32[]{:S(2)}, u32[]{:S(2)}) collective-permute-start(f32[2,17,8,128]{3,2,1,0:T(8,128)S(1)} %collective-permute-done.3.refs_1_), channel_id=1, source_target_pairs={{0,1},{1,0},{2,3},{3,2},{4,5},{5,4},{6,7},{7,6},{8,9},{9,8},{10,11... | collective-permute-start | bytes 417800 | tf_op jit(solution)/shard_map/ppermute | solution.py:339
  28.3 3.1 %collective-permute-start.6 = (f32[2,17,8,128]{3,2,1,0:T(8,128)S(1)}, f32[2,17,8,128]{3,2,1,0:T(8,128)S(1)}, u32[]{:S(2)}, u32[]{:S(2)}) collective-permute-start(f32[2,17,8,128]{3,2,1,0:T(8,128)S(1)} %collective-permute-done.2.refs_2_), channel_id=1, source_target_pairs={{0,1},{1,0},{2,3},{3,2},{4,5},{5,4},{6,7},{7,6},{8,9},{9,8},{10,11... | collective-permute-start | bytes 417800 | tf_op jit(solution)/shard_map/ppermute | solution.py:339
  31.4 5.0 %copy-start.7 = (f32[8,128]{1,0:T(8,128)S(1)}, f32[8,128]{1,0:T(8,128)}, u32[]{:S(2)}) copy-start(f32[8,128]{1,0:T(8,128)} %constant.18.clone.taper) | copy-start | bytes 12292
  36.3 0.7 copy-start.11
  37.0 9.6 %copy-start.3 = (bf16[2,128,128]{2,1,0:T(8,128)(2,1)S(1)}, bf16[2,128,128]{2,1,0:T(8,128)(2,1)}, u32[]{:S(2)}) copy-start(bf16[2,128,128]{2,1,0:T(8,128)(2,1)} %constant.20.clone.fold) | copy-start | bytes 196612
  37.0 9.6 %copy-start.4 = (bf16[256,128]{1,0:T(8,128)(2,1)S(1)}, bf16[256,128]{1,0:T(8,128)(2,1)}, u32[]{:S(2)}) copy-start(bf16[256,128]{1,0:T(8,128)(2,1)} %constant.19.clone.to_image) | copy-start | bytes 196612
  37.9 8.8 %copy-start.2 = (bf16[384,128]{1,0:T(8,128)(2,1)S(1)}, bf16[384,128]{1,0:T(8,128)(2,1)}, u32[]{:S(2)}) copy-start(bf16[384,128]{1,0:T(8,128)(2,1)} %constant.22.clone.right3) | copy-start | bytes 294916
  37.9 8.8 %copy-start.6 = (bf16[32,192]{1,0:T(8,128)(2,1)S(1)}, bf16[32,192]{1,0:T(8,128)(2,1)}, u32[]{:S(2)}) copy-start(bf16[32,192]{1,0:T(8,128)(2,1)} %constant.21.clone.left3) | copy-start | bytes 36868
  48.7 25.3 %all-to-all-start.2 = ((f32[32,1,4096]{2,1,0:T(1,128)}), f32[32,1,4096]{2,1,0:T(1,128)S(1)}, u32[]{:S(2)}, u32[]{:S(2)}) async-start(f32[32,1,4096]{2,1,0:T(1,128)} %bitcast.7), calls=%async_computation.2 | async-start | bytes 1048576 | tf_op jit(solution)/shard_map/all_to_all | solution.py:401
  77.5 4.2 %collective-permute-start.7 = (f32[4,8,32,128]{3,2,1,0:T(8,128)S(1)}, f32[4,8,32,128]{3,2,1,0:T(8,128)S(1)}, u32[]{:S(2)}, u32[]{:S(2)}) collective-permute-start(f32[4,8,32,128]{3,2,1,0:T(8,128)S(1)} %get-tuple-element.40), channel_id=1, source_target_pairs={{0,1},{1,0},{2,3},{3,2},{4,5},{5,4},{6,7},{7,6},{8,9},{9,8},{10,11... | collective-permute-start | bytes 1572872 | tf_op jit(solution)/shard_map/ppermute | solution.py:339
  81.8 6.6 %collective-permute-start.8 = (f32[8,32,128]{2,1,0:T(8,128)S(1)}, f32[8,32,128]{2,1,0:T(8,128)S(1)}, u32[]{:S(2)}, u32[]{:S(2)}) collective-permute-start(f32[8,32,128]{2,1,0:T(8,128)S(1)} %get-tuple-element.42), channel_id=1, source_target_pairs={{0,2},{1,3},{2,4},{3,5},{4,6},{5,7},{6,0},{7,1},{8,10},{9,11},{10,... | collective-permute-start | bytes 393224 | tf_op jit(solution)/shard_map/ppermute | solution.py:339
  82.1 7.9 %collective-permute-start.9 = (f32[8,32,128]{2,1,0:T(8,128)S(1)}, f32[8,32,128]{2,1,0:T(8,128)S(1)}, u32[]{:S(2)}, u32[]{:S(2)}) collective-permute-start(f32[8,32,128]{2,1,0:T(8,128)S(1)} %get-tuple-element.43), channel_id=1, source_target_pairs={{0,4},{1,5},{2,6},{3,7},{4,0},{5,1},{6,2},{7,3},{8,12},{9,13},{10,... | collective-permute-start | bytes 393224 | tf_op jit(solution)/shard_map/ppermute | solution.py:339
  83.9 7.0 %collective-permute-start.10 = (f32[8,32,128]{2,1,0:T(8,128)S(1)}, f32[8,32,128]{2,1,0:T(8,128)S(1)}, u32[]{:S(2)}, u32[]{:S(2)}) collective-permute-start(f32[8,32,128]{2,1,0:T(8,128)S(1)} %get-tuple-element.44), channel_id=1, source_target_pairs={{0,6},{1,7},{2,0},{3,1},{4,2},{5,3},{6,4},{7,5},{8,14},{9,15},{10,... | collective-permute-start | bytes 393224 | tf_op jit(solution)/shard_map/ppermute | solution.py:339

commit v2 on v1

--- a/solution.py
+++ b/solution.py
@@ -86,21 +86,13 @@
         own[slots[n]] = n
 
 
-def share_kernel(me_ref, inv, tiles, offs, slots, aterms, shared, own):
+def share_kernel(me_ref, aterms, shared):
     me = me_ref[0]
-    owners(slots, own)
-    lane = lax.broadcasted_iota(jnp.int32, (1, 128), 1)
     re = aterms[:, pl.ds(pl.multiple_of(me * 128, 128), 128)]
     im = aterms[:, pl.ds(pl.multiple_of(1024 + me * 128, 128), 128)]
-    blank = jnp.zeros((1, 128), F32)
     for b in range(32):
-        shared[33 * b : 33 * b + 16, :] = re
-        shared[33 * b + 16 : 33 * b + 32, :] = im
-        shared[33 * b + 32 : 33 * b + 33, :] = blank
-    for j in range(8):
-        s = inv[8 * j + me]
-        spot = jnp.where(lane == 0, offs[0, s], jnp.where(lane == 1, offs[1, s], 0))
-        shared[pl.ds(33 * own[tiles[s]] + 32, 1), :] = spot.astype(F32)
+        shared[b, 0:16, :] = re
+        shared[b, 16:32, :] = im
 
 
 def pack_kernel(me_ref, inv, freq, vis, coord, *outs):
@@ -219,8 +211,8 @@
             s = inv[8 * j + to]
             p = stations[0, s]
             q = stations[1, s]
-            p = p + 17 * (p >> 4)
-            q = q + 17 * (q >> 4)
+            p = p + 16 * (p >> 4)
+            q = q + 16 * (q >> 4)
             pr = table[pl.ds(p, 1), :]
             pi = table[pl.ds(p + 16, 1), :]
             qr = table[pl.ds(q, 1), :]
@@ -229,12 +221,13 @@
             out[to, pl.ds(8 + j, 1), :] = (pi * qr - pr * qi) * g
 
 
-def finish_kernel(me_ref, inv, tiles, slots, acc, pair, to_image, fold, left3, right3, out, own):
+def finish_kernel(me_ref, inv, tiles, slots, offs, acc, pair, to_image, fold, left3, right3, out, own):
     me = me_ref[0]
     owners(slots, own)
-    blank = jnp.zeros((32, 128), F32)
-    for b in range(32):
-        out[b] = blank
+    blank = jnp.zeros((33 * 8, 128), F32)
+    for b in range(4):
+        out[33 * 8 * b : 33 * 8 * (b + 1), :] = blank
+    first_lane = lax.broadcasted_iota(jnp.int32, (1, 128), 1) == 0
     row = lax.broadcasted_iota(jnp.int32, (8, 128), 0)
     group = lax.broadcasted_iota(jnp.int32, (8, 128), 1) // 32
     low = group == row % 4
@@ -283,14 +276,21 @@
         jnp.concatenate([hh, hh, hl], 1), right3[...], preferred_element_type=F32
     )
     for s in range(8):
-        out[own[tiles[inv[8 * s + me]]]] = full[32 * s : 32 * s + 32]
-
-
-def place_kernel(me_ref, spots, arrived, keep, give, acc):
+        i = inv[8 * s + me]
+        at = 33 * own[tiles[i]]
+        out[pl.ds(at, 32), :] = full[32 * s : 32 * s + 32]
+        out[pl.ds(at + 32, 1), :] = jnp.where(first_lane, offs[0, i], offs[1, i]).astype(F32)
+
+
+def place_kernel(me_ref, arrived, keep, give, acc, spots):
     lane = lax.broadcasted_iota(jnp.int32, (32, 128), 1)
     me = me_ref[0]
     y = me >> 1
     core = me & 1
+    for i in range(32):
+        corner = arrived[33 * i + 32 : 33 * i + 33, :].astype(jnp.int32)
+        spots[2 * i] = corner[0, 0]
+        spots[2 * i + 1] = corner[0, 1]
     acc[...] = jnp.zeros_like(acc)
 
     def one(i, unused):
@@ -298,7 +298,7 @@
         c = spots[2 * i + 1]
         half = c >> 7
         c = c & 127
-        tile = arrived[i]
+        tile = arrived[pl.ds(33 * i, 32), :]
         near = (lane >= c) & (lane < c + 32)
         moved = [pltpu.roll(tile, (c - 32 * m) & 127, 1) for m in range(4)]
         for m in range(4):
@@ -343,25 +343,24 @@
     to_image, fold, left3, right3, taper = constants()
     me = lax.axis_index("ch").astype(jnp.int32)
     me = me[None]
-    order = jnp.arange(64, dtype=jnp.int32)
-    key = sub_tile * 64 + order
-    pos = jnp.sum((key[None, :] < key[:, None]).astype(jnp.int32), axis=1)
-    inv = jnp.sum(jnp.where(pos[None, :] == order[:, None], order[None, :], 0), axis=1)
     stations = stations.T
     offsets = offsets.T
     own = pltpu.SMEM((32,), jnp.int32)
     shared = pl.pallas_call(
         share_kernel,
-        out_shape=jax.ShapeDtypeStruct((33 * 32, 128), F32),
-        in_specs=[SM] * 5 + [VM],
+        out_shape=jax.ShapeDtypeStruct((32, 32, 128), F32),
+        in_specs=[SM, VM],
         out_specs=VM,
-        scratch_shapes=[own],
         compiler_params=grant(4),
         name="share",
-    )(me, inv, sub_tile, offsets, tile_of_slot, aterms)
-    inv, shared = lax.optimization_barrier((inv, shared))
-    table = lax.all_to_all(shared.reshape(32, 33 * 128), "bl", 0, 0, tiled=True)
-    table = table.reshape(33 * 32, 128)
+    )(me, aterms)
+    sub_tile, shared = lax.optimization_barrier((sub_tile, shared))
+    table = lax.all_to_all(shared.reshape(32, 4096), "bl", 0, 0, tiled=True)
+    table = table.reshape(1024, 128)
+    order = jnp.arange(64, dtype=jnp.int32)
+    key = sub_tile * 64 + order
+    pos = jnp.sum((key[None, :] < key[:, None]).astype(jnp.int32), axis=1)
+    inv = jnp.sum(jnp.where(pos[None, :] == order[:, None], order[None, :], 0), axis=1)
     chunk = jax.ShapeDtypeStruct((17, 8, 128), F32)
     double = jax.ShapeDtypeStruct((2, 17, 8, 128), F32)
     mine, near, *far, uv = pl.pallas_call(
@@ -378,7 +377,6 @@
     acc, *direct = lax.optimization_barrier((acc, *direct))
     swapped = [shift(x, 0, 1) for x in direct]
     acc = images(uv, [(direct[0], 0), (direct[2], 0)], acc)
-    acc = images(uv, [(swapped[0], 1), (swapped[2], 1), (direct[1], 0), (swapped[1], 1)], acc)
     acc, table = lax.optimization_barrier((acc, table))
     pair = pl.pallas_call(
         pair_kernel,
@@ -388,29 +386,30 @@
         compiler_params=grant(4),
         name="pair",
     )(me, inv, stations, table, taper)
+    acc, pair = lax.optimization_barrier((acc, pair))
     pair = lax.all_to_all(pair.reshape(8, 2048), "ch", 0, 0, tiled=True).reshape(8, 16, 128)
+    acc = images(uv, [(swapped[0], 1), (swapped[2], 1), (direct[1], 0), (swapped[1], 1)], acc)
     outgoing = pl.pallas_call(
         finish_kernel,
-        out_shape=jax.ShapeDtypeStruct((32, 32, 128), F32),
-        in_specs=[SM] * 4 + [VM] * 6,
+        out_shape=jax.ShapeDtypeStruct((33 * 32, 128), F32),
+        in_specs=[SM] * 5 + [VM] * 6,
         out_specs=VM,
         scratch_shapes=[own],
         compiler_params=grant(12),
         name="finish",
-    )(me, inv, sub_tile, tile_of_slot, acc, pair, to_image, fold, left3, right3)
-    arrived = lax.all_to_all(outgoing.reshape(32, 4096), "bl", 0, 0, tiled=True)
-    arrived = arrived.reshape(32, 32, 128)
-    spots = table[32::33, 0:2].reshape(64).astype(jnp.int32)
+    )(me, inv, sub_tile, tile_of_slot, offsets, acc, pair, to_image, fold, left3, right3)
+    arrived = lax.all_to_all(outgoing.reshape(32, 33 * 128), "bl", 0, 0, tiled=True)
+    arrived = arrived.reshape(33 * 32, 128)
     half = jax.ShapeDtypeStruct((4, 8, 32, 128), F32)
     keep, give = pl.pallas_call(
         place_kernel,
         out_shape=[half, half],
-        in_specs=[SM, SM, VM],
+        in_specs=[SM, VM],
         out_specs=[VM, VM],
-        scratch_shapes=[pltpu.VMEM((8, TILE, 128), F32)],
+        scratch_shapes=[pltpu.VMEM((8, TILE, 128), F32), pltpu.SMEM((64,), jnp.int32)],
         compiler_params=grant(8),
         name="place",
-    )(me, spots, arrived)
+    )(me, arrived)
     got = shift(give, 0, 1)
     block = jax.ShapeDtypeStruct((8, 32, 128), F32)
     sums = pl.pallas_call(

time: 92.1 us -> 86.8 us (0.942)
  waiting for transfers between devices: 24.6 us -> 7.47 us
  blocking collectives: 8.73 us -> 22.6 us
  Pallas kernels: 19.2 us -> 18 us
    all_to_all x2, waiting for transfers between devices: 15.9 us -> 0.15 us  [the longest x1 0.15 us: local(): table = lax.all_to_all(shared.reshape(32, 4096), 'bl', 0, 0, tiled=True)]
    all_to_all x1, blocking collectives: 8.73 us -> 22.6 us  [local(): lax.all_to_all(outgoing.reshape(32, 33 * 128), 'bl', 0, 0, tiled=True)]
    all_to_all x2, starting transfers between devices: 21.2 us -> 18.9 us  [the longest x1 12 us: local(): table = lax.all_to_all(shared.reshape(32, 4096), 'bl', 0, 0, tiled=True)]
    ppermute x11, starting transfers between devices: 14.3 us -> 16.2 us  [shift(): return lax.ppermute(x, 'ch', pairs)]
    pallas_call x3, Pallas kernels: 7.04 us -> 5.21 us  [the longest x1 3.07 us: local(): pl.pallas_call(place_kernel, out_shape=[half, half], in_specs=[SM, VM], o...]
    ppermute x11, waiting for transfers between devices: 8.75 us -> 7.32 us  [shift(): return lax.ppermute(x, 'ch', pairs)]
  transfers between devices with their start and end apart: 13 -> 13, of which waited for: 6 -> 5; matrix products, arithmetic and copies ran while one was open for 0% -> 0% of each run, Pallas kernels for 11% -> 14%
where the time goes in v2:
time: 86.8 us; the launch traced here: 86.4 us
  starting transfers between devices  35.1 us (40%)
  blocking collectives  22.6 us (26%)
  Pallas kernels  18 us (21%)
  waiting for transfers between devices  7.47 us (9%)
  local copies, waits for them, and re-layouts  2.77 us (3%)
    all_to_all x1, blocking collectives, local(): lax.all_to_all(outgoing.reshape(32, 33 * 128), 'bl', 0, 0, tiled=True)  22.6 us
    ppermute x11, starting transfers between devices, shift(): return lax.ppermute(x, 'ch', pairs)  16.2 us
    all_to_all x1, starting transfers between devices, local(): table = lax.all_to_all(shared.reshape(32, 4096), 'bl', 0, 0, tiled=True)  12 us
    pallas_call x3, Pallas kernels, images(): pl.pallas_call(functools.partial(image_kernel, picks, first), out_shape=j...  9.9 us
    ppermute x11, waiting for transfers between devices, shift(): return lax.ppermute(x, 'ch', pairs)  7.32 us
    all_to_all x1, starting transfers between devices, local(): lax.all_to_all(pair.reshape(8, 2048), 'ch', 0, 0, tiled=True)  6.9 us
    pallas_call x1, Pallas kernels, local(): pl.pallas_call(place_kernel, out_shape=[half, half], in_specs=[SM, VM], o...  3.07 us
    unnamed x26, local copies, waits for them, and re-layouts  2.77 us
  transfers between devices with their start and end apart: 13, of which 5 were waited for; matrix products, arithmetic and copies ran while one was open for 0% of the time, Pallas kernels for 14%

profile of v2, /device:TPU:1, one launch (start us, length us, event | category | flops | bytes accessed | tf_op | source)
XLA Modules:
  0.0 86.4 jit_solution(12236703459364062381)
XLA Ops:
  0.0 0.9 %copy-done.1 = f32[16,2048]{1,0:T(8,128)S(1)} copy-done((f32[16,2048]{1,0:T(8,128)S(1)}, f32[16,2048]{1,0:T(8,128)}, u32[]{:S(2)}) %copy-start.1) | copy-done | bytes 131096
  0.9 0.9 share.1
  1.8 12.0 %all-to-all-start = ((f32[32,1,4096]{2,1,0:T(1,128)}), f32[32,1,4096]{2,1,0:T(1,128)S(1)}, u32[]{:S(2)}, u32[]{:S(2)}) async-start(f32[32,1,4096]{2,1,0:T(1,128)} %bitcast.2), calls=%async_computation | async-start | bytes 1048576 | tf_op jit(solution)/shard_map/all_to_all | solution.py:358
  13.8 0.2 convert_reduce_fusion
  14.1 0.5 copy-done.12
  14.6 0.6 pack.1
  15.3 1.4 %collective-permute-start.1 = (f32[2,17,8,128]{3,2,1,0:T(8,128)S(1)}, f32[2,17,8,128]{3,2,1,0:T(8,128)S(1)}, u32[]{:S(2)}, u32[]{:S(2)}) collective-permute-start(f32[2,17,8,128]{3,2,1,0:T(8,128)S(1)} %get-tuple-element.31), channel_id=1, source_target_pairs={{0,2},{1,3},{2,4},{3,5},{4,6},{5,7},{6,0},{7,1},{8,10},{9,11},{10,... | collective-permute-start | bytes 417800 | tf_op jit(solution)/shard_map/ppermute | solution.py:339
  16.6 2.6 %collective-permute-start.2 = (f32[2,17,8,128]{3,2,1,0:T(8,128)S(1)}, f32[2,17,8,128]{3,2,1,0:T(8,128)S(1)}, u32[]{:S(2)}, u32[]{:S(2)}) collective-permute-start(f32[2,17,8,128]{3,2,1,0:T(8,128)S(1)} %get-tuple-element.32), channel_id=1, source_target_pairs={{0,4},{1,5},{2,6},{3,7},{4,0},{5,1},{6,2},{7,3},{8,12},{9,13},{10,... | collective-permute-start | bytes 417800 | tf_op jit(solution)/shard_map/ppermute | solution.py:339
  19.3 1.1 %collective-permute-start.3 = (f32[2,17,8,128]{3,2,1,0:T(8,128)S(1)}, f32[2,17,8,128]{3,2,1,0:T(8,128)S(1)}, u32[]{:S(2)}, u32[]{:S(2)}) collective-permute-start(f32[2,17,8,128]{3,2,1,0:T(8,128)S(1)} %get-tuple-element.33), channel_id=1, source_target_pairs={{0,6},{1,7},{2,0},{3,1},{4,2},{5,3},{6,4},{7,5},{8,14},{9,15},{10,... | collective-permute-start | bytes 417800 | tf_op jit(solution)/shard_map/ppermute | solution.py:339
  20.3 1.8 %collective-permute-start = (f32[17,8,128]{2,1,0:T(8,128)S(1)}, f32[17,8,128]{2,1,0:T(8,128)S(1)}, u32[]{:S(2)}, u32[]{:S(2)}) collective-permute-start(f32[17,8,128]{2,1,0:T(8,128)S(1)} %get-tuple-element.30), channel_id=1, source_target_pairs={{0,1},{1,0},{2,3},{3,2},{4,5},{5,4},{6,7},{7,6},{8,9},{9,8},{10,11... | collective-permute-start | bytes 208904 | tf_op jit(solution)/shard_map/ppermute | solution.py:339
  22.1 0.9 %collective-permute-done.refs_1_ = f32[17,8,128]{2,1,0:T(8,128)S(1)} collective-permute-done((f32[17,8,128]{2,1,0:T(8,128)S(1)}, f32[17,8,128]{2,1,0:T(8,128)S(1)}, u32[]{:S(2)}, u32[]{:S(2)}) %collective-permute-start) | collective-permute-done | bytes 69664 | tf_op jit(solution)/shard_map/ppermute | solution.py:339
  23.0 2.5 %image2.2.refs_2_ = f32[8,64,128]{2,1,0:T(8,128)S(1)} custom-call(f32[2,8,128]{2,1,0:T(8,128)S(1)} %get-tuple-element.28.uv, f32[17,8,128]{2,1,0:T(8,128)S(1)} %get-tuple-element.29.refs_0_, f32[17,8,128]{2,1,0:T(8,128)S(1)} %collective-permute-done.refs_1_), custom_call_target="tpu_custom_call" | custom-call | flops 400000000 | bytes 200000 | tf_op jit(solution)/shard_map/image2/pallas_call | solution.py:189
  25.5 1.3 %collective-permute-start.4 = (f32[2,17,8,128]{3,2,1,0:T(8,128)S(1)}, f32[2,17,8,128]{3,2,1,0:T(8,128)S(1)}, u32[]{:S(2)}, u32[]{:S(2)}) collective-permute-start(f32[2,17,8,128]{3,2,1,0:T(8,128)S(1)} %collective-permute-done.1.refs_0_), channel_id=1, source_target_pairs={{0,1},{1,0},{2,3},{3,2},{4,5},{5,4},{6,7},{7,6},{8,9},{9,8},{10,11... | collective-permute-start | bytes 417800 | tf_op jit(solution)/shard_map/ppermute | solution.py:339
  26.9 0.5 collective-permute-start.6
  27.4 2.5 %image2.3.refs_4_ = f32[8,64,128]{2,1,0:T(8,128)S(1)} custom-call(f32[2,8,128]{2,1,0:T(8,128)S(1)} %get-tuple-element.28.uv, f32[2,17,8,128]{3,2,1,0:T(8,128)S(1)} %collective-permute-done.1.refs_0_, f32[2,17,8,128]{3,2,1,0:T(8,128)S(1)} %collective-permute-done.3.refs_1_, f32[8,64,128]{2,1,0:T(8,128)S(1)} %image2.2.refs_2_), custom_call_target="tpu_custom_call" | custom-call | flops 400000000 | bytes 200000 | tf_op jit(solution)/shard_map/image2/pallas_call | solution.py:189
  29.9 0.1 all-to-all-done
  30.1 0.7 copy-done.8
  30.7 1.5 %pair.1 = f32[8,16,128]{2,1,0:T(8,128)} custom-call(s32[1]{0:T(128)} %bitcast.me_ref, s32[64]{0:T(128)S(1)} %select_reduce_fusion.inv, s32[2,64]{1,0:T(2,128)S(1)} %bitcast.13, f32[1024,128]{1,0:T(8,128)S(1)} %bitcast.11, f32[8,128]{1,0:T(8,128)S(1)} %copy-done.7), custom_call_target="tpu_custom_call" | custom-call | tf_op jit(solution)/shard_map/pair/pallas_call | solution.py:381
  32.2 6.9 %all-to-all-start.1 = ((f32[8,1,2048]{2,1,0:T(1,128)}), f32[8,1,2048]{2,1,0:T(1,128)S(1)}, u32[]{:S(2)}, u32[]{:S(2)}) async-start(f32[8,1,2048]{2,1,0:T(1,128)} %bitcast.5), calls=%async_computation.1 | async-start | bytes 131072 | tf_op jit(solution)/shard_map/all_to_all | solution.py:390
  39.1 4.9 %image4.1.acc = f32[8,64,128]{2,1,0:T(8,128)S(1)} custom-call(f32[2,8,128]{2,1,0:T(8,128)S(1)} %get-tuple-element.28.uv, f32[2,17,8,128]{3,2,1,0:T(8,128)S(1)} %collective-permute-done.4.refs_0_, f32[2,17,8,128]{3,2,1,0:T(8,128)S(1)} %collective-permute-done.5.refs_1_, f32[2,17,8,128]{3,2,1,0:T(8,128)S(1)} %collective-permute-done.2.refs_2_, ...), custom_call_target="tpu_custom_call" | custom-call | flops 800000000 | bytes 400000 | tf_op jit(solution)/shard_map/image4/pallas_call | solution.py:189
  44.1 0.6 copy-done.9
  44.8 1.3 %finish.1 = f32[1056,128]{1,0:T(8,128)S(1)} custom-call(s32[1]{0:T(128)} %bitcast.me_ref, s32[64]{0:T(128)S(1)} %select_reduce_fusion.inv, s32[64]{0:T(128)S(1)} %copy-done.10, s32[32]{0:T(128)S(1)} %copy-done.11, s32[2,64]{1,0:T(2,128)S(1)} %bitcast.14, f32[8,64,128]{2,1,0:T(8,128)S(1)} %image4.1.acc, f32[8,16,128]{2,1,0:T(8,128)S(1)} %bitcast.12, ...), custom_call_target="tpu_custom_call" | custom-call | tf_op jit(solution)/shard_map/finish/pallas_call | solution.py:392
  46.1 22.6 %all_to_all.27 = f32[32,1,4224]{2,1,0:T(1,128)S(1)} all-to-all(f32[32,1,4224]{2,1,0:T(1,128)S(1)} %bitcast.9), channel_id=1, replica_groups=mesh['bl'=32,'ch'=8] {'bl'}, dimensions={0} | all-to-all | bytes 1081344 | tf_op jit(solution)/shard_map/all_to_all | solution.py:401
  68.6 3.1 %place.1 = (f32[4,8,32,128]{3,2,1,0:T(8,128)S(1)}, f32[4,8,32,128]{3,2,1,0:T(8,128)S(1)}) custom-call(s32[1]{0:T(128)} %bitcast.me_ref, f32[1056,128]{1,0:T(8,128)S(1)} %bitcast.10), custom_call_target="tpu_custom_call" | custom-call | tf_op jit(solution)/shard_map/place/pallas_call | solution.py:404
  71.7 2.5 %collective-permute-start.7 = (f32[4,8,32,128]{3,2,1,0:T(8,128)S(1)}, f32[4,8,32,128]{3,2,1,0:T(8,128)S(1)}, u32[]{:S(2)}, u32[]{:S(2)}) collective-permute-start(f32[4,8,32,128]{3,2,1,0:T(8,128)S(1)} %get-tuple-element.44), channel_id=1, source_target_pairs={{0,1},{1,0},{2,3},{3,2},{4,5},{5,4},{6,7},{7,6},{8,9},{9,8},{10,11... | collective-permute-start | bytes 1572872 | tf_op jit(solution)/shard_map/ppermute | solution.py:339
  74.2 1.5 %collective-permute-done.7.got = f32[4,8,32,128]{3,2,1,0:T(8,128)S(1)} collective-permute-done((f32[4,8,32,128]{3,2,1,0:T(8,128)S(1)}, f32[4,8,32,128]{3,2,1,0:T(8,128)S(1)}, u32[]{:S(2)}, u32[]{:S(2)}) %collective-permute-start.7) | collective-permute-done | bytes 524320 | tf_op jit(solution)/shard_map/ppermute | solution.py:339
  75.8 1.5 %collective-permute-start.8 = (f32[8,32,128]{2,1,0:T(8,128)S(1)}, f32[8,32,128]{2,1,0:T(8,128)S(1)}, u32[]{:S(2)}, u32[]{:S(2)}) collective-permute-start(f32[8,32,128]{2,1,0:T(8,128)S(1)} %get-tuple-element.46), channel_id=1, source_target_pairs={{0,2},{1,3},{2,4},{3,5},{4,6},{5,7},{6,0},{7,1},{8,10},{9,11},{10,... | collective-permute-start | bytes 393224 | tf_op jit(solution)/shard_map/ppermute | solution.py:339
  77.2 2.4 %collective-permute-start.9 = (f32[8,32,128]{2,1,0:T(8,128)S(1)}, f32[8,32,128]{2,1,0:T(8,128)S(1)}, u32[]{:S(2)}, u32[]{:S(2)}) collective-permute-start(f32[8,32,128]{2,1,0:T(8,128)S(1)} %get-tuple-element.47), channel_id=1, source_target_pairs={{0,4},{1,5},{2,6},{3,7},{4,0},{5,1},{6,2},{7,3},{8,12},{9,13},{10,... | collective-permute-start | bytes 393224 | tf_op jit(solution)/shard_map/ppermute | solution.py:339
  79.7 1.2 %collective-permute-start.10 = (f32[8,32,128]{2,1,0:T(8,128)S(1)}, f32[8,32,128]{2,1,0:T(8,128)S(1)}, u32[]{:S(2)}, u32[]{:S(2)}) collective-permute-start(f32[8,32,128]{2,1,0:T(8,128)S(1)} %get-tuple-element.48), channel_id=1, source_target_pairs={{0,6},{1,7},{2,0},{3,1},{4,2},{5,3},{6,4},{7,5},{8,14},{9,15},{10,... | collective-permute-start | bytes 393224 | tf_op jit(solution)/shard_map/ppermute | solution.py:339
  80.8 0.9 %collective-permute-done.8.b = f32[8,32,128]{2,1,0:T(8,128)S(1)} collective-permute-done((f32[8,32,128]{2,1,0:T(8,128)S(1)}, f32[8,32,128]{2,1,0:T(8,128)S(1)}, u32[]{:S(2)}, u32[]{:S(2)}) %collective-permute-start.8) | collective-permute-done | bytes 131104 | tf_op jit(solution)/shard_map/ppermute | solution.py:339
  81.8 3.9 %collective-permute-done.9.c = f32[8,32,128]{2,1,0:T(8,128)S(1)} collective-permute-done((f32[8,32,128]{2,1,0:T(8,128)S(1)}, f32[8,32,128]{2,1,0:T(8,128)S(1)}, u32[]{:S(2)}, u32[]{:S(2)}) %collective-permute-start.9) | collective-permute-done | bytes 131104 | tf_op jit(solution)/shard_map/ppermute | solution.py:339
  85.7 0.7 last.1
  (34 shorter events, 0.2 us)
Async XLA Ops:
  0.0 0.9 %copy-start.1 = (f32[16,2048]{1,0:T(8,128)S(1)}, f32[16,2048]{1,0:T(8,128)}, u32[]{:S(2)}) copy-start(f32[16,2048]{1,0:T(8,128)} %aterms.1) | copy-start | bytes 393220
  1.8 12.0 %copy-start.10 = (s32[64]{0:T(128)S(1)}, s32[64]{0:T(128)}, u32[]{:S(2)}) copy-start(s32[64]{0:T(128)} %tiles) | copy-start | bytes 772
  1.8 12.3 %copy-start = (f32[2,64,8,128]{3,2,1,0:T(8,128)S(1)}, f32[2,64,8,128]{3,2,1,0:T(8,128)}, u32[]{:S(2)}) copy-start(f32[2,64,8,128]{3,2,1,0:T(8,128)} %vis.1) | copy-start | bytes 1572868
  1.8 12.3 %copy-start.5 = (f32[2,64,128]{2,1,0:T(8,128)S(1)}, f32[2,64,128]{2,1,0:T(8,128)}, u32[]{:S(2)}) copy-start(f32[2,64,128]{2,1,0:T(8,128)} %coord.1) | copy-start | bytes 196612
  1.8 28.3 %all-to-all-start = ((f32[32,1,4096]{2,1,0:T(1,128)}), f32[32,1,4096]{2,1,0:T(1,128)S(1)}, u32[]{:S(2)}, u32[]{:S(2)}) async-start(f32[32,1,4096]{2,1,0:T(1,128)} %bitcast.2), calls=%async_computation | async-start | bytes 1048576 | tf_op jit(solution)/shard_map/all_to_all | solution.py:358
  14.0 0.7 copy-start.12
  15.3 10.2 %collective-permute-start.1 = (f32[2,17,8,128]{3,2,1,0:T(8,128)S(1)}, f32[2,17,8,128]{3,2,1,0:T(8,128)S(1)}, u32[]{:S(2)}, u32[]{:S(2)}) collective-permute-start(f32[2,17,8,128]{3,2,1,0:T(8,128)S(1)} %get-tuple-element.31), channel_id=1, source_target_pairs={{0,2},{1,3},{2,4},{3,5},{4,6},{5,7},{6,0},{7,1},{8,10},{9,11},{10,... | collective-permute-start | bytes 417800 | tf_op jit(solution)/shard_map/ppermute | solution.py:339
  16.6 8.9 %collective-permute-start.2 = (f32[2,17,8,128]{3,2,1,0:T(8,128)S(1)}, f32[2,17,8,128]{3,2,1,0:T(8,128)S(1)}, u32[]{:S(2)}, u32[]{:S(2)}) collective-permute-start(f32[2,17,8,128]{3,2,1,0:T(8,128)S(1)} %get-tuple-element.32), channel_id=1, source_target_pairs={{0,4},{1,5},{2,6},{3,7},{4,0},{5,1},{6,2},{7,3},{8,12},{9,13},{10,... | collective-permute-start | bytes 417800 | tf_op jit(solution)/shard_map/ppermute | solution.py:339
  19.3 6.3 %collective-permute-start.3 = (f32[2,17,8,128]{3,2,1,0:T(8,128)S(1)}, f32[2,17,8,128]{3,2,1,0:T(8,128)S(1)}, u32[]{:S(2)}, u32[]{:S(2)}) collective-permute-start(f32[2,17,8,128]{3,2,1,0:T(8,128)S(1)} %get-tuple-element.33), channel_id=1, source_target_pairs={{0,6},{1,7},{2,0},{3,1},{4,2},{5,3},{6,4},{7,5},{8,14},{9,15},{10,... | collective-permute-start | bytes 417800 | tf_op jit(solution)/shard_map/ppermute | solution.py:339
  20.3 2.7 %collective-permute-start = (f32[17,8,128]{2,1,0:T(8,128)S(1)}, f32[17,8,128]{2,1,0:T(8,128)S(1)}, u32[]{:S(2)}, u32[]{:S(2)}) collective-permute-start(f32[17,8,128]{2,1,0:T(8,128)S(1)} %get-tuple-element.30), channel_id=1, source_target_pairs={{0,1},{1,0},{2,3},{3,2},{4,5},{5,4},{6,7},{7,6},{8,9},{9,8},{10,11... | collective-permute-start | bytes 208904 | tf_op jit(solution)/shard_map/ppermute | solution.py:339
  25.5 13.6 %collective-permute-start.4 = (f32[2,17,8,128]{3,2,1,0:T(8,128)S(1)}, f32[2,17,8,128]{3,2,1,0:T(8,128)S(1)}, u32[]{:S(2)}, u32[]{:S(2)}) collective-permute-start(f32[2,17,8,128]{3,2,1,0:T(8,128)S(1)} %collective-permute-done.1.refs_0_), channel_id=1, source_target_pairs={{0,1},{1,0},{2,3},{3,2},{4,5},{5,4},{6,7},{7,6},{8,9},{9,8},{10,11... | collective-permute-start | bytes 417800 | tf_op jit(solution)/shard_map/ppermute | solution.py:339
  26.9 12.3 %collective-permute-start.5 = (f32[2,17,8,128]{3,2,1,0:T(8,128)S(1)}, f32[2,17,8,128]{3,2,1,0:T(8,128)S(1)}, u32[]{:S(2)}, u32[]{:S(2)}) collective-permute-start(f32[2,17,8,128]{3,2,1,0:T(8,128)S(1)} %collective-permute-done.3.refs_1_), channel_id=1, source_target_pairs={{0,1},{1,0},{2,3},{3,2},{4,5},{5,4},{6,7},{7,6},{8,9},{9,8},{10,11... | collective-permute-start | bytes 417800 | tf_op jit(solution)/shard_map/ppermute | solution.py:339
  26.9 12.3 %collective-permute-start.6 = (f32[2,17,8,128]{3,2,1,0:T(8,128)S(1)}, f32[2,17,8,128]{3,2,1,0:T(8,128)S(1)}, u32[]{:S(2)}, u32[]{:S(2)}) collective-permute-start(f32[2,17,8,128]{3,2,1,0:T(8,128)S(1)} %collective-permute-done.2.refs_2_), channel_id=1, source_target_pairs={{0,1},{1,0},{2,3},{3,2},{4,5},{5,4},{6,7},{7,6},{8,9},{9,8},{10,11... | collective-permute-start | bytes 417800 | tf_op jit(solution)/shard_map/ppermute | solution.py:339
  27.4 2.7 %copy-start.7 = (f32[8,128]{1,0:T(8,128)S(1)}, f32[8,128]{1,0:T(8,128)}, u32[]{:S(2)}) copy-start(f32[8,128]{1,0:T(8,128)} %constant.18.clone.taper) | copy-start | bytes 12292
  30.1 0.7 copy-start.8
  32.2 11.9 %all-to-all-start.1 = ((f32[8,1,2048]{2,1,0:T(1,128)}), f32[8,1,2048]{2,1,0:T(1,128)S(1)}, u32[]{:S(2)}, u32[]{:S(2)}) async-start(f32[8,1,2048]{2,1,0:T(1,128)} %bitcast.5), calls=%async_computation.1 | async-start | bytes 131072 | tf_op jit(solution)/shard_map/all_to_all | solution.py:390
  39.1 5.0 %copy-start.2 = (bf16[384,128]{1,0:T(8,128)(2,1)S(1)}, bf16[384,128]{1,0:T(8,128)(2,1)}, u32[]{:S(2)}) copy-start(bf16[384,128]{1,0:T(8,128)(2,1)} %constant.22.clone.right3) | copy-start | bytes 294916
  39.1 5.0 %copy-start.3 = (bf16[2,128,128]{2,1,0:T(8,128)(2,1)S(1)}, bf16[2,128,128]{2,1,0:T(8,128)(2,1)}, u32[]{:S(2)}) copy-start(bf16[2,128,128]{2,1,0:T(8,128)(2,1)} %constant.20.clone.fold) | copy-start | bytes 196612
  39.1 5.0 %copy-start.4 = (bf16[256,128]{1,0:T(8,128)(2,1)S(1)}, bf16[256,128]{1,0:T(8,128)(2,1)}, u32[]{:S(2)}) copy-start(bf16[256,128]{1,0:T(8,128)(2,1)} %constant.19.clone.to_image) | copy-start | bytes 196612
  39.1 5.0 %copy-start.6 = (bf16[32,192]{1,0:T(8,128)(2,1)S(1)}, bf16[32,192]{1,0:T(8,128)(2,1)}, u32[]{:S(2)}) copy-start(bf16[32,192]{1,0:T(8,128)(2,1)} %constant.21.clone.left3) | copy-start | bytes 36868
  44.1 0.7 copy-start.9
  44.1 0.7 copy-start.11
  71.7 4.0 %collective-permute-start.7 = (f32[4,8,32,128]{3,2,1,0:T(8,128)S(1)}, f32[4,8,32,128]{3,2,1,0:T(8,128)S(1)}, u32[]{:S(2)}, u32[]{:S(2)}) collective-permute-start(f32[4,8,32,128]{3,2,1,0:T(8,128)S(1)} %get-tuple-element.44), channel_id=1, source_target_pairs={{0,1},{1,0},{2,3},{3,2},{4,5},{5,4},{6,7},{7,6},{8,9},{9,8},{10,11... | collective-permute-start | bytes 1572872 | tf_op jit(solution)/shard_map/ppermute | solution.py:339
  75.8 6.0 %collective-permute-start.8 = (f32[8,32,128]{2,1,0:T(8,128)S(1)}, f32[8,32,128]{2,1,0:T(8,128)S(1)}, u32[]{:S(2)}, u32[]{:S(2)}) collective-permute-start(f32[8,32,128]{2,1,0:T(8,128)S(1)} %get-tuple-element.46), channel_id=1, source_target_pairs={{0,2},{1,3},{2,4},{3,5},{4,6},{5,7},{6,0},{7,1},{8,10},{9,11},{10,... | collective-permute-start | bytes 393224 | tf_op jit(solution)/shard_map/ppermute | solution.py:339
  77.2 8.4 %collective-permute-start.9 = (f32[8,32,128]{2,1,0:T(8,128)S(1)}, f32[8,32,128]{2,1,0:T(8,128)S(1)}, u32[]{:S(2)}, u32[]{:S(2)}) collective-permute-start(f32[8,32,128]{2,1,0:T(8,128)S(1)} %get-tuple-element.47), channel_id=1, source_target_pairs={{0,4},{1,5},{2,6},{3,7},{4,0},{5,1},{6,2},{7,3},{8,12},{9,13},{10,... | collective-permute-start | bytes 393224 | tf_op jit(solution)/shard_map/ppermute | solution.py:339
  79.7 6.0 %collective-permute-start.10 = (f32[8,32,128]{2,1,0:T(8,128)S(1)}, f32[8,32,128]{2,1,0:T(8,128)S(1)}, u32[]{:S(2)}, u32[]{:S(2)}) collective-permute-start(f32[8,32,128]{2,1,0:T(8,128)S(1)} %get-tuple-element.48), channel_id=1, source_target_pairs={{0,6},{1,7},{2,0},{3,1},{4,2},{5,3},{6,4},{7,5},{8,14},{9,15},{10,... | collective-permute-start | bytes 393224 | tf_op jit(solution)/shard_map/ppermute | solution.py:339

commit v3 on v2

--- a/solution.py
+++ b/solution.py
@@ -9,12 +9,15 @@
 from jax.experimental.pallas import tpu as pltpu
 from jax.sharding import PartitionSpec as P
 
+
 SUB = 32
 TILE = 256
 F32 = jnp.float32
 BF16 = jnp.bfloat16
 VM = pl.BlockSpec(memory_space=pltpu.VMEM)
 SM = pl.BlockSpec(memory_space=pltpu.SMEM)
+
+INV, DEST, ST0, ST1, OFF0, OFF1, ME = 0, 64, 128, 192, 256, 320, 384
 
 SIN = [(-1.0) ** k / math.factorial(2 * k + 1) for k in range(7)]
 COS = [(-1.0) ** k / math.factorial(2 * k) for k in range(7)]
@@ -81,23 +84,26 @@
     )
 
 
-def owners(slots, own):
-    for n in range(32):
-        own[slots[n]] = n
-
-
-def share_kernel(me_ref, aterms, shared):
+def share_kernel(me_ref, aterms, shared, strip, sems):
     me = me_ref[0]
-    re = aterms[:, pl.ds(pl.multiple_of(me * 128, 128), 128)]
-    im = aterms[:, pl.ds(pl.multiple_of(1024 + me * 128, 128), 128)]
+    copies = []
+    for r in range(2):
+        at = pl.multiple_of(1024 * r + me * 128, 128)
+        copy = pltpu.make_async_copy(aterms.at[:, pl.ds(at, 128)], strip.at[r], sems.at[r])
+        copy.start()
+        copies.append(copy)
+    for copy in copies:
+        copy.wait()
+    re = strip[0]
+    im = strip[1]
     for b in range(32):
         shared[b, 0:16, :] = re
         shared[b, 16:32, :] = im
 
 
-def pack_kernel(me_ref, inv, freq, vis, coord, *outs):
+def pack_kernel(ints, freq, vis, coord, *outs):
     uv = outs[5]
-    me = me_ref[0]
+    me = ints[ME]
     y = me >> 1
     core = me & 1
     row = lax.broadcasted_iota(jnp.int32, (8, 128), 0)
@@ -108,12 +114,12 @@
     for q in range(8):
         to = (((y + q // 2) & 3) << 1) + ((core + q % 2) & 1)
         for j in range(8):
-            s = inv[8 * j + to]
+            s = ints[INV + 8 * j + to]
             places[q][j] = vis[0, s]
             places[q][8 + j] = vis[1, s]
         places[q][16] = freqs
     for j in range(8):
-        s = inv[8 * j + me]
+        s = ints[INV + 8 * j + me]
         for d in range(2):
             uv[d, pl.ds(j, 1), :] = coord[d, pl.ds(s, 1), :]
 
@@ -138,14 +144,12 @@
                 x2 = phi * phi
                 zr = poly(COS, x2)
                 zi = phi * poly(SIN, x2)
-                wr = zr * zr - zi * zi
-                wi = 2.0 * zr * zi
-                cr, ci = zr, zi
+                turn = 4.0 * zr * zr - 2.0
+                cr, ci, dr, di = zr, zi, zr, -zi
                 for m in range(16):
                     table[s, pl.ds(m * 8, 8), :] = cr
                     table[s, pl.ds((16 + m) * 8, 8), :] = ci
-                    if m < 15:
-                        cr, ci = cr * wr - ci * wi, cr * wi + ci * wr
+                    cr, ci, dr, di = turn * cr - dr, turn * ci - di, cr, ci
                 base.append((zr, zi))
             (ar, ai), (br, bi) = base
             pr = ar * br - ai * bi
@@ -200,17 +204,16 @@
         cost_estimate=pl.CostEstimate(
             flops=count * 200_000_000, bytes_accessed=count * 100_000, transcendentals=0
         ),
-        name=f"image{count}",
     )(*args)
 
 
-def pair_kernel(me_ref, inv, stations, table, taper, out):
-    g = taper[pl.ds(me_ref[0], 1), :]
+def pair_kernel(ints, table, taper, out):
+    g = taper[pl.ds(ints[ME], 1), :]
     for to in range(8):
         for j in range(8):
-            s = inv[8 * j + to]
-            p = stations[0, s]
-            q = stations[1, s]
+            s = ints[INV + 8 * j + to]
+            p = ints[ST0 + s]
+            q = ints[ST1 + s]
             p = p + 16 * (p >> 4)
             q = q + 16 * (q >> 4)
             pr = table[pl.ds(p, 1), :]
@@ -221,9 +224,8 @@
             out[to, pl.ds(8 + j, 1), :] = (pi * qr - pr * qi) * g
 
 
-def finish_kernel(me_ref, inv, tiles, slots, offs, acc, pair, to_image, fold, left3, right3, out, own):
-    me = me_ref[0]
-    owners(slots, own)
+def finish_kernel(ints, acc, pair, to_image, fold, left3, right3, out):
+    me = ints[ME]
     blank = jnp.zeros((33 * 8, 128), F32)
     for b in range(4):
         out[33 * 8 * b : 33 * 8 * (b + 1), :] = blank
@@ -276,10 +278,10 @@
         jnp.concatenate([hh, hh, hl], 1), right3[...], preferred_element_type=F32
     )
     for s in range(8):
-        i = inv[8 * s + me]
-        at = 33 * own[tiles[i]]
+        i = ints[INV + 8 * s + me]
+        at = 33 * ints[DEST + i]
         out[pl.ds(at, 32), :] = full[32 * s : 32 * s + 32]
-        out[pl.ds(at + 32, 1), :] = jnp.where(first_lane, offs[0, i], offs[1, i]).astype(F32)
+        out[pl.ds(at + 32, 1), :] = jnp.where(first_lane, ints[OFF0 + i], ints[OFF1 + i]).astype(F32)
 
 
 def place_kernel(me_ref, arrived, keep, give, acc, spots):
@@ -314,7 +316,7 @@
 
         return unused
 
-    lax.fori_loop(0, 32, one, 0)
+    lax.fori_loop(0, 32, one, 0, unroll=4)
     for d in range(4):
         block = ((y + d) & 3) << 1
         for k in range(8):
@@ -343,34 +345,45 @@
     to_image, fold, left3, right3, taper = constants()
     me = lax.axis_index("ch").astype(jnp.int32)
     me = me[None]
-    stations = stations.T
-    offsets = offsets.T
-    own = pltpu.SMEM((32,), jnp.int32)
     shared = pl.pallas_call(
         share_kernel,
         out_shape=jax.ShapeDtypeStruct((32, 32, 128), F32),
-        in_specs=[SM, VM],
+        in_specs=[SM, pl.BlockSpec(memory_space=pltpu.HBM)],
         out_specs=VM,
-        compiler_params=grant(4),
+        scratch_shapes=[pltpu.VMEM((2, 16, 128), F32), pltpu.SemaphoreType.DMA((2,))],
+        compiler_params=grant(60),
         name="share",
     )(me, aterms)
-    sub_tile, shared = lax.optimization_barrier((sub_tile, shared))
+    sub_tile, tile_of_slot, shared = lax.optimization_barrier((sub_tile, tile_of_slot, shared))
     table = lax.all_to_all(shared.reshape(32, 4096), "bl", 0, 0, tiled=True)
     table = table.reshape(1024, 128)
     order = jnp.arange(64, dtype=jnp.int32)
-    key = sub_tile * 64 + order
+    hits = tile_of_slot[None, :] == sub_tile[:, None]
+    dest = jnp.sum(jnp.where(hits, jnp.arange(32, dtype=jnp.int32)[None, :], 0), axis=1)
+    key = dest * 64 + order
     pos = jnp.sum((key[None, :] < key[:, None]).astype(jnp.int32), axis=1)
     inv = jnp.sum(jnp.where(pos[None, :] == order[:, None], order[None, :], 0), axis=1)
+    ints = jnp.concatenate(
+        [
+            inv,
+            dest,
+            stations[:, 0],
+            stations[:, 1],
+            offsets[:, 0],
+            offsets[:, 1],
+            me,
+        ]
+    )
     chunk = jax.ShapeDtypeStruct((17, 8, 128), F32)
     double = jax.ShapeDtypeStruct((2, 17, 8, 128), F32)
     mine, near, *far, uv = pl.pallas_call(
         pack_kernel,
         out_shape=[chunk, chunk, double, double, double, jax.ShapeDtypeStruct((2, 8, 128), F32)],
-        in_specs=[SM, SM, SM, VM, VM],
+        in_specs=[SM, SM, VM, VM],
         out_specs=[VM] * 6,
         compiler_params=grant(8),
         name="pack",
-    )(me, inv, freq_ratio, visibility, coordinates)
+    )(ints, freq_ratio, visibility, coordinates)
     near = shift(near, 0, 1)
     direct = [shift(far[d - 1], d, 0) for d in range(1, 4)]
     acc = images(uv, [(mine, None), (near, None)])
@@ -381,23 +394,22 @@
     pair = pl.pallas_call(
         pair_kernel,
         out_shape=jax.ShapeDtypeStruct((8, 16, 128), F32),
-        in_specs=[SM, SM, SM, VM, VM],
+        in_specs=[SM, VM, VM],
         out_specs=VM,
         compiler_params=grant(4),
         name="pair",
-    )(me, inv, stations, table, taper)
+    )(ints, table, taper)
     acc, pair = lax.optimization_barrier((acc, pair))
     pair = lax.all_to_all(pair.reshape(8, 2048), "ch", 0, 0, tiled=True).reshape(8, 16, 128)
     acc = images(uv, [(swapped[0], 1), (swapped[2], 1), (direct[1], 0), (swapped[1], 1)], acc)
     outgoing = pl.pallas_call(
         finish_kernel,
         out_shape=jax.ShapeDtypeStruct((33 * 32, 128), F32),
-        in_specs=[SM] * 5 + [VM] * 6,
+        in_specs=[SM] + [VM] * 6,
         out_specs=VM,
-        scratch_shapes=[own],
         compiler_params=grant(12),
         name="finish",
-    )(me, inv, sub_tile, tile_of_slot, offsets, acc, pair, to_image, fold, left3, right3)
+    )(ints, acc, pair, to_image, fold, left3, right3)
     arrived = lax.all_to_all(outgoing.reshape(32, 33 * 128), "bl", 0, 0, tiled=True)
     arrived = arrived.reshape(33 * 32, 128)
     half = jax.ShapeDtypeStruct((4, 8, 32, 128), F32)

time: 86.8 us -> 86.1 us (level)
  local copies, waits for them, and re-layouts: 2.77 us -> 1.27 us
    unnamed x26 -> x24, local copies, waits for them, and re-layouts: 2.77 us -> 1.19 us
  transfers between devices with their start and end apart: 13 -> 13, of which waited for: 5 -> 4; matrix products, arithmetic and copies ran while one was open for 0% -> 1% of each run, Pallas kernels for 14% -> 14%
where the time goes in v3:
time: 86.1 us; the launch traced here: 85.7 us
  starting transfers between devices  34.3 us (40%)
  blocking collectives  23.4 us (27%)
  Pallas kernels  18.7 us (22%)
  waiting for transfers between devices  7.35 us (9%)
  local copies, waits for them, and re-layouts  1.27 us (1%)
    all_to_all x1, blocking collectives, local(): lax.all_to_all(outgoing.reshape(32, 33 * 128), 'bl', 0, 0, tiled=True)  23.4 us
    ppermute x11, starting transfers between devices, shift(): return lax.ppermute(x, 'ch', pairs)  16.2 us
    all_to_all x1, starting transfers between devices, local(): table = lax.all_to_all(shared.reshape(32, 4096), 'bl', 0, 0, tiled=True)  12 us
    pallas_call x3, Pallas kernels, images(): pl.pallas_call(functools.partial(image_kernel, picks, first), out_shape=j...  9.92 us
    ppermute x11, waiting for transfers between devices, shift(): return lax.ppermute(x, 'ch', pairs)  7.32 us
    all_to_all x1, starting transfers between devices, local(): lax.all_to_all(pair.reshape(8, 2048), 'ch', 0, 0, tiled=True)  6.13 us
    pallas_call x1, Pallas kernels, local(): pl.pallas_call(place_kernel, out_shape=[half, half], in_specs=[SM, VM], o...  3 us
  transfers between devices with their start and end apart: 13, of which 4 were waited for; matrix products, arithmetic and copies ran while one was open for 1% of the time, Pallas kernels for 14%

profile of v3, /device:TPU:1, one launch (start us, length us, event | category | flops | bytes accessed | tf_op | source)
XLA Modules:
  0.0 85.7 jit_solution(5003245187372941541)
XLA Ops:
  0.0 1.6 %share.1 = f32[32,32,128]{2,1,0:T(8,128)} custom-call(s32[1]{0:T(128)} %bitcast.me_ref, f32[16,2048]{1,0:T(8,128)} %aterms.1), custom_call_target="tpu_custom_call" | custom-call | tf_op jit(solution)/shard_map/share/pallas_call | solution.py:348
  1.7 12.0 %all-to-all-start = ((f32[32,1,4096]{2,1,0:T(1,128)}), f32[32,1,4096]{2,1,0:T(1,128)S(1)}, u32[]{:S(2)}, u32[]{:S(2)}) async-start(f32[32,1,4096]{2,1,0:T(1,128)} %bitcast.19), calls=%async_computation | async-start | bytes 1048576 | tf_op jit(solution)/shard_map/all_to_all | solution.py:358
  13.7 0.1 select_reduce_fusion.1
  13.8 0.2 convert_reduce_fusion
  14.0 0.1 select_reduce_fusion
  14.1 0.6 copy-done.8
  14.7 0.1 concatenate.3.ints
  14.7 0.6 copy-done.7
  15.3 0.7 pack.1
  16.0 1.4 %collective-permute-start.1 = (f32[2,17,8,128]{3,2,1,0:T(8,128)S(1)}, f32[2,17,8,128]{3,2,1,0:T(8,128)S(1)}, u32[]{:S(2)}, u32[]{:S(2)}) collective-permute-start(f32[2,17,8,128]{3,2,1,0:T(8,128)S(1)} %get-tuple-element.33), channel_id=1, source_target_pairs={{0,2},{1,3},{2,4},{3,5},{4,6},{5,7},{6,0},{7,1},{8,10},{9,11},{10,... | collective-permute-start | bytes 417800 | tf_op jit(solution)/shard_map/ppermute | solution.py:341
  17.4 2.6 %collective-permute-start.2 = (f32[2,17,8,128]{3,2,1,0:T(8,128)S(1)}, f32[2,17,8,128]{3,2,1,0:T(8,128)S(1)}, u32[]{:S(2)}, u32[]{:S(2)}) collective-permute-start(f32[2,17,8,128]{3,2,1,0:T(8,128)S(1)} %get-tuple-element.34), channel_id=1, source_target_pairs={{0,4},{1,5},{2,6},{3,7},{4,0},{5,1},{6,2},{7,3},{8,12},{9,13},{10,... | collective-permute-start | bytes 417800 | tf_op jit(solution)/shard_map/ppermute | solution.py:341
  20.0 1.1 %collective-permute-start.3 = (f32[2,17,8,128]{3,2,1,0:T(8,128)S(1)}, f32[2,17,8,128]{3,2,1,0:T(8,128)S(1)}, u32[]{:S(2)}, u32[]{:S(2)}) collective-permute-start(f32[2,17,8,128]{3,2,1,0:T(8,128)S(1)} %get-tuple-element.35), channel_id=1, source_target_pairs={{0,6},{1,7},{2,0},{3,1},{4,2},{5,3},{6,4},{7,5},{8,14},{9,15},{10,... | collective-permute-start | bytes 417800 | tf_op jit(solution)/shard_map/ppermute | solution.py:341
  21.0 1.8 %collective-permute-start = (f32[17,8,128]{2,1,0:T(8,128)S(1)}, f32[17,8,128]{2,1,0:T(8,128)S(1)}, u32[]{:S(2)}, u32[]{:S(2)}) collective-permute-start(f32[17,8,128]{2,1,0:T(8,128)S(1)} %get-tuple-element.32), channel_id=1, source_target_pairs={{0,1},{1,0},{2,3},{3,2},{4,5},{5,4},{6,7},{7,6},{8,9},{9,8},{10,11... | collective-permute-start | bytes 208904 | tf_op jit(solution)/shard_map/ppermute | solution.py:341
  22.8 0.9 %collective-permute-done.refs_1_ = f32[17,8,128]{2,1,0:T(8,128)S(1)} collective-permute-done((f32[17,8,128]{2,1,0:T(8,128)S(1)}, f32[17,8,128]{2,1,0:T(8,128)S(1)}, u32[]{:S(2)}, u32[]{:S(2)}) %collective-permute-start) | collective-permute-done | bytes 69664 | tf_op jit(solution)/shard_map/ppermute | solution.py:341
  23.7 2.6 %shard_map.127.refs_2_ = f32[8,64,128]{2,1,0:T(8,128)S(1)} custom-call(f32[2,8,128]{2,1,0:T(8,128)S(1)} %get-tuple-element.30.uv, f32[17,8,128]{2,1,0:T(8,128)S(1)} %get-tuple-element.31.refs_0_, f32[17,8,128]{2,1,0:T(8,128)S(1)} %collective-permute-done.refs_1_), custom_call_target="tpu_custom_call" | custom-call | flops 400000000 | bytes 200000 | tf_op jit(solution)/shard_map/pallas_call | solution.py:193
  26.3 1.2 %collective-permute-start.4 = (f32[2,17,8,128]{3,2,1,0:T(8,128)S(1)}, f32[2,17,8,128]{3,2,1,0:T(8,128)S(1)}, u32[]{:S(2)}, u32[]{:S(2)}) collective-permute-start(f32[2,17,8,128]{3,2,1,0:T(8,128)S(1)} %collective-permute-done.1.refs_0_), channel_id=1, source_target_pairs={{0,1},{1,0},{2,3},{3,2},{4,5},{5,4},{6,7},{7,6},{8,9},{9,8},{10,11... | collective-permute-start | bytes 417800 | tf_op jit(solution)/shard_map/ppermute | solution.py:341
  27.6 0.5 collective-permute-start.6
  28.1 2.6 %shard_map.128.refs_4_ = f32[8,64,128]{2,1,0:T(8,128)S(1)} custom-call(f32[2,8,128]{2,1,0:T(8,128)S(1)} %get-tuple-element.30.uv, f32[2,17,8,128]{3,2,1,0:T(8,128)S(1)} %collective-permute-done.1.refs_0_, f32[2,17,8,128]{3,2,1,0:T(8,128)S(1)} %collective-permute-done.3.refs_1_, f32[8,64,128]{2,1,0:T(8,128)S(1)} %shard_map.127.refs_2_), custom_call_target="tpu_custom_call" | custom-call | flops 400000000 | bytes 200000 | tf_op jit(solution)/shard_map/pallas_call | solution.py:193
  30.7 1.4 %pair.1 = f32[8,16,128]{2,1,0:T(8,128)} custom-call(s32[385]{0:T(512)S(1)} %concatenate.3.ints, f32[1024,128]{1,0:T(8,128)S(1)} %bitcast.17, f32[8,128]{1,0:T(8,128)S(1)} %copy-done.6), custom_call_target="tpu_custom_call" | custom-call | tf_op jit(solution)/shard_map/pair/pallas_call | solution.py:394
  32.2 6.1 %all-to-all-start.1 = ((f32[8,1,2048]{2,1,0:T(1,128)}), f32[8,1,2048]{2,1,0:T(1,128)S(1)}, u32[]{:S(2)}, u32[]{:S(2)}) async-start(f32[8,1,2048]{2,1,0:T(1,128)} %bitcast.7), calls=%async_computation.1 | async-start | bytes 131072 | tf_op jit(solution)/shard_map/all_to_all | solution.py:403
  38.3 4.8 %shard_map.129.acc = f32[8,64,128]{2,1,0:T(8,128)S(1)} custom-call(f32[2,8,128]{2,1,0:T(8,128)S(1)} %get-tuple-element.30.uv, f32[2,17,8,128]{3,2,1,0:T(8,128)S(1)} %collective-permute-done.4.refs_0_, f32[2,17,8,128]{3,2,1,0:T(8,128)S(1)} %collective-permute-done.5.refs_1_, f32[2,17,8,128]{3,2,1,0:T(8,128)S(1)} %collective-permute-done.2.refs_2_, ...), custom_call_target="tpu_custom_call" | custom-call | flops 800000000 | bytes 400000 | tf_op jit(solution)/shard_map/pallas_call | solution.py:193
  43.2 1.3 %finish.1 = f32[1056,128]{1,0:T(8,128)S(1)} custom-call(s32[385]{0:T(512)S(1)} %concatenate.3.ints, f32[8,64,128]{2,1,0:T(8,128)S(1)} %shard_map.129.acc, f32[8,16,128]{2,1,0:T(8,128)S(1)} %bitcast.18, bf16[256,128]{1,0:T(8,128)(2,1)S(1)} %copy-done.3, bf16[2,128,128]{2,1,0:T(8,128)(2,1)S(1)} %copy-done.2, bf16[32,192]{1,0:T(8,128)(2,1)S(1)} %copy-done.5, ...), custom_call_target="tpu_custom_call" | custom-call | tf_op jit(solution)/shard_map/finish/pallas_call | solution.py:405
  44.5 23.4 %all_to_all.27 = f32[32,1,4224]{2,1,0:T(1,128)S(1)} all-to-all(f32[32,1,4224]{2,1,0:T(1,128)S(1)} %bitcast.15), channel_id=1, replica_groups=mesh['bl'=32,'ch'=8] {'bl'}, dimensions={0} | all-to-all | bytes 1081344 | tf_op jit(solution)/shard_map/all_to_all | solution.py:413
  67.9 3.0 %place.1 = (f32[4,8,32,128]{3,2,1,0:T(8,128)S(1)}, f32[4,8,32,128]{3,2,1,0:T(8,128)S(1)}) custom-call(s32[1]{0:T(128)} %bitcast.me_ref, f32[1056,128]{1,0:T(8,128)S(1)} %bitcast.16), custom_call_target="tpu_custom_call" | custom-call | tf_op jit(solution)/shard_map/place/pallas_call | solution.py:416
  70.9 2.5 %collective-permute-start.7 = (f32[4,8,32,128]{3,2,1,0:T(8,128)S(1)}, f32[4,8,32,128]{3,2,1,0:T(8,128)S(1)}, u32[]{:S(2)}, u32[]{:S(2)}) collective-permute-start(f32[4,8,32,128]{3,2,1,0:T(8,128)S(1)} %get-tuple-element.46), channel_id=1, source_target_pairs={{0,1},{1,0},{2,3},{3,2},{4,5},{5,4},{6,7},{7,6},{8,9},{9,8},{10,11... | collective-permute-start | bytes 1572872 | tf_op jit(solution)/shard_map/ppermute | solution.py:341
  73.4 1.5 %collective-permute-done.7.got = f32[4,8,32,128]{3,2,1,0:T(8,128)S(1)} collective-permute-done((f32[4,8,32,128]{3,2,1,0:T(8,128)S(1)}, f32[4,8,32,128]{3,2,1,0:T(8,128)S(1)}, u32[]{:S(2)}, u32[]{:S(2)}) %collective-permute-start.7) | collective-permute-done | bytes 524320 | tf_op jit(solution)/shard_map/ppermute | solution.py:341
  75.0 1.5 %collective-permute-start.8 = (f32[8,32,128]{2,1,0:T(8,128)S(1)}, f32[8,32,128]{2,1,0:T(8,128)S(1)}, u32[]{:S(2)}, u32[]{:S(2)}) collective-permute-start(f32[8,32,128]{2,1,0:T(8,128)S(1)} %get-tuple-element.48), channel_id=1, source_target_pairs={{0,2},{1,3},{2,4},{3,5},{4,6},{5,7},{6,0},{7,1},{8,10},{9,11},{10,... | collective-permute-start | bytes 393224 | tf_op jit(solution)/shard_map/ppermute | solution.py:341
  76.5 2.4 %collective-permute-start.9 = (f32[8,32,128]{2,1,0:T(8,128)S(1)}, f32[8,32,128]{2,1,0:T(8,128)S(1)}, u32[]{:S(2)}, u32[]{:S(2)}) collective-permute-start(f32[8,32,128]{2,1,0:T(8,128)S(1)} %get-tuple-element.49), channel_id=1, source_target_pairs={{0,4},{1,5},{2,6},{3,7},{4,0},{5,1},{6,2},{7,3},{8,12},{9,13},{10,... | collective-permute-start | bytes 393224 | tf_op jit(solution)/shard_map/ppermute | solution.py:341
  78.9 1.2 %collective-permute-start.10 = (f32[8,32,128]{2,1,0:T(8,128)S(1)}, f32[8,32,128]{2,1,0:T(8,128)S(1)}, u32[]{:S(2)}, u32[]{:S(2)}) collective-permute-start(f32[8,32,128]{2,1,0:T(8,128)S(1)} %get-tuple-element.50), channel_id=1, source_target_pairs={{0,6},{1,7},{2,0},{3,1},{4,2},{5,3},{6,4},{7,5},{8,14},{9,15},{10,... | collective-permute-start | bytes 393224 | tf_op jit(solution)/shard_map/ppermute | solution.py:341
  80.1 0.9 %collective-permute-done.8.b = f32[8,32,128]{2,1,0:T(8,128)S(1)} collective-permute-done((f32[8,32,128]{2,1,0:T(8,128)S(1)}, f32[8,32,128]{2,1,0:T(8,128)S(1)}, u32[]{:S(2)}, u32[]{:S(2)}) %collective-permute-start.8) | collective-permute-done | bytes 131104 | tf_op jit(solution)/shard_map/ppermute | solution.py:341
  80.9 4.0 %collective-permute-done.9.c = f32[8,32,128]{2,1,0:T(8,128)S(1)} collective-permute-done((f32[8,32,128]{2,1,0:T(8,128)S(1)}, f32[8,32,128]{2,1,0:T(8,128)S(1)}, u32[]{:S(2)}, u32[]{:S(2)}) %collective-permute-start.9) | collective-permute-done | bytes 131104 | tf_op jit(solution)/shard_map/ppermute | solution.py:341
  84.9 0.7 last.1
  (35 shorter events, 0.2 us)
Async XLA Ops:
  1.6 12.1 %copy-start.10 = (s32[64]{0:T(128)S(1)}, s32[64]{0:T(128)}, u32[]{:S(2)}) copy-start(s32[64]{0:T(128)} %param.18) | copy-start | bytes 772
  1.6 12.1 %copy-start.11 = (s32[32]{0:T(128)S(1)}, s32[32]{0:T(128)}, u32[]{:S(2)}) copy-start(s32[32]{0:T(128)} %param.20) | copy-start | bytes 388
  1.6 12.5 %copy-start.9 = (s32[64,2]{0,1:T(2,128)S(1)}, s32[64,2]{0,1:T(2,128)}, u32[]{:S(2)}) copy-start(s32[64,2]{0,1:T(2,128)} %param.17) | copy-start | bytes 1540
  1.6 13.1 %copy-start = (f32[2,64,8,128]{3,2,1,0:T(8,128)S(1)}, f32[2,64,8,128]{3,2,1,0:T(8,128)}, u32[]{:S(2)}) copy-start(f32[2,64,8,128]{3,2,1,0:T(8,128)} %vis.1) | copy-start | bytes 1572868
  1.7 13.1 %copy-start.4 = (f32[2,64,128]{2,1,0:T(8,128)S(1)}, f32[2,64,128]{2,1,0:T(8,128)}, u32[]{:S(2)}) copy-start(f32[2,64,128]{2,1,0:T(8,128)} %coord.1) | copy-start | bytes 196612
  1.7 29.0 %all-to-all-start = ((f32[32,1,4096]{2,1,0:T(1,128)}), f32[32,1,4096]{2,1,0:T(1,128)S(1)}, u32[]{:S(2)}, u32[]{:S(2)}) async-start(f32[32,1,4096]{2,1,0:T(1,128)} %bitcast.19), calls=%async_computation | async-start | bytes 1048576 | tf_op jit(solution)/shard_map/all_to_all | solution.py:358
  14.0 0.7 copy-start.8
  14.7 0.7 copy-start.7
  16.0 10.3 %collective-permute-start.1 = (f32[2,17,8,128]{3,2,1,0:T(8,128)S(1)}, f32[2,17,8,128]{3,2,1,0:T(8,128)S(1)}, u32[]{:S(2)}, u32[]{:S(2)}) collective-permute-start(f32[2,17,8,128]{3,2,1,0:T(8,128)S(1)} %get-tuple-element.33), channel_id=1, source_target_pairs={{0,2},{1,3},{2,4},{3,5},{4,6},{5,7},{6,0},{7,1},{8,10},{9,11},{10,... | collective-permute-start | bytes 417800 | tf_op jit(solution)/shard_map/ppermute | solution.py:341
  17.4 9.0 %collective-permute-start.2 = (f32[2,17,8,128]{3,2,1,0:T(8,128)S(1)}, f32[2,17,8,128]{3,2,1,0:T(8,128)S(1)}, u32[]{:S(2)}, u32[]{:S(2)}) collective-permute-start(f32[2,17,8,128]{3,2,1,0:T(8,128)S(1)} %get-tuple-element.34), channel_id=1, source_target_pairs={{0,4},{1,5},{2,6},{3,7},{4,0},{5,1},{6,2},{7,3},{8,12},{9,13},{10,... | collective-permute-start | bytes 417800 | tf_op jit(solution)/shard_map/ppermute | solution.py:341
  20.0 6.4 %collective-permute-start.3 = (f32[2,17,8,128]{3,2,1,0:T(8,128)S(1)}, f32[2,17,8,128]{3,2,1,0:T(8,128)S(1)}, u32[]{:S(2)}, u32[]{:S(2)}) collective-permute-start(f32[2,17,8,128]{3,2,1,0:T(8,128)S(1)} %get-tuple-element.35), channel_id=1, source_target_pairs={{0,6},{1,7},{2,0},{3,1},{4,2},{5,3},{6,4},{7,5},{8,14},{9,15},{10,... | collective-permute-start | bytes 417800 | tf_op jit(solution)/shard_map/ppermute | solution.py:341
  21.0 2.7 %collective-permute-start = (f32[17,8,128]{2,1,0:T(8,128)S(1)}, f32[17,8,128]{2,1,0:T(8,128)S(1)}, u32[]{:S(2)}, u32[]{:S(2)}) collective-permute-start(f32[17,8,128]{2,1,0:T(8,128)S(1)} %get-tuple-element.32), channel_id=1, source_target_pairs={{0,1},{1,0},{2,3},{3,2},{4,5},{5,4},{6,7},{7,6},{8,9},{9,8},{10,11... | collective-permute-start | bytes 208904 | tf_op jit(solution)/shard_map/ppermute | solution.py:341
  26.3 12.0 %collective-permute-start.4 = (f32[2,17,8,128]{3,2,1,0:T(8,128)S(1)}, f32[2,17,8,128]{3,2,1,0:T(8,128)S(1)}, u32[]{:S(2)}, u32[]{:S(2)}) collective-permute-start(f32[2,17,8,128]{3,2,1,0:T(8,128)S(1)} %collective-permute-done.1.refs_0_), channel_id=1, source_target_pairs={{0,1},{1,0},{2,3},{3,2},{4,5},{5,4},{6,7},{7,6},{8,9},{9,8},{10,11... | collective-permute-start | bytes 417800 | tf_op jit(solution)/shard_map/ppermute | solution.py:341
  27.6 10.7 %collective-permute-start.5 = (f32[2,17,8,128]{3,2,1,0:T(8,128)S(1)}, f32[2,17,8,128]{3,2,1,0:T(8,128)S(1)}, u32[]{:S(2)}, u32[]{:S(2)}) collective-permute-start(f32[2,17,8,128]{3,2,1,0:T(8,128)S(1)} %collective-permute-done.3.refs_1_), channel_id=1, source_target_pairs={{0,1},{1,0},{2,3},{3,2},{4,5},{5,4},{6,7},{7,6},{8,9},{9,8},{10,11... | collective-permute-start | bytes 417800 | tf_op jit(solution)/shard_map/ppermute | solution.py:341
  27.6 10.8 %collective-permute-start.6 = (f32[2,17,8,128]{3,2,1,0:T(8,128)S(1)}, f32[2,17,8,128]{3,2,1,0:T(8,128)S(1)}, u32[]{:S(2)}, u32[]{:S(2)}) collective-permute-start(f32[2,17,8,128]{3,2,1,0:T(8,128)S(1)} %collective-permute-done.2.refs_2_), channel_id=1, source_target_pairs={{0,1},{1,0},{2,3},{3,2},{4,5},{5,4},{6,7},{7,6},{8,9},{9,8},{10,11... | collective-permute-start | bytes 417800 | tf_op jit(solution)/shard_map/ppermute | solution.py:341
  28.1 2.6 %copy-start.6 = (f32[8,128]{1,0:T(8,128)S(1)}, f32[8,128]{1,0:T(8,128)}, u32[]{:S(2)}) copy-start(f32[8,128]{1,0:T(8,128)} %constant.18.clone.taper) | copy-start | bytes 12292
  32.2 11.0 %all-to-all-start.1 = ((f32[8,1,2048]{2,1,0:T(1,128)}), f32[8,1,2048]{2,1,0:T(1,128)S(1)}, u32[]{:S(2)}, u32[]{:S(2)}) async-start(f32[8,1,2048]{2,1,0:T(1,128)} %bitcast.7), calls=%async_computation.1 | async-start | bytes 131072 | tf_op jit(solution)/shard_map/all_to_all | solution.py:403
  38.3 4.9 %copy-start.1 = (bf16[384,128]{1,0:T(8,128)(2,1)S(1)}, bf16[384,128]{1,0:T(8,128)(2,1)}, u32[]{:S(2)}) copy-start(bf16[384,128]{1,0:T(8,128)(2,1)} %constant.22.clone.right3) | copy-start | bytes 294916
  38.3 4.9 %copy-start.2 = (bf16[2,128,128]{2,1,0:T(8,128)(2,1)S(1)}, bf16[2,128,128]{2,1,0:T(8,128)(2,1)}, u32[]{:S(2)}) copy-start(bf16[2,128,128]{2,1,0:T(8,128)(2,1)} %constant.20.clone.fold) | copy-start | bytes 196612
  38.3 4.9 %copy-start.3 = (bf16[256,128]{1,0:T(8,128)(2,1)S(1)}, bf16[256,128]{1,0:T(8,128)(2,1)}, u32[]{:S(2)}) copy-start(bf16[256,128]{1,0:T(8,128)(2,1)} %constant.19.clone.to_image) | copy-start | bytes 196612
  38.3 4.9 %copy-start.5 = (bf16[32,192]{1,0:T(8,128)(2,1)S(1)}, bf16[32,192]{1,0:T(8,128)(2,1)}, u32[]{:S(2)}) copy-start(bf16[32,192]{1,0:T(8,128)(2,1)} %constant.21.clone.left3) | copy-start | bytes 36868
  70.9 4.0 %collective-permute-start.7 = (f32[4,8,32,128]{3,2,1,0:T(8,128)S(1)}, f32[4,8,32,128]{3,2,1,0:T(8,128)S(1)}, u32[]{:S(2)}, u32[]{:S(2)}) collective-permute-start(f32[4,8,32,128]{3,2,1,0:T(8,128)S(1)} %get-tuple-element.46), channel_id=1, source_target_pairs={{0,1},{1,0},{2,3},{3,2},{4,5},{5,4},{6,7},{7,6},{8,9},{9,8},{10,11... | collective-permute-start | bytes 1572872 | tf_op jit(solution)/shard_map/ppermute | solution.py:341
  75.0 6.0 %collective-permute-start.8 = (f32[8,32,128]{2,1,0:T(8,128)S(1)}, f32[8,32,128]{2,1,0:T(8,128)S(1)}, u32[]{:S(2)}, u32[]{:S(2)}) collective-permute-start(f32[8,32,128]{2,1,0:T(8,128)S(1)} %get-tuple-element.48), channel_id=1, source_target_pairs={{0,2},{1,3},{2,4},{3,5},{4,6},{5,7},{6,0},{7,1},{8,10},{9,11},{10,... | collective-permute-start | bytes 393224 | tf_op jit(solution)/shard_map/ppermute | solution.py:341
  76.5 8.4 %collective-permute-start.9 = (f32[8,32,128]{2,1,0:T(8,128)S(1)}, f32[8,32,128]{2,1,0:T(8,128)S(1)}, u32[]{:S(2)}, u32[]{:S(2)}) collective-permute-start(f32[8,32,128]{2,1,0:T(8,128)S(1)} %get-tuple-element.49), channel_id=1, source_target_pairs={{0,4},{1,5},{2,6},{3,7},{4,0},{5,1},{6,2},{7,3},{8,12},{9,13},{10,... | collective-permute-start | bytes 393224 | tf_op jit(solution)/shard_map/ppermute | solution.py:341
  78.9 6.0 %collective-permute-start.10 = (f32[8,32,128]{2,1,0:T(8,128)S(1)}, f32[8,32,128]{2,1,0:T(8,128)S(1)}, u32[]{:S(2)}, u32[]{:S(2)}) collective-permute-start(f32[8,32,128]{2,1,0:T(8,128)S(1)} %get-tuple-element.50), channel_id=1, source_target_pairs={{0,6},{1,7},{2,0},{3,1},{4,2},{5,3},{6,4},{7,5},{8,14},{9,15},{10,... | collective-permute-start | bytes 393224 | tf_op jit(solution)/shard_map/ppermute | solution.py:341

commit v4 on v3

--- a/solution.py
+++ b/solution.py
@@ -307,13 +307,10 @@
             at = (2 * m + half, pl.ds(r, 32), slice(None))
             acc[at] = acc[at] + jnp.where(near, moved[m], 0.0)
 
-        @pl.when(c > 96)
-        def _():
-            far = lane < c - 96
-            for m in range(4):
-                at = (2 * m + 1, pl.ds(r, 32), slice(None))
-                acc[at] = acc[at] + jnp.where(far, moved[m], 0.0)
-
+        far = lane < c - 96
+        for m in range(4):
+            at = (2 * m + 1, pl.ds(r, 32), slice(None))
+            acc[at] = acc[at] + jnp.where(far, moved[m], 0.0)
         return unused
 
     lax.fori_loop(0, 32, one, 0, unroll=4)
@@ -387,9 +384,11 @@
     near = shift(near, 0, 1)
     direct = [shift(far[d - 1], d, 0) for d in range(1, 4)]
     acc = images(uv, [(mine, None), (near, None)])
-    acc, *direct = lax.optimization_barrier((acc, *direct))
-    swapped = [shift(x, 0, 1) for x in direct]
-    acc = images(uv, [(direct[0], 0), (direct[2], 0)], acc)
+    acc, one, three = lax.optimization_barrier((acc, direct[0], direct[2]))
+    swap_one, swap_three = shift(one, 0, 1), shift(three, 0, 1)
+    acc = images(uv, [(one, 0), (three, 0)], acc)
+    acc, two = lax.optimization_barrier((acc, direct[1]))
+    swap_two = shift(two, 0, 1)
     acc, table = lax.optimization_barrier((acc, table))
     pair = pl.pallas_call(
         pair_kernel,
@@ -401,7 +400,7 @@
     )(ints, table, taper)
     acc, pair = lax.optimization_barrier((acc, pair))
     pair = lax.all_to_all(pair.reshape(8, 2048), "ch", 0, 0, tiled=True).reshape(8, 16, 128)
-    acc = images(uv, [(swapped[0], 1), (swapped[2], 1), (direct[1], 0), (swapped[1], 1)], acc)
+    acc = images(uv, [(swap_one, 1), (swap_three, 1), (two, 0), (swap_two, 1)], acc)
     outgoing = pl.pallas_call(
         finish_kernel,
         out_shape=jax.ShapeDtypeStruct((33 * 32, 128), F32),

time: 86.1 us -> 81.9 us (0.951)
  blocking collectives: 23.4 us -> 20.9 us
  Pallas kernels: 18.7 us -> 17.1 us
  starting transfers between devices: 34.3 us -> 33.4 us
  waiting for transfers between devices: 7.35 us -> 8.23 us
    all_to_all x1, blocking collectives: 23.4 us -> 20.9 us  [local(): lax.all_to_all(outgoing.reshape(32, 33 * 128), 'bl', 0, 0, tiled=True)]
    all_to_all x1, waiting for transfers between devices: 0.01 us -> 1.83 us  [local(): table = lax.all_to_all(shared.reshape(32, 4096), 'bl', 0, 0, tiled=True)]
    ppermute x11, starting transfers between devices: 16.2 us -> 14.6 us  [shift(): return lax.ppermute(x, 'ch', pairs)]
    pallas_call x1, Pallas kernels: 3 us -> 1.41 us  [local(): pl.pallas_call(place_kernel, out_shape=[half, half], in_specs=[SM, VM], o...]
    ppermute x11, waiting for transfers between devices: 7.32 us -> 6.38 us  [shift(): return lax.ppermute(x, 'ch', pairs)]
  transfers between devices with their start and end apart: 13 -> 13, of which waited for: 4 -> 4; matrix products, arithmetic and copies ran while one was open for 1% -> 1% of each run, Pallas kernels for 14% -> 15%
where the time goes in v4:
time: 81.9 us; the launch traced here: 81.5 us
  starting transfers between devices  33.4 us (41%)
  blocking collectives  20.9 us (26%)
  Pallas kernels  17.1 us (21%)
  waiting for transfers between devices  8.23 us (10%)
  local copies, waits for them, and re-layouts  1.27 us (2%)
    all_to_all x1, blocking collectives, local(): lax.all_to_all(outgoing.reshape(32, 33 * 128), 'bl', 0, 0, tiled=True)  20.9 us
    ppermute x11, starting transfers between devices, shift(): return lax.ppermute(x, 'ch', pairs)  14.6 us
    all_to_all x1, starting transfers between devices, local(): table = lax.all_to_all(shared.reshape(32, 4096), 'bl', 0, 0, tiled=True)  12 us
    pallas_call x3, Pallas kernels, images(): pl.pallas_call(functools.partial(image_kernel, picks, first), out_shape=j...  9.91 us
    all_to_all x1, starting transfers between devices, local(): lax.all_to_all(pair.reshape(8, 2048), 'ch', 0, 0, tiled=True)  6.9 us
    ppermute x11, waiting for transfers between devices, shift(): return lax.ppermute(x, 'ch', pairs)  6.38 us
    all_to_all x1, waiting for transfers between devices, local(): table = lax.all_to_all(shared.reshape(32, 4096), 'bl', 0, 0, tiled=True)  1.83 us
  transfers between devices with their start and end apart: 13, of which 4 were waited for; matrix products, arithmetic and copies ran while one was open for 1% of the time, Pallas kernels for 15%

profile of v4, /device:TPU:1, one launch (start us, length us, event | category | flops | bytes accessed | tf_op | source)
XLA Modules:
  0.0 81.5 jit_solution(14748185687218255129)
XLA Ops:
  0.0 1.6 %share.1 = f32[32,32,128]{2,1,0:T(8,128)} custom-call(s32[1]{0:T(128)} %bitcast.me_ref, f32[16,2048]{1,0:T(8,128)} %aterms.1), custom_call_target="tpu_custom_call" | custom-call | tf_op jit(solution)/shard_map/share/pallas_call | solution.py:345
  1.7 12.0 %all-to-all-start = ((f32[32,1,4096]{2,1,0:T(1,128)}), f32[32,1,4096]{2,1,0:T(1,128)S(1)}, u32[]{:S(2)}, u32[]{:S(2)}) async-start(f32[32,1,4096]{2,1,0:T(1,128)} %bitcast.19), calls=%async_computation | async-start | bytes 1048576 | tf_op jit(solution)/shard_map/all_to_all | solution.py:355
  13.7 0.1 select_reduce_fusion.1
  13.8 0.2 convert_reduce_fusion
  14.0 0.1 select_reduce_fusion
  14.1 0.6 copy-done.8
  14.7 0.6 copy-done.7
  15.3 0.7 pack.1
  16.0 1.4 %collective-permute-start.1 = (f32[2,17,8,128]{3,2,1,0:T(8,128)S(1)}, f32[2,17,8,128]{3,2,1,0:T(8,128)S(1)}, u32[]{:S(2)}, u32[]{:S(2)}) collective-permute-start(f32[2,17,8,128]{3,2,1,0:T(8,128)S(1)} %get-tuple-element.34), channel_id=1, source_target_pairs={{0,2},{1,3},{2,4},{3,5},{4,6},{5,7},{6,0},{7,1},{8,10},{9,11},{10,... | collective-permute-start | bytes 417800 | tf_op jit(solution)/shard_map/ppermute | solution.py:338
  17.4 1.5 %collective-permute-start.2 = (f32[2,17,8,128]{3,2,1,0:T(8,128)S(1)}, f32[2,17,8,128]{3,2,1,0:T(8,128)S(1)}, u32[]{:S(2)}, u32[]{:S(2)}) collective-permute-start(f32[2,17,8,128]{3,2,1,0:T(8,128)S(1)} %get-tuple-element.35), channel_id=1, source_target_pairs={{0,6},{1,7},{2,0},{3,1},{4,2},{5,3},{6,4},{7,5},{8,14},{9,15},{10,... | collective-permute-start | bytes 417800 | tf_op jit(solution)/shard_map/ppermute | solution.py:338
  18.9 1.4 %collective-permute-start = (f32[17,8,128]{2,1,0:T(8,128)S(1)}, f32[17,8,128]{2,1,0:T(8,128)S(1)}, u32[]{:S(2)}, u32[]{:S(2)}) collective-permute-start(f32[17,8,128]{2,1,0:T(8,128)S(1)} %get-tuple-element.33), channel_id=1, source_target_pairs={{0,1},{1,0},{2,3},{3,2},{4,5},{5,4},{6,7},{7,6},{8,9},{9,8},{10,11... | collective-permute-start | bytes 208904 | tf_op jit(solution)/shard_map/ppermute | solution.py:338
  20.2 1.7 %collective-permute-start.5 = (f32[2,17,8,128]{3,2,1,0:T(8,128)S(1)}, f32[2,17,8,128]{3,2,1,0:T(8,128)S(1)}, u32[]{:S(2)}, u32[]{:S(2)}) collective-permute-start(f32[2,17,8,128]{3,2,1,0:T(8,128)S(1)} %get-tuple-element.39), channel_id=1, source_target_pairs={{0,4},{1,5},{2,6},{3,7},{4,0},{5,1},{6,2},{7,3},{8,12},{9,13},{10,... | collective-permute-start | bytes 417800 | tf_op jit(solution)/shard_map/ppermute | solution.py:338
  22.0 2.6 %shard_map.127.refs_2_ = f32[8,64,128]{2,1,0:T(8,128)S(1)} custom-call(f32[2,8,128]{2,1,0:T(8,128)S(1)} %get-tuple-element.31.uv, f32[17,8,128]{2,1,0:T(8,128)S(1)} %get-tuple-element.32.refs_0_, f32[17,8,128]{2,1,0:T(8,128)S(1)} %collective-permute-done.refs_1_), custom_call_target="tpu_custom_call" | custom-call | flops 400000000 | bytes 200000 | tf_op jit(solution)/shard_map/pallas_call | solution.py:193
  24.5 0.4 collective-permute-start.3
  24.9 0.2 collective-permute-start.4
  25.1 2.6 %shard_map.128.refs_4_ = f32[8,64,128]{2,1,0:T(8,128)S(1)} custom-call(f32[2,8,128]{2,1,0:T(8,128)S(1)} %get-tuple-element.31.uv, f32[2,17,8,128]{3,2,1,0:T(8,128)S(1)} %collective-permute-done.1.refs_0_, f32[2,17,8,128]{3,2,1,0:T(8,128)S(1)} %collective-permute-done.2.refs_1_, f32[8,64,128]{2,1,0:T(8,128)S(1)} %shard_map.127.refs_2_), custom_call_target="tpu_custom_call" | custom-call | flops 400000000 | bytes 200000 | tf_op jit(solution)/shard_map/pallas_call | solution.py:193
  27.8 0.4 collective-permute-start.6
  28.1 1.8 %all-to-all-done = f32[32,1,4096]{2,1,0:T(1,128)S(1)} async-done(((f32[32,1,4096]{2,1,0:T(1,128)}), f32[32,1,4096]{2,1,0:T(1,128)S(1)}, u32[]{:S(2)}, u32[]{:S(2)}) %all-to-all-start) | async-done | bytes 524320 | tf_op jit(solution)/shard_map/all_to_all | solution.py:355
  30.0 1.4 %pair.1 = f32[8,16,128]{2,1,0:T(8,128)} custom-call(s32[385]{0:T(512)S(1)} %concatenate.3.ints, f32[1024,128]{1,0:T(8,128)S(1)} %bitcast.17, f32[8,128]{1,0:T(8,128)S(1)} %copy-done.6), custom_call_target="tpu_custom_call" | custom-call | tf_op jit(solution)/shard_map/pair/pallas_call | solution.py:393
  31.4 6.9 %all-to-all-start.1 = ((f32[8,1,2048]{2,1,0:T(1,128)}), f32[8,1,2048]{2,1,0:T(1,128)S(1)}, u32[]{:S(2)}, u32[]{:S(2)}) async-start(f32[8,1,2048]{2,1,0:T(1,128)} %bitcast.7), calls=%async_computation.1 | async-start | bytes 131072 | tf_op jit(solution)/shard_map/all_to_all | solution.py:402
  38.3 4.8 %shard_map.129.acc = f32[8,64,128]{2,1,0:T(8,128)S(1)} custom-call(f32[2,8,128]{2,1,0:T(8,128)S(1)} %get-tuple-element.31.uv, f32[2,17,8,128]{3,2,1,0:T(8,128)S(1)} %collective-permute-done.3.refs_0_, f32[2,17,8,128]{3,2,1,0:T(8,128)S(1)} %collective-permute-done.4.refs_1_, f32[2,17,8,128]{3,2,1,0:T(8,128)S(1)} %collective-permute-done.5.refs_2_, ...), custom_call_target="tpu_custom_call" | custom-call | flops 800000000 | bytes 400000 | tf_op jit(solution)/shard_map/pallas_call | solution.py:193
  43.2 1.3 %finish.1 = f32[1056,128]{1,0:T(8,128)S(1)} custom-call(s32[385]{0:T(512)S(1)} %concatenate.3.ints, f32[8,64,128]{2,1,0:T(8,128)S(1)} %shard_map.129.acc, f32[8,16,128]{2,1,0:T(8,128)S(1)} %bitcast.18, bf16[256,128]{1,0:T(8,128)(2,1)S(1)} %copy-done.3, bf16[2,128,128]{2,1,0:T(8,128)(2,1)S(1)} %copy-done.2, bf16[32,192]{1,0:T(8,128)(2,1)S(1)} %copy-done.5, ...), custom_call_target="tpu_custom_call" | custom-call | tf_op jit(solution)/shard_map/finish/pallas_call | solution.py:404
  44.5 20.9 %all_to_all.27 = f32[32,1,4224]{2,1,0:T(1,128)S(1)} all-to-all(f32[32,1,4224]{2,1,0:T(1,128)S(1)} %bitcast.15), channel_id=1, replica_groups=mesh['bl'=32,'ch'=8] {'bl'}, dimensions={0} | all-to-all | bytes 1081344 | tf_op jit(solution)/shard_map/all_to_all | solution.py:412
  65.3 1.4 %place.1 = (f32[4,8,32,128]{3,2,1,0:T(8,128)S(1)}, f32[4,8,32,128]{3,2,1,0:T(8,128)S(1)}) custom-call(s32[1]{0:T(128)} %bitcast.me_ref, f32[1056,128]{1,0:T(8,128)S(1)} %bitcast.16), custom_call_target="tpu_custom_call" | custom-call | tf_op jit(solution)/shard_map/place/pallas_call | solution.py:415
  66.7 2.5 %collective-permute-start.7 = (f32[4,8,32,128]{3,2,1,0:T(8,128)S(1)}, f32[4,8,32,128]{3,2,1,0:T(8,128)S(1)}, u32[]{:S(2)}, u32[]{:S(2)}) collective-permute-start(f32[4,8,32,128]{3,2,1,0:T(8,128)S(1)} %get-tuple-element.48), channel_id=1, source_target_pairs={{0,1},{1,0},{2,3},{3,2},{4,5},{5,4},{6,7},{7,6},{8,9},{9,8},{10,11... | collective-permute-start | bytes 1572872 | tf_op jit(solution)/shard_map/ppermute | solution.py:338
  69.2 1.5 %collective-permute-done.7.got = f32[4,8,32,128]{3,2,1,0:T(8,128)S(1)} collective-permute-done((f32[4,8,32,128]{3,2,1,0:T(8,128)S(1)}, f32[4,8,32,128]{3,2,1,0:T(8,128)S(1)}, u32[]{:S(2)}, u32[]{:S(2)}) %collective-permute-start.7) | collective-permute-done | bytes 524320 | tf_op jit(solution)/shard_map/ppermute | solution.py:338
  70.8 1.5 %collective-permute-start.8 = (f32[8,32,128]{2,1,0:T(8,128)S(1)}, f32[8,32,128]{2,1,0:T(8,128)S(1)}, u32[]{:S(2)}, u32[]{:S(2)}) collective-permute-start(f32[8,32,128]{2,1,0:T(8,128)S(1)} %get-tuple-element.50), channel_id=1, source_target_pairs={{0,2},{1,3},{2,4},{3,5},{4,6},{5,7},{6,0},{7,1},{8,10},{9,11},{10,... | collective-permute-start | bytes 393224 | tf_op jit(solution)/shard_map/ppermute | solution.py:338
  72.4 2.4 %collective-permute-start.9 = (f32[8,32,128]{2,1,0:T(8,128)S(1)}, f32[8,32,128]{2,1,0:T(8,128)S(1)}, u32[]{:S(2)}, u32[]{:S(2)}) collective-permute-start(f32[8,32,128]{2,1,0:T(8,128)S(1)} %get-tuple-element.51), channel_id=1, source_target_pairs={{0,4},{1,5},{2,6},{3,7},{4,0},{5,1},{6,2},{7,3},{8,12},{9,13},{10,... | collective-permute-start | bytes 393224 | tf_op jit(solution)/shard_map/ppermute | solution.py:338
  74.7 1.2 %collective-permute-start.10 = (f32[8,32,128]{2,1,0:T(8,128)S(1)}, f32[8,32,128]{2,1,0:T(8,128)S(1)}, u32[]{:S(2)}, u32[]{:S(2)}) collective-permute-start(f32[8,32,128]{2,1,0:T(8,128)S(1)} %get-tuple-element.52), channel_id=1, source_target_pairs={{0,6},{1,7},{2,0},{3,1},{4,2},{5,3},{6,4},{7,5},{8,14},{9,15},{10,... | collective-permute-start | bytes 393224 | tf_op jit(solution)/shard_map/ppermute | solution.py:338
  76.0 0.9 %collective-permute-done.8.b = f32[8,32,128]{2,1,0:T(8,128)S(1)} collective-permute-done((f32[8,32,128]{2,1,0:T(8,128)S(1)}, f32[8,32,128]{2,1,0:T(8,128)S(1)}, u32[]{:S(2)}, u32[]{:S(2)}) %collective-permute-start.8) | collective-permute-done | bytes 131104 | tf_op jit(solution)/shard_map/ppermute | solution.py:338
  76.8 4.0 %collective-permute-done.9.c = f32[8,32,128]{2,1,0:T(8,128)S(1)} collective-permute-done((f32[8,32,128]{2,1,0:T(8,128)S(1)}, f32[8,32,128]{2,1,0:T(8,128)S(1)}, u32[]{:S(2)}, u32[]{:S(2)}) %collective-permute-start.9) | collective-permute-done | bytes 131104 | tf_op jit(solution)/shard_map/ppermute | solution.py:338
  80.8 0.7 last.1
  (35 shorter events, 0.3 us)
Async XLA Ops:
  1.6 12.1 %copy-start.10 = (s32[64]{0:T(128)S(1)}, s32[64]{0:T(128)}, u32[]{:S(2)}) copy-start(s32[64]{0:T(128)} %param.18) | copy-start | bytes 772
  1.6 12.1 %copy-start.11 = (s32[32]{0:T(128)S(1)}, s32[32]{0:T(128)}, u32[]{:S(2)}) copy-start(s32[32]{0:T(128)} %param.20) | copy-start | bytes 388
  1.6 12.5 %copy-start.9 = (s32[64,2]{0,1:T(2,128)S(1)}, s32[64,2]{0,1:T(2,128)}, u32[]{:S(2)}) copy-start(s32[64,2]{0,1:T(2,128)} %param.17) | copy-start | bytes 1540
  1.6 13.1 %copy-start = (f32[2,64,8,128]{3,2,1,0:T(8,128)S(1)}, f32[2,64,8,128]{3,2,1,0:T(8,128)}, u32[]{:S(2)}) copy-start(f32[2,64,8,128]{3,2,1,0:T(8,128)} %vis.1) | copy-start | bytes 1572868
  1.7 13.1 %copy-start.4 = (f32[2,64,128]{2,1,0:T(8,128)S(1)}, f32[2,64,128]{2,1,0:T(8,128)}, u32[]{:S(2)}) copy-start(f32[2,64,128]{2,1,0:T(8,128)} %coord.1) | copy-start | bytes 196612
  1.7 28.3 %all-to-all-start = ((f32[32,1,4096]{2,1,0:T(1,128)}), f32[32,1,4096]{2,1,0:T(1,128)S(1)}, u32[]{:S(2)}, u32[]{:S(2)}) async-start(f32[32,1,4096]{2,1,0:T(1,128)} %bitcast.19), calls=%async_computation | async-start | bytes 1048576 | tf_op jit(solution)/shard_map/all_to_all | solution.py:355
  14.0 0.7 copy-start.8
  14.7 0.7 copy-start.7
  16.0 8.5 %collective-permute-start.1 = (f32[2,17,8,128]{3,2,1,0:T(8,128)S(1)}, f32[2,17,8,128]{3,2,1,0:T(8,128)S(1)}, u32[]{:S(2)}, u32[]{:S(2)}) collective-permute-start(f32[2,17,8,128]{3,2,1,0:T(8,128)S(1)} %get-tuple-element.34), channel_id=1, source_target_pairs={{0,2},{1,3},{2,4},{3,5},{4,6},{5,7},{6,0},{7,1},{8,10},{9,11},{10,... | collective-permute-start | bytes 417800 | tf_op jit(solution)/shard_map/ppermute | solution.py:338
  17.4 7.2 %collective-permute-start.2 = (f32[2,17,8,128]{3,2,1,0:T(8,128)S(1)}, f32[2,17,8,128]{3,2,1,0:T(8,128)S(1)}, u32[]{:S(2)}, u32[]{:S(2)}) collective-permute-start(f32[2,17,8,128]{3,2,1,0:T(8,128)S(1)} %get-tuple-element.35), channel_id=1, source_target_pairs={{0,6},{1,7},{2,0},{3,1},{4,2},{5,3},{6,4},{7,5},{8,14},{9,15},{10,... | collective-permute-start | bytes 417800 | tf_op jit(solution)/shard_map/ppermute | solution.py:338
  18.9 3.1 %collective-permute-start = (f32[17,8,128]{2,1,0:T(8,128)S(1)}, f32[17,8,128]{2,1,0:T(8,128)S(1)}, u32[]{:S(2)}, u32[]{:S(2)}) collective-permute-start(f32[17,8,128]{2,1,0:T(8,128)S(1)} %get-tuple-element.33), channel_id=1, source_target_pairs={{0,1},{1,0},{2,3},{3,2},{4,5},{5,4},{6,7},{7,6},{8,9},{9,8},{10,11... | collective-permute-start | bytes 208904 | tf_op jit(solution)/shard_map/ppermute | solution.py:338
  20.2 7.5 %collective-permute-start.5 = (f32[2,17,8,128]{3,2,1,0:T(8,128)S(1)}, f32[2,17,8,128]{3,2,1,0:T(8,128)S(1)}, u32[]{:S(2)}, u32[]{:S(2)}) collective-permute-start(f32[2,17,8,128]{3,2,1,0:T(8,128)S(1)} %get-tuple-element.39), channel_id=1, source_target_pairs={{0,4},{1,5},{2,6},{3,7},{4,0},{5,1},{6,2},{7,3},{8,12},{9,13},{10,... | collective-permute-start | bytes 417800 | tf_op jit(solution)/shard_map/ppermute | solution.py:338
  24.5 13.8 %collective-permute-start.3 = (f32[2,17,8,128]{3,2,1,0:T(8,128)S(1)}, f32[2,17,8,128]{3,2,1,0:T(8,128)S(1)}, u32[]{:S(2)}, u32[]{:S(2)}) collective-permute-start(f32[2,17,8,128]{3,2,1,0:T(8,128)S(1)} %collective-permute-done.1.refs_0_), channel_id=1, source_target_pairs={{0,1},{1,0},{2,3},{3,2},{4,5},{5,4},{6,7},{7,6},{8,9},{9,8},{10,11... | collective-permute-start | bytes 417800 | tf_op jit(solution)/shard_map/ppermute | solution.py:338
  24.9 13.4 %collective-permute-start.4 = (f32[2,17,8,128]{3,2,1,0:T(8,128)S(1)}, f32[2,17,8,128]{3,2,1,0:T(8,128)S(1)}, u32[]{:S(2)}, u32[]{:S(2)}) collective-permute-start(f32[2,17,8,128]{3,2,1,0:T(8,128)S(1)} %collective-permute-done.2.refs_1_), channel_id=1, source_target_pairs={{0,1},{1,0},{2,3},{3,2},{4,5},{5,4},{6,7},{7,6},{8,9},{9,8},{10,11... | collective-permute-start | bytes 417800 | tf_op jit(solution)/shard_map/ppermute | solution.py:338
  25.1 4.8 %copy-start.6 = (f32[8,128]{1,0:T(8,128)S(1)}, f32[8,128]{1,0:T(8,128)}, u32[]{:S(2)}) copy-start(f32[8,128]{1,0:T(8,128)} %constant.18.clone.taper) | copy-start | bytes 12292
  27.8 10.6 %collective-permute-start.6 = (f32[2,17,8,128]{3,2,1,0:T(8,128)S(1)}, f32[2,17,8,128]{3,2,1,0:T(8,128)S(1)}, u32[]{:S(2)}, u32[]{:S(2)}) collective-permute-start(f32[2,17,8,128]{3,2,1,0:T(8,128)S(1)} %collective-permute-done.5.refs_2_), channel_id=1, source_target_pairs={{0,1},{1,0},{2,3},{3,2},{4,5},{5,4},{6,7},{7,6},{8,9},{9,8},{10,11... | collective-permute-start | bytes 417800 | tf_op jit(solution)/shard_map/ppermute | solution.py:338
  31.4 11.8 %all-to-all-start.1 = ((f32[8,1,2048]{2,1,0:T(1,128)}), f32[8,1,2048]{2,1,0:T(1,128)S(1)}, u32[]{:S(2)}, u32[]{:S(2)}) async-start(f32[8,1,2048]{2,1,0:T(1,128)} %bitcast.7), calls=%async_computation.1 | async-start | bytes 131072 | tf_op jit(solution)/shard_map/all_to_all | solution.py:402
  38.3 4.9 %copy-start.1 = (bf16[384,128]{1,0:T(8,128)(2,1)S(1)}, bf16[384,128]{1,0:T(8,128)(2,1)}, u32[]{:S(2)}) copy-start(bf16[384,128]{1,0:T(8,128)(2,1)} %constant.22.clone.right3) | copy-start | bytes 294916
  38.3 4.9 %copy-start.2 = (bf16[2,128,128]{2,1,0:T(8,128)(2,1)S(1)}, bf16[2,128,128]{2,1,0:T(8,128)(2,1)}, u32[]{:S(2)}) copy-start(bf16[2,128,128]{2,1,0:T(8,128)(2,1)} %constant.20.clone.fold) | copy-start | bytes 196612
  38.3 4.9 %copy-start.3 = (bf16[256,128]{1,0:T(8,128)(2,1)S(1)}, bf16[256,128]{1,0:T(8,128)(2,1)}, u32[]{:S(2)}) copy-start(bf16[256,128]{1,0:T(8,128)(2,1)} %constant.19.clone.to_image) | copy-start | bytes 196612
  38.3 4.9 %copy-start.5 = (bf16[32,192]{1,0:T(8,128)(2,1)S(1)}, bf16[32,192]{1,0:T(8,128)(2,1)}, u32[]{:S(2)}) copy-start(bf16[32,192]{1,0:T(8,128)(2,1)} %constant.21.clone.left3) | copy-start | bytes 36868
  66.7 4.0 %collective-permute-start.7 = (f32[4,8,32,128]{3,2,1,0:T(8,128)S(1)}, f32[4,8,32,128]{3,2,1,0:T(8,128)S(1)}, u32[]{:S(2)}, u32[]{:S(2)}) collective-permute-start(f32[4,8,32,128]{3,2,1,0:T(8,128)S(1)} %get-tuple-element.48), channel_id=1, source_target_pairs={{0,1},{1,0},{2,3},{3,2},{4,5},{5,4},{6,7},{7,6},{8,9},{9,8},{10,11... | collective-permute-start | bytes 1572872 | tf_op jit(solution)/shard_map/ppermute | solution.py:338
  70.8 6.0 %collective-permute-start.8 = (f32[8,32,128]{2,1,0:T(8,128)S(1)}, f32[8,32,128]{2,1,0:T(8,128)S(1)}, u32[]{:S(2)}, u32[]{:S(2)}) collective-permute-start(f32[8,32,128]{2,1,0:T(8,128)S(1)} %get-tuple-element.50), channel_id=1, source_target_pairs={{0,2},{1,3},{2,4},{3,5},{4,6},{5,7},{6,0},{7,1},{8,10},{9,11},{10,... | collective-permute-start | bytes 393224 | tf_op jit(solution)/shard_map/ppermute | solution.py:338
  72.4 8.4 %collective-permute-start.9 = (f32[8,32,128]{2,1,0:T(8,128)S(1)}, f32[8,32,128]{2,1,0:T(8,128)S(1)}, u32[]{:S(2)}, u32[]{:S(2)}) collective-permute-start(f32[8,32,128]{2,1,0:T(8,128)S(1)} %get-tuple-element.51), channel_id=1, source_target_pairs={{0,4},{1,5},{2,6},{3,7},{4,0},{5,1},{6,2},{7,3},{8,12},{9,13},{10,... | collective-permute-start | bytes 393224 | tf_op jit(solution)/shard_map/ppermute | solution.py:338
  74.7 6.0 %collective-permute-start.10 = (f32[8,32,128]{2,1,0:T(8,128)S(1)}, f32[8,32,128]{2,1,0:T(8,128)S(1)}, u32[]{:S(2)}, u32[]{:S(2)}) collective-permute-start(f32[8,32,128]{2,1,0:T(8,128)S(1)} %get-tuple-element.52), channel_id=1, source_target_pairs={{0,6},{1,7},{2,0},{3,1},{4,2},{5,3},{6,4},{7,5},{8,14},{9,15},{10,... | collective-permute-start | bytes 393224 | tf_op jit(solution)/shard_map/ppermute | solution.py:338

commit v5 on v4

--- a/solution.py
+++ b/solution.py
@@ -84,8 +84,8 @@
     )
 
 
-def share_kernel(me_ref, aterms, shared, strip, sems):
-    me = me_ref[0]
+def share_kernel(aterms, shared, strip, sems):
+    me = lax.axis_index("ch")
     copies = []
     for r in range(2):
         at = pl.multiple_of(1024 * r + me * 128, 128)
@@ -284,7 +284,8 @@
         out[pl.ds(at + 32, 1), :] = jnp.where(first_lane, ints[OFF0 + i], ints[OFF1 + i]).astype(F32)
 
 
-def place_kernel(me_ref, arrived, keep, give, acc, spots):
+def place_kernel(me_ref, arrived, keep, give_two, give, acc, spots):
+    gives = [give.at[0], give.at[1], give_two, give.at[2]]
     lane = lax.broadcasted_iota(jnp.int32, (32, 128), 1)
     me = me_ref[0]
     y = me >> 1
@@ -318,12 +319,16 @@
         block = ((y + d) & 3) << 1
         for k in range(8):
             keep[d, k] = acc[k, pl.ds(pl.multiple_of((block + core) * 32, 32), 32), :]
-            give[d, k] = acc[k, pl.ds(pl.multiple_of((block + 1 - core) * 32, 32), 32), :]
+            gives[d][k] = acc[k, pl.ds(pl.multiple_of((block + 1 - core) * 32, 32), 32), :]
+
+
+def merge_two_kernel(keep, got, out):
+    out[...] = keep[2] + got[...]
 
 
 def merge_kernel(keep, got, *outs):
-    for d in range(4):
-        outs[d][...] = keep[d] + got[d]
+    for i, d in enumerate((0, 1, 3)):
+        outs[i][...] = keep[d] + got[i]
 
 
 def last_kernel(a, b, c, d, out):
@@ -345,12 +350,12 @@
     shared = pl.pallas_call(
         share_kernel,
         out_shape=jax.ShapeDtypeStruct((32, 32, 128), F32),
-        in_specs=[SM, pl.BlockSpec(memory_space=pltpu.HBM)],
+        in_specs=[pl.BlockSpec(memory_space=pltpu.HBM)],
         out_specs=VM,
         scratch_shapes=[pltpu.VMEM((2, 16, 128), F32), pltpu.SemaphoreType.DMA((2,))],
         compiler_params=grant(60),
         name="share",
-    )(me, aterms)
+    )(aterms)
     sub_tile, tile_of_slot, shared = lax.optimization_barrier((sub_tile, tile_of_slot, shared))
     table = lax.all_to_all(shared.reshape(32, 4096), "bl", 0, 0, tiled=True)
     table = table.reshape(1024, 128)
@@ -389,6 +394,7 @@
     acc = images(uv, [(one, 0), (three, 0)], acc)
     acc, two = lax.optimization_barrier((acc, direct[1]))
     swap_two = shift(two, 0, 1)
+    acc = images(uv, [(swap_one, 1)], acc)
     acc, table = lax.optimization_barrier((acc, table))
     pair = pl.pallas_call(
         pair_kernel,
@@ -400,7 +406,7 @@
     )(ints, table, taper)
     acc, pair = lax.optimization_barrier((acc, pair))
     pair = lax.all_to_all(pair.reshape(8, 2048), "ch", 0, 0, tiled=True).reshape(8, 16, 128)
-    acc = images(uv, [(swap_one, 1), (swap_three, 1), (two, 0), (swap_two, 1)], acc)
+    acc = images(uv, [(swap_three, 1), (two, 0), (swap_two, 1)], acc)
     outgoing = pl.pallas_call(
         finish_kernel,
         out_shape=jax.ShapeDtypeStruct((33 * 32, 128), F32),
@@ -411,27 +417,38 @@
     )(ints, acc, pair, to_image, fold, left3, right3)
     arrived = lax.all_to_all(outgoing.reshape(32, 33 * 128), "bl", 0, 0, tiled=True)
     arrived = arrived.reshape(33 * 32, 128)
+    block = jax.ShapeDtypeStruct((8, 32, 128), F32)
     half = jax.ShapeDtypeStruct((4, 8, 32, 128), F32)
-    keep, give = pl.pallas_call(
+    rest = jax.ShapeDtypeStruct((3, 8, 32, 128), F32)
+    keep, give_two, give = pl.pallas_call(
         place_kernel,
-        out_shape=[half, half],
+        out_shape=[half, block, rest],
         in_specs=[SM, VM],
-        out_specs=[VM, VM],
+        out_specs=[VM] * 3,
         scratch_shapes=[pltpu.VMEM((8, TILE, 128), F32), pltpu.SMEM((64,), jnp.int32)],
         compiler_params=grant(8),
         name="place",
     )(me, arrived)
+    got_two = shift(give_two, 0, 1)
     got = shift(give, 0, 1)
-    block = jax.ShapeDtypeStruct((8, 32, 128), F32)
+    two = pl.pallas_call(
+        merge_two_kernel,
+        out_shape=block,
+        in_specs=[VM, VM],
+        out_specs=VM,
+        compiler_params=grant(6),
+        name="merge2",
+    )(keep, got_two)
+    two = shift(two, 2, 0)
     sums = pl.pallas_call(
         merge_kernel,
-        out_shape=[block] * 4,
+        out_shape=[block] * 3,
         in_specs=[VM, VM],
-        out_specs=[VM] * 4,
+        out_specs=[VM] * 3,
         compiler_params=grant(6),
         name="merge",
     )(keep, got)
-    parts = [sums[0]] + [shift(sums[d], d, 0) for d in range(1, 4)]
+    parts = [sums[0], shift(sums[1], 1, 0), two, shift(sums[2], 3, 0)]
     return pl.pallas_call(
         last_kernel,
         out_shape=jax.ShapeDtypeStruct((1, 32, 4, TILE), F32),

time: 81.9 us -> 82.8 us (1.011)
  blocking collectives: 20.9 us -> 22.3 us
    all_to_all x1, waiting for transfers between devices: 1.83 us -> 0.39 us  [local(): table = lax.all_to_all(shared.reshape(32, 4096), 'bl', 0, 0, tiled=True)]
    all_to_all x1, blocking collectives: 20.9 us -> 22.3 us  [local(): lax.all_to_all(outgoing.reshape(32, 33 * 128), 'bl', 0, 0, tiled=True)]
    all_to_all x1, waiting for transfers between devices: 0.03 us -> 1.04 us  [local(): lax.all_to_all(pair.reshape(8, 2048), 'ch', 0, 0, tiled=True)]
    pallas_call x3 -> x4, Pallas kernels: 9.91 us -> 10.3 us  [images(): pl.pallas_call(functools.partial(image_kernel, picks, first), out_shape=j...]
    ppermute x11 -> x12, starting transfers between devices: 14.6 us -> 14.3 us  [shift(): return lax.ppermute(x, 'ch', pairs)]
    ppermute x11 -> x12, waiting for transfers between devices: 6.38 us -> 6.13 us  [shift(): return lax.ppermute(x, 'ch', pairs)]
  transfers between devices with their start and end apart: 13 -> 14, of which waited for: 4 -> 5; matrix products, arithmetic and copies ran while one was open for 1% -> 1% of each run, Pallas kernels for 15% -> 15%
where the time goes in v5:
time: 82.8 us; the launch traced here: 82.4 us
  starting transfers between devices  33.2 us (40%)
  blocking collectives  22.3 us (27%)
  Pallas kernels  17.5 us (21%)
  waiting for transfers between devices  7.56 us (9%)
  local copies, waits for them, and re-layouts  1.27 us (2%)
    all_to_all x1, blocking collectives, local(): lax.all_to_all(outgoing.reshape(32, 33 * 128), 'bl', 0, 0, tiled=True)  22.3 us
    ppermute x12, starting transfers between devices, shift(): return lax.ppermute(x, 'ch', pairs)  14.3 us
    all_to_all x1, starting transfers between devices, local(): table = lax.all_to_all(shared.reshape(32, 4096), 'bl', 0, 0, tiled=True)  12 us
    pallas_call x4, Pallas kernels, images(): pl.pallas_call(functools.partial(image_kernel, picks, first), out_shape=j...  10.3 us
    all_to_all x1, starting transfers between devices, local(): lax.all_to_all(pair.reshape(8, 2048), 'ch', 0, 0, tiled=True)  6.9 us
    ppermute x12, waiting for transfers between devices, shift(): return lax.ppermute(x, 'ch', pairs)  6.13 us
  transfers between devices with their start and end apart: 14, of which 5 were waited for; matrix products, arithmetic and copies ran while one was open for 1% of the time, Pallas kernels for 15%

profile of v5, /device:TPU:1, one launch (start us, length us, event | category | flops | bytes accessed | tf_op | source)
XLA Modules:
  0.0 82.4 jit_solution(6409469801450436297)
XLA Ops:
  0.0 1.6 %share.1 = f32[32,32,128]{2,1,0:T(8,128)} custom-call(f32[16,2048]{1,0:T(8,128)} %aterms.1), custom_call_target="tpu_custom_call" | custom-call | tf_op jit(solution)/shard_map/share/pallas_call | solution.py:350
  1.7 12.0 %all-to-all-start = ((f32[32,1,4096]{2,1,0:T(1,128)}), f32[32,1,4096]{2,1,0:T(1,128)S(1)}, u32[]{:S(2)}, u32[]{:S(2)}) async-start(f32[32,1,4096]{2,1,0:T(1,128)} %bitcast.19), calls=%async_computation | async-start | bytes 1048576 | tf_op jit(solution)/shard_map/all_to_all | solution.py:360
  13.8 0.2 convert_reduce_fusion
  14.1 0.6 copy-done.8
  14.7 0.6 copy-done.7
  15.3 0.7 pack.1
  16.0 1.4 %collective-permute-start.1 = (f32[2,17,8,128]{3,2,1,0:T(8,128)S(1)}, f32[2,17,8,128]{3,2,1,0:T(8,128)S(1)}, u32[]{:S(2)}, u32[]{:S(2)}) collective-permute-start(f32[2,17,8,128]{3,2,1,0:T(8,128)S(1)} %get-tuple-element.34), channel_id=1, source_target_pairs={{0,2},{1,3},{2,4},{3,5},{4,6},{5,7},{6,0},{7,1},{8,10},{9,11},{10,... | collective-permute-start | bytes 417800 | tf_op jit(solution)/shard_map/ppermute | solution.py:343
  17.3 1.5 %collective-permute-start.2 = (f32[2,17,8,128]{3,2,1,0:T(8,128)S(1)}, f32[2,17,8,128]{3,2,1,0:T(8,128)S(1)}, u32[]{:S(2)}, u32[]{:S(2)}) collective-permute-start(f32[2,17,8,128]{3,2,1,0:T(8,128)S(1)} %get-tuple-element.35), channel_id=1, source_target_pairs={{0,6},{1,7},{2,0},{3,1},{4,2},{5,3},{6,4},{7,5},{8,14},{9,15},{10,... | collective-permute-start | bytes 417800 | tf_op jit(solution)/shard_map/ppermute | solution.py:343
  18.9 1.4 %collective-permute-start = (f32[17,8,128]{2,1,0:T(8,128)S(1)}, f32[17,8,128]{2,1,0:T(8,128)S(1)}, u32[]{:S(2)}, u32[]{:S(2)}) collective-permute-start(f32[17,8,128]{2,1,0:T(8,128)S(1)} %get-tuple-element.33), channel_id=1, source_target_pairs={{0,1},{1,0},{2,3},{3,2},{4,5},{5,4},{6,7},{7,6},{8,9},{9,8},{10,11... | collective-permute-start | bytes 208904 | tf_op jit(solution)/shard_map/ppermute | solution.py:343
  20.2 1.7 %collective-permute-start.4 = (f32[2,17,8,128]{3,2,1,0:T(8,128)S(1)}, f32[2,17,8,128]{3,2,1,0:T(8,128)S(1)}, u32[]{:S(2)}, u32[]{:S(2)}) collective-permute-start(f32[2,17,8,128]{3,2,1,0:T(8,128)S(1)} %get-tuple-element.39), channel_id=1, source_target_pairs={{0,4},{1,5},{2,6},{3,7},{4,0},{5,1},{6,2},{7,3},{8,12},{9,13},{10,... | collective-permute-start | bytes 417800 | tf_op jit(solution)/shard_map/ppermute | solution.py:343
  22.0 2.6 %shard_map.127.refs_2_ = f32[8,64,128]{2,1,0:T(8,128)S(1)} custom-call(f32[2,8,128]{2,1,0:T(8,128)S(1)} %get-tuple-element.31.uv, f32[17,8,128]{2,1,0:T(8,128)S(1)} %get-tuple-element.32.refs_0_, f32[17,8,128]{2,1,0:T(8,128)S(1)} %collective-permute-done.refs_1_), custom_call_target="tpu_custom_call" | custom-call | flops 400000000 | bytes 200000 | tf_op jit(solution)/shard_map/pallas_call | solution.py:193
  24.5 0.4 collective-permute-start.3
  24.9 0.2 collective-permute-start.6
  25.1 2.6 %shard_map.128.refs_1_ = f32[8,64,128]{2,1,0:T(8,128)S(1)} custom-call(f32[2,8,128]{2,1,0:T(8,128)S(1)} %get-tuple-element.31.uv, f32[2,17,8,128]{3,2,1,0:T(8,128)S(1)} %collective-permute-done.1.refs_0_, f32[2,17,8,128]{3,2,1,0:T(8,128)S(1)} %collective-permute-done.2.refs_1_, f32[8,64,128]{2,1,0:T(8,128)S(1)} %shard_map.127.refs_2_), custom_call_target="tpu_custom_call" | custom-call | flops 400000000 | bytes 200000 | tf_op jit(solution)/shard_map/pallas_call | solution.py:193
  27.8 0.4 collective-permute-start.5
  28.1 1.4 %shard_map.129.refs_3_ = f32[8,64,128]{2,1,0:T(8,128)S(1)} custom-call(f32[2,8,128]{2,1,0:T(8,128)S(1)} %get-tuple-element.31.uv, f32[2,17,8,128]{3,2,1,0:T(8,128)S(1)} %collective-permute-done.6.refs_0_, f32[8,64,128]{2,1,0:T(8,128)S(1)} %shard_map.128.refs_1_), custom_call_target="tpu_custom_call" | custom-call | flops 200000000 | bytes 100000 | tf_op jit(solution)/shard_map/pallas_call | solution.py:193
  29.6 0.4 all-to-all-done
  29.9 1.4 %pair.1 = f32[8,16,128]{2,1,0:T(8,128)} custom-call(s32[385]{0:T(512)S(1)} %concatenate.3.ints, f32[1024,128]{1,0:T(8,128)S(1)} %bitcast.17, f32[8,128]{1,0:T(8,128)S(1)} %copy-done.6), custom_call_target="tpu_custom_call" | custom-call | tf_op jit(solution)/shard_map/pair/pallas_call | solution.py:399
  31.4 6.9 %all-to-all-start.1 = ((f32[8,1,2048]{2,1,0:T(1,128)}), f32[8,1,2048]{2,1,0:T(1,128)S(1)}, u32[]{:S(2)}, u32[]{:S(2)}) async-start(f32[8,1,2048]{2,1,0:T(1,128)} %bitcast.7), calls=%async_computation.1 | async-start | bytes 131072 | tf_op jit(solution)/shard_map/all_to_all | solution.py:408
  38.3 3.8 %shard_map.130.acc = f32[8,64,128]{2,1,0:T(8,128)S(1)} custom-call(f32[2,8,128]{2,1,0:T(8,128)S(1)} %get-tuple-element.31.uv, f32[2,17,8,128]{3,2,1,0:T(8,128)S(1)} %collective-permute-done.3.refs_0_, f32[2,17,8,128]{3,2,1,0:T(8,128)S(1)} %collective-permute-done.4.refs_1_, f32[2,17,8,128]{3,2,1,0:T(8,128)S(1)} %collective-permute-done.5.refs_2_, ...), custom_call_target="tpu_custom_call" | custom-call | flops 600000000 | bytes 300000 | tf_op jit(solution)/shard_map/pallas_call | solution.py:193
  42.1 1.0 %all-to-all-done.1 = f32[8,1,2048]{2,1,0:T(1,128)S(1)} async-done(((f32[8,1,2048]{2,1,0:T(1,128)}), f32[8,1,2048]{2,1,0:T(1,128)S(1)}, u32[]{:S(2)}, u32[]{:S(2)}) %all-to-all-start.1) | async-done | bytes 65568 | tf_op jit(solution)/shard_map/all_to_all | solution.py:408
  43.2 1.3 %finish.1 = f32[1056,128]{1,0:T(8,128)S(1)} custom-call(s32[385]{0:T(512)S(1)} %concatenate.3.ints, f32[8,64,128]{2,1,0:T(8,128)S(1)} %shard_map.130.acc, f32[8,16,128]{2,1,0:T(8,128)S(1)} %bitcast.18, bf16[256,128]{1,0:T(8,128)(2,1)S(1)} %copy-done.3, bf16[2,128,128]{2,1,0:T(8,128)(2,1)S(1)} %copy-done.2, bf16[32,192]{1,0:T(8,128)(2,1)S(1)} %copy-done.5, ...), custom_call_target="tpu_custom_call" | custom-call | tf_op jit(solution)/shard_map/finish/pallas_call | solution.py:410
  44.5 22.3 %all_to_all.27 = f32[32,1,4224]{2,1,0:T(1,128)S(1)} all-to-all(f32[32,1,4224]{2,1,0:T(1,128)S(1)} %bitcast.15), channel_id=1, replica_groups=mesh['bl'=32,'ch'=8] {'bl'}, dimensions={0} | all-to-all | bytes 1081344 | tf_op jit(solution)/shard_map/all_to_all | solution.py:418
  66.8 1.4 %place.1 = (f32[4,8,32,128]{3,2,1,0:T(8,128)S(1)}, f32[8,32,128]{2,1,0:T(8,128)S(1)}, f32[3,8,32,128]{3,2,1,0:T(8,128)S(1)}) custom-call(s32[1]{0:T(128)} %bitcast.me_ref, f32[1056,128]{1,0:T(8,128)S(1)} %bitcast.16), custom_call_target="tpu_custom_call" | custom-call | tf_op jit(solution)/shard_map/place/pallas_call | solution.py:423
  68.2 2.5 %collective-permute-start.7 = (f32[3,8,32,128]{3,2,1,0:T(8,128)S(1)}, f32[3,8,32,128]{3,2,1,0:T(8,128)S(1)}, u32[]{:S(2)}, u32[]{:S(2)}) collective-permute-start(f32[3,8,32,128]{3,2,1,0:T(8,128)S(1)} %get-tuple-element.48), channel_id=1, source_target_pairs={{0,1},{1,0},{2,3},{3,2},{4,5},{5,4},{6,7},{7,6},{8,9},{9,8},{10,11... | collective-permute-start | bytes 1179656 | tf_op jit(solution)/shard_map/ppermute | solution.py:343
  70.8 1.4 %collective-permute-done.9.got = f32[8,32,128]{2,1,0:T(8,128)S(1)} collective-permute-done((f32[8,32,128]{2,1,0:T(8,128)S(1)}, f32[8,32,128]{2,1,0:T(8,128)S(1)}, u32[]{:S(2)}, u32[]{:S(2)}) %collective-permute-start.9) | collective-permute-done | bytes 131104 | tf_op jit(solution)/shard_map/ppermute | solution.py:343
  72.2 2.0 %collective-permute-start.10 = (f32[8,32,128]{2,1,0:T(8,128)S(1)}, f32[8,32,128]{2,1,0:T(8,128)S(1)}, u32[]{:S(2)}, u32[]{:S(2)}) collective-permute-start(f32[8,32,128]{2,1,0:T(8,128)S(1)} %merge2.1), channel_id=1, source_target_pairs={{0,4},{1,5},{2,6},{3,7},{4,0},{5,1},{6,2},{7,3},{8,12},{9,13},{10,... | collective-permute-start | bytes 393224 | tf_op jit(solution)/shard_map/ppermute | solution.py:343
  74.3 0.4 collective-permute-start.8
  74.7 2.4 %collective-permute-start.11 = (f32[8,32,128]{2,1,0:T(8,128)S(1)}, f32[8,32,128]{2,1,0:T(8,128)S(1)}, u32[]{:S(2)}, u32[]{:S(2)}) collective-permute-start(f32[8,32,128]{2,1,0:T(8,128)S(1)} %get-tuple-element.52), channel_id=1, source_target_pairs={{0,6},{1,7},{2,0},{3,1},{4,2},{5,3},{6,4},{7,5},{8,14},{9,15},{10,... | collective-permute-start | bytes 393224 | tf_op jit(solution)/shard_map/ppermute | solution.py:343
  77.0 1.5 %collective-permute-done.10.c = f32[8,32,128]{2,1,0:T(8,128)S(1)} collective-permute-done((f32[8,32,128]{2,1,0:T(8,128)S(1)}, f32[8,32,128]{2,1,0:T(8,128)S(1)}, u32[]{:S(2)}, u32[]{:S(2)}) %collective-permute-start.10) | collective-permute-done | bytes 131104 | tf_op jit(solution)/shard_map/ppermute | solution.py:343
  78.5 3.2 %collective-permute-done.8.b = f32[8,32,128]{2,1,0:T(8,128)S(1)} collective-permute-done((f32[8,32,128]{2,1,0:T(8,128)S(1)}, f32[8,32,128]{2,1,0:T(8,128)S(1)}, u32[]{:S(2)}, u32[]{:S(2)}) %collective-permute-start.8) | collective-permute-done | bytes 131104 | tf_op jit(solution)/shard_map/ppermute | solution.py:343
  81.7 0.7 last.1
  (39 shorter events, 0.5 us)
Async XLA Ops:
  1.6 12.1 %copy-start.10 = (s32[64]{0:T(128)S(1)}, s32[64]{0:T(128)}, u32[]{:S(2)}) copy-start(s32[64]{0:T(128)} %param.18) | copy-start | bytes 772
  1.6 12.1 %copy-start.11 = (s32[32]{0:T(128)S(1)}, s32[32]{0:T(128)}, u32[]{:S(2)}) copy-start(s32[32]{0:T(128)} %param.20) | copy-start | bytes 388
  1.6 12.5 %copy-start.9 = (s32[64,2]{0,1:T(2,128)S(1)}, s32[64,2]{0,1:T(2,128)}, u32[]{:S(2)}) copy-start(s32[64,2]{0,1:T(2,128)} %param.17) | copy-start | bytes 1540
  1.6 13.1 %copy-start = (f32[2,64,8,128]{3,2,1,0:T(8,128)S(1)}, f32[2,64,8,128]{3,2,1,0:T(8,128)}, u32[]{:S(2)}) copy-start(f32[2,64,8,128]{3,2,1,0:T(8,128)} %vis.1) | copy-start | bytes 1572868
  1.6 13.1 %copy-start.4 = (f32[2,64,128]{2,1,0:T(8,128)S(1)}, f32[2,64,128]{2,1,0:T(8,128)}, u32[]{:S(2)}) copy-start(f32[2,64,128]{2,1,0:T(8,128)} %coord.1) | copy-start | bytes 196612
  1.7 28.3 %all-to-all-start = ((f32[32,1,4096]{2,1,0:T(1,128)}), f32[32,1,4096]{2,1,0:T(1,128)S(1)}, u32[]{:S(2)}, u32[]{:S(2)}) async-start(f32[32,1,4096]{2,1,0:T(1,128)} %bitcast.19), calls=%async_computation | async-start | bytes 1048576 | tf_op jit(solution)/shard_map/all_to_all | solution.py:360
  14.0 0.7 copy-start.8
  14.7 0.7 copy-start.7
  16.0 8.5 %collective-permute-start.1 = (f32[2,17,8,128]{3,2,1,0:T(8,128)S(1)}, f32[2,17,8,128]{3,2,1,0:T(8,128)S(1)}, u32[]{:S(2)}, u32[]{:S(2)}) collective-permute-start(f32[2,17,8,128]{3,2,1,0:T(8,128)S(1)} %get-tuple-element.34), channel_id=1, source_target_pairs={{0,2},{1,3},{2,4},{3,5},{4,6},{5,7},{6,0},{7,1},{8,10},{9,11},{10,... | collective-permute-start | bytes 417800 | tf_op jit(solution)/shard_map/ppermute | solution.py:343
  17.3 7.2 %collective-permute-start.2 = (f32[2,17,8,128]{3,2,1,0:T(8,128)S(1)}, f32[2,17,8,128]{3,2,1,0:T(8,128)S(1)}, u32[]{:S(2)}, u32[]{:S(2)}) collective-permute-start(f32[2,17,8,128]{3,2,1,0:T(8,128)S(1)} %get-tuple-element.35), channel_id=1, source_target_pairs={{0,6},{1,7},{2,0},{3,1},{4,2},{5,3},{6,4},{7,5},{8,14},{9,15},{10,... | collective-permute-start | bytes 417800 | tf_op jit(solution)/shard_map/ppermute | solution.py:343
  18.9 3.1 %collective-permute-start = (f32[17,8,128]{2,1,0:T(8,128)S(1)}, f32[17,8,128]{2,1,0:T(8,128)S(1)}, u32[]{:S(2)}, u32[]{:S(2)}) collective-permute-start(f32[17,8,128]{2,1,0:T(8,128)S(1)} %get-tuple-element.33), channel_id=1, source_target_pairs={{0,1},{1,0},{2,3},{3,2},{4,5},{5,4},{6,7},{7,6},{8,9},{9,8},{10,11... | collective-permute-start | bytes 208904 | tf_op jit(solution)/shard_map/ppermute | solution.py:343
  20.2 7.5 %collective-permute-start.4 = (f32[2,17,8,128]{3,2,1,0:T(8,128)S(1)}, f32[2,17,8,128]{3,2,1,0:T(8,128)S(1)}, u32[]{:S(2)}, u32[]{:S(2)}) collective-permute-start(f32[2,17,8,128]{3,2,1,0:T(8,128)S(1)} %get-tuple-element.39), channel_id=1, source_target_pairs={{0,4},{1,5},{2,6},{3,7},{4,0},{5,1},{6,2},{7,3},{8,12},{9,13},{10,... | collective-permute-start | bytes 417800 | tf_op jit(solution)/shard_map/ppermute | solution.py:343
  24.5 13.8 %collective-permute-start.3 = (f32[2,17,8,128]{3,2,1,0:T(8,128)S(1)}, f32[2,17,8,128]{3,2,1,0:T(8,128)S(1)}, u32[]{:S(2)}, u32[]{:S(2)}) collective-permute-start(f32[2,17,8,128]{3,2,1,0:T(8,128)S(1)} %collective-permute-done.2.refs_1_), channel_id=1, source_target_pairs={{0,1},{1,0},{2,3},{3,2},{4,5},{5,4},{6,7},{7,6},{8,9},{9,8},{10,11... | collective-permute-start | bytes 417800 | tf_op jit(solution)/shard_map/ppermute | solution.py:343
  24.9 3.2 %collective-permute-start.6 = (f32[2,17,8,128]{3,2,1,0:T(8,128)S(1)}, f32[2,17,8,128]{3,2,1,0:T(8,128)S(1)}, u32[]{:S(2)}, u32[]{:S(2)}) collective-permute-start(f32[2,17,8,128]{3,2,1,0:T(8,128)S(1)} %collective-permute-done.1.refs_0_), channel_id=1, source_target_pairs={{0,1},{1,0},{2,3},{3,2},{4,5},{5,4},{6,7},{7,6},{8,9},{9,8},{10,11... | collective-permute-start | bytes 417800 | tf_op jit(solution)/shard_map/ppermute | solution.py:343
  27.8 10.6 %collective-permute-start.5 = (f32[2,17,8,128]{3,2,1,0:T(8,128)S(1)}, f32[2,17,8,128]{3,2,1,0:T(8,128)S(1)}, u32[]{:S(2)}, u32[]{:S(2)}) collective-permute-start(f32[2,17,8,128]{3,2,1,0:T(8,128)S(1)} %collective-permute-done.4.refs_1_), channel_id=1, source_target_pairs={{0,1},{1,0},{2,3},{3,2},{4,5},{5,4},{6,7},{7,6},{8,9},{9,8},{10,11... | collective-permute-start | bytes 417800 | tf_op jit(solution)/shard_map/ppermute | solution.py:343
  28.1 1.8 %copy-start.6 = (f32[8,128]{1,0:T(8,128)S(1)}, f32[8,128]{1,0:T(8,128)}, u32[]{:S(2)}) copy-start(f32[8,128]{1,0:T(8,128)} %constant.18.clone.taper) | copy-start | bytes 12292
  31.4 11.8 %all-to-all-start.1 = ((f32[8,1,2048]{2,1,0:T(1,128)}), f32[8,1,2048]{2,1,0:T(1,128)S(1)}, u32[]{:S(2)}, u32[]{:S(2)}) async-start(f32[8,1,2048]{2,1,0:T(1,128)} %bitcast.7), calls=%async_computation.1 | async-start | bytes 131072 | tf_op jit(solution)/shard_map/all_to_all | solution.py:408
  38.3 4.9 %copy-start.1 = (bf16[384,128]{1,0:T(8,128)(2,1)S(1)}, bf16[384,128]{1,0:T(8,128)(2,1)}, u32[]{:S(2)}) copy-start(bf16[384,128]{1,0:T(8,128)(2,1)} %constant.22.clone.right3) | copy-start | bytes 294916
  38.3 4.9 %copy-start.2 = (bf16[2,128,128]{2,1,0:T(8,128)(2,1)S(1)}, bf16[2,128,128]{2,1,0:T(8,128)(2,1)}, u32[]{:S(2)}) copy-start(bf16[2,128,128]{2,1,0:T(8,128)(2,1)} %constant.20.clone.fold) | copy-start | bytes 196612
  38.3 4.9 %copy-start.3 = (bf16[256,128]{1,0:T(8,128)(2,1)S(1)}, bf16[256,128]{1,0:T(8,128)(2,1)}, u32[]{:S(2)}) copy-start(bf16[256,128]{1,0:T(8,128)(2,1)} %constant.19.clone.to_image) | copy-start | bytes 196612
  38.3 4.9 %copy-start.5 = (bf16[32,192]{1,0:T(8,128)(2,1)S(1)}, bf16[32,192]{1,0:T(8,128)(2,1)}, u32[]{:S(2)}) copy-start(bf16[32,192]{1,0:T(8,128)(2,1)} %constant.21.clone.left3) | copy-start | bytes 36868
  68.2 6.1 %collective-permute-start.7 = (f32[3,8,32,128]{3,2,1,0:T(8,128)S(1)}, f32[3,8,32,128]{3,2,1,0:T(8,128)S(1)}, u32[]{:S(2)}, u32[]{:S(2)}) collective-permute-start(f32[3,8,32,128]{3,2,1,0:T(8,128)S(1)} %get-tuple-element.48), channel_id=1, source_target_pairs={{0,1},{1,0},{2,3},{3,2},{4,5},{5,4},{6,7},{7,6},{8,9},{9,8},{10,11... | collective-permute-start | bytes 1179656 | tf_op jit(solution)/shard_map/ppermute | solution.py:343
  70.7 1.5 %collective-permute-start.9 = (f32[8,32,128]{2,1,0:T(8,128)S(1)}, f32[8,32,128]{2,1,0:T(8,128)S(1)}, u32[]{:S(2)}, u32[]{:S(2)}) collective-permute-start(f32[8,32,128]{2,1,0:T(8,128)S(1)} %get-tuple-element.51), channel_id=1, source_target_pairs={{0,1},{1,0},{2,3},{3,2},{4,5},{5,4},{6,7},{7,6},{8,9},{9,8},{10,11... | collective-permute-start | bytes 393224 | tf_op jit(solution)/shard_map/ppermute | solution.py:343
  72.2 6.3 %collective-permute-start.10 = (f32[8,32,128]{2,1,0:T(8,128)S(1)}, f32[8,32,128]{2,1,0:T(8,128)S(1)}, u32[]{:S(2)}, u32[]{:S(2)}) collective-permute-start(f32[8,32,128]{2,1,0:T(8,128)S(1)} %merge2.1), channel_id=1, source_target_pairs={{0,4},{1,5},{2,6},{3,7},{4,0},{5,1},{6,2},{7,3},{8,12},{9,13},{10,... | collective-permute-start | bytes 393224 | tf_op jit(solution)/shard_map/ppermute | solution.py:343
  74.3 7.4 %collective-permute-start.8 = (f32[8,32,128]{2,1,0:T(8,128)S(1)}, f32[8,32,128]{2,1,0:T(8,128)S(1)}, u32[]{:S(2)}, u32[]{:S(2)}) collective-permute-start(f32[8,32,128]{2,1,0:T(8,128)S(1)} %get-tuple-element.50), channel_id=1, source_target_pairs={{0,2},{1,3},{2,4},{3,5},{4,6},{5,7},{6,0},{7,1},{8,10},{9,11},{10,... | collective-permute-start | bytes 393224 | tf_op jit(solution)/shard_map/ppermute | solution.py:343
  74.7 7.0 %collective-permute-start.11 = (f32[8,32,128]{2,1,0:T(8,128)S(1)}, f32[8,32,128]{2,1,0:T(8,128)S(1)}, u32[]{:S(2)}, u32[]{:S(2)}) collective-permute-start(f32[8,32,128]{2,1,0:T(8,128)S(1)} %get-tuple-element.52), channel_id=1, source_target_pairs={{0,6},{1,7},{2,0},{3,1},{4,2},{5,3},{6,4},{7,5},{8,14},{9,15},{10,... | collective-permute-start | bytes 393224 | tf_op jit(solution)/shard_map/ppermute | solution.py:343

commit v6 on v4

--- a/solution.py
+++ b/solution.py
@@ -314,11 +314,13 @@
         return unused
 
     lax.fori_loop(0, 32, one, 0, unroll=4)
+    sign = 1 - 2 * core
     for d in range(4):
-        block = ((y + d) & 3) << 1
+        own = (((y + sign * d) & 3) << 1) + core
+        other = (((y - sign * d) & 3) << 1) + 1 - core
         for k in range(8):
-            keep[d, k] = acc[k, pl.ds(pl.multiple_of((block + core) * 32, 32), 32), :]
-            give[d, k] = acc[k, pl.ds(pl.multiple_of((block + 1 - core) * 32, 32), 32), :]
+            keep[d, k] = acc[k, pl.ds(pl.multiple_of(own * 32, 32), 32), :]
+            give[d, k] = acc[k, pl.ds(pl.multiple_of(other * 32, 32), 32), :]
 
 
 def merge_kernel(keep, got, *outs):
@@ -326,15 +328,24 @@
         outs[d][...] = keep[d] + got[d]
 
 
-def last_kernel(a, b, c, d, out):
+def join_kernel(a, b, out):
+    out[...] = a[...] + b[...]
+
+
+def last_kernel(a, b, c, out):
     for m in range(4):
         for half in range(2):
             k = 2 * m + half
-            out[0, :, m, 128 * half : 128 * half + 128] = (a[k] + b[k]) + (c[k] + d[k])
+            out[0, :, m, 128 * half : 128 * half + 128] = a[k] + b[k] + c[k]
 
 
 def shift(x, dy, dc):
     pairs = [(i, ((i // 2 + dy) % 4) * 2 + (i + dc) % 2) for i in range(8)]
+    return lax.ppermute(x, "ch", pairs)
+
+
+def step_y(x, way):
+    pairs = [(i, ((i // 2 + way * (1 - 2 * (i % 2))) % 4) * 2 + i % 2) for i in range(8)]
     return lax.ppermute(x, "ch", pairs)
 
 
@@ -431,15 +442,25 @@
         compiler_params=grant(6),
         name="merge",
     )(keep, got)
-    parts = [sums[0]] + [shift(sums[d], d, 0) for d in range(1, 4)]
+    relayed = step_y(sums[2], 1)
+    back = step_y(sums[3], -1)
+    onward = pl.pallas_call(
+        join_kernel,
+        out_shape=block,
+        in_specs=[VM, VM],
+        out_specs=VM,
+        compiler_params=grant(4),
+        name="join",
+    )(sums[1], relayed)
+    ahead = step_y(onward, 1)
     return pl.pallas_call(
         last_kernel,
         out_shape=jax.ShapeDtypeStruct((1, 32, 4, TILE), F32),
-        in_specs=[VM] * 4,
+        in_specs=[VM] * 3,
         out_specs=VM,
         compiler_params=grant(4),
         name="last",
-    )(*parts)
+    )(sums[0], back, ahead)
 
 
 def solution(mesh):

time: 81.9 us -> 82.9 us (1.012)
  starting transfers between devices: 33.4 us -> 34.6 us
    ppermute x0 -> x3, starting transfers between devices: none -> 6.22 us  [step_y(): return lax.ppermute(x, 'ch', pairs)]
    ppermute x11 -> x8, starting transfers between devices: 14.6 us -> 9.43 us  [shift(): return lax.ppermute(x, 'ch', pairs)]
    ppermute x11 -> x8, waiting for transfers between devices: 6.38 us -> 1.56 us  [shift(): return lax.ppermute(x, 'ch', pairs)]
    ppermute x0 -> x3, waiting for transfers between devices: none -> 4.12 us  [step_y(): return lax.ppermute(x, 'ch', pairs)]
where the time goes in v6:
time: 82.9 us; the launch traced here: 81.9 us
  starting transfers between devices  34.6 us (42%)
  blocking collectives  20.9 us (25%)
  Pallas kernels  17.1 us (21%)
  waiting for transfers between devices  7.53 us (9%)
  local copies, waits for them, and re-layouts  1.27 us (2%)
    all_to_all x1, blocking collectives, local(): lax.all_to_all(outgoing.reshape(32, 33 * 128), 'bl', 0, 0, tiled=True)  20.9 us
    all_to_all x1, starting transfers between devices, local(): table = lax.all_to_all(shared.reshape(32, 4096), 'bl', 0, 0, tiled=True)  12 us
    pallas_call x3, Pallas kernels, images(): pl.pallas_call(functools.partial(image_kernel, picks, first), out_shape=j...  9.91 us
    ppermute x8, starting transfers between devices, shift(): return lax.ppermute(x, 'ch', pairs)  9.43 us
    all_to_all x1, starting transfers between devices, local(): lax.all_to_all(pair.reshape(8, 2048), 'ch', 0, 0, tiled=True)  6.9 us
    ppermute x3, starting transfers between devices, step_y(): return lax.ppermute(x, 'ch', pairs)  6.22 us
    ppermute x3, waiting for transfers between devices, step_y(): return lax.ppermute(x, 'ch', pairs)  4.12 us
    all_to_all x1, waiting for transfers between devices, local(): table = lax.all_to_all(shared.reshape(32, 4096), 'bl', 0, 0, tiled=True)  1.83 us
  transfers between devices with their start and end apart: 13, of which 4 were waited for; matrix products, arithmetic and copies ran while one was open for 1% of the time, Pallas kernels for 15%

profile of v6, /device:TPU:1, one launch (start us, length us, event | category | flops | bytes accessed | tf_op | source)
XLA Modules:
  0.0 81.9 jit_solution(17342982749033078043)
XLA Ops:
  0.0 1.6 %share.1 = f32[32,32,128]{2,1,0:T(8,128)} custom-call(s32[1]{0:T(128)} %bitcast.me_ref, f32[16,2048]{1,0:T(8,128)} %aterms.1), custom_call_target="tpu_custom_call" | custom-call | tf_op jit(solution)/shard_map/share/pallas_call | solution.py:356
  1.7 12.0 %all-to-all-start = ((f32[32,1,4096]{2,1,0:T(1,128)}), f32[32,1,4096]{2,1,0:T(1,128)S(1)}, u32[]{:S(2)}, u32[]{:S(2)}) async-start(f32[32,1,4096]{2,1,0:T(1,128)} %bitcast.19), calls=%async_computation | async-start | bytes 1048576 | tf_op jit(solution)/shard_map/all_to_all | solution.py:366
  13.7 0.1 select_reduce_fusion.1
  13.8 0.2 convert_reduce_fusion
  14.0 0.1 select_reduce_fusion
  14.1 0.6 copy-done.8
  14.7 0.1 concatenate.3.ints
  14.7 0.6 copy-done.7
  15.3 0.7 pack.1
  16.0 1.4 %collective-permute-start.1 = (f32[2,17,8,128]{3,2,1,0:T(8,128)S(1)}, f32[2,17,8,128]{3,2,1,0:T(8,128)S(1)}, u32[]{:S(2)}, u32[]{:S(2)}) collective-permute-start(f32[2,17,8,128]{3,2,1,0:T(8,128)S(1)} %get-tuple-element.34), channel_id=1, source_target_pairs={{0,2},{1,3},{2,4},{3,5},{4,6},{5,7},{6,0},{7,1},{8,10},{9,11},{10,... | collective-permute-start | bytes 417800 | tf_op jit(solution)/shard_map/ppermute | solution.py:344
  17.4 1.5 %collective-permute-start.2 = (f32[2,17,8,128]{3,2,1,0:T(8,128)S(1)}, f32[2,17,8,128]{3,2,1,0:T(8,128)S(1)}, u32[]{:S(2)}, u32[]{:S(2)}) collective-permute-start(f32[2,17,8,128]{3,2,1,0:T(8,128)S(1)} %get-tuple-element.35), channel_id=1, source_target_pairs={{0,6},{1,7},{2,0},{3,1},{4,2},{5,3},{6,4},{7,5},{8,14},{9,15},{10,... | collective-permute-start | bytes 417800 | tf_op jit(solution)/shard_map/ppermute | solution.py:344
  18.9 1.4 %collective-permute-start = (f32[17,8,128]{2,1,0:T(8,128)S(1)}, f32[17,8,128]{2,1,0:T(8,128)S(1)}, u32[]{:S(2)}, u32[]{:S(2)}) collective-permute-start(f32[17,8,128]{2,1,0:T(8,128)S(1)} %get-tuple-element.33), channel_id=1, source_target_pairs={{0,1},{1,0},{2,3},{3,2},{4,5},{5,4},{6,7},{7,6},{8,9},{9,8},{10,11... | collective-permute-start | bytes 208904 | tf_op jit(solution)/shard_map/ppermute | solution.py:344
  20.2 1.7 %collective-permute-start.5 = (f32[2,17,8,128]{3,2,1,0:T(8,128)S(1)}, f32[2,17,8,128]{3,2,1,0:T(8,128)S(1)}, u32[]{:S(2)}, u32[]{:S(2)}) collective-permute-start(f32[2,17,8,128]{3,2,1,0:T(8,128)S(1)} %get-tuple-element.39), channel_id=1, source_target_pairs={{0,4},{1,5},{2,6},{3,7},{4,0},{5,1},{6,2},{7,3},{8,12},{9,13},{10,... | collective-permute-start | bytes 417800 | tf_op jit(solution)/shard_map/ppermute | solution.py:344
  22.0 2.6 %shard_map.127.refs_2_ = f32[8,64,128]{2,1,0:T(8,128)S(1)} custom-call(f32[2,8,128]{2,1,0:T(8,128)S(1)} %get-tuple-element.31.uv, f32[17,8,128]{2,1,0:T(8,128)S(1)} %get-tuple-element.32.refs_0_, f32[17,8,128]{2,1,0:T(8,128)S(1)} %collective-permute-done.refs_1_), custom_call_target="tpu_custom_call" | custom-call | flops 400000000 | bytes 200000 | tf_op jit(solution)/shard_map/pallas_call | solution.py:193
  24.5 0.4 collective-permute-start.3
  24.9 0.2 collective-permute-start.4
  25.1 2.6 %shard_map.128.refs_4_ = f32[8,64,128]{2,1,0:T(8,128)S(1)} custom-call(f32[2,8,128]{2,1,0:T(8,128)S(1)} %get-tuple-element.31.uv, f32[2,17,8,128]{3,2,1,0:T(8,128)S(1)} %collective-permute-done.1.refs_0_, f32[2,17,8,128]{3,2,1,0:T(8,128)S(1)} %collective-permute-done.2.refs_1_, f32[8,64,128]{2,1,0:T(8,128)S(1)} %shard_map.127.refs_2_), custom_call_target="tpu_custom_call" | custom-call | flops 400000000 | bytes 200000 | tf_op jit(solution)/shard_map/pallas_call | solution.py:193
  27.8 0.4 collective-permute-start.6
  28.1 1.8 %all-to-all-done = f32[32,1,4096]{2,1,0:T(1,128)S(1)} async-done(((f32[32,1,4096]{2,1,0:T(1,128)}), f32[32,1,4096]{2,1,0:T(1,128)S(1)}, u32[]{:S(2)}, u32[]{:S(2)}) %all-to-all-start) | async-done | bytes 524320 | tf_op jit(solution)/shard_map/all_to_all | solution.py:366
  30.0 1.4 %pair.1 = f32[8,16,128]{2,1,0:T(8,128)} custom-call(s32[385]{0:T(512)S(1)} %concatenate.3.ints, f32[1024,128]{1,0:T(8,128)S(1)} %bitcast.17, f32[8,128]{1,0:T(8,128)S(1)} %copy-done.6), custom_call_target="tpu_custom_call" | custom-call | tf_op jit(solution)/shard_map/pair/pallas_call | solution.py:404
  31.4 6.9 %all-to-all-start.1 = ((f32[8,1,2048]{2,1,0:T(1,128)}), f32[8,1,2048]{2,1,0:T(1,128)S(1)}, u32[]{:S(2)}, u32[]{:S(2)}) async-start(f32[8,1,2048]{2,1,0:T(1,128)} %bitcast.7), calls=%async_computation.1 | async-start | bytes 131072 | tf_op jit(solution)/shard_map/all_to_all | solution.py:413
  38.3 4.8 %shard_map.129.acc = f32[8,64,128]{2,1,0:T(8,128)S(1)} custom-call(f32[2,8,128]{2,1,0:T(8,128)S(1)} %get-tuple-element.31.uv, f32[2,17,8,128]{3,2,1,0:T(8,128)S(1)} %collective-permute-done.3.refs_0_, f32[2,17,8,128]{3,2,1,0:T(8,128)S(1)} %collective-permute-done.4.refs_1_, f32[2,17,8,128]{3,2,1,0:T(8,128)S(1)} %collective-permute-done.5.refs_2_, ...), custom_call_target="tpu_custom_call" | custom-call | flops 800000000 | bytes 400000 | tf_op jit(solution)/shard_map/pallas_call | solution.py:193
  43.2 1.3 %finish.1 = f32[1056,128]{1,0:T(8,128)S(1)} custom-call(s32[385]{0:T(512)S(1)} %concatenate.3.ints, f32[8,64,128]{2,1,0:T(8,128)S(1)} %shard_map.129.acc, f32[8,16,128]{2,1,0:T(8,128)S(1)} %bitcast.18, bf16[256,128]{1,0:T(8,128)(2,1)S(1)} %copy-done.3, bf16[2,128,128]{2,1,0:T(8,128)(2,1)S(1)} %copy-done.2, bf16[32,192]{1,0:T(8,128)(2,1)S(1)} %copy-done.5, ...), custom_call_target="tpu_custom_call" | custom-call | tf_op jit(solution)/shard_map/finish/pallas_call | solution.py:415
  44.5 20.9 %all_to_all.27 = f32[32,1,4224]{2,1,0:T(1,128)S(1)} all-to-all(f32[32,1,4224]{2,1,0:T(1,128)S(1)} %bitcast.15), channel_id=1, replica_groups=mesh['bl'=32,'ch'=8] {'bl'}, dimensions={0} | all-to-all | bytes 1081344 | tf_op jit(solution)/shard_map/all_to_all | solution.py:423
  65.3 1.4 %place.1 = (f32[4,8,32,128]{3,2,1,0:T(8,128)S(1)}, f32[4,8,32,128]{3,2,1,0:T(8,128)S(1)}) custom-call(s32[1]{0:T(128)} %bitcast.me_ref, f32[1056,128]{1,0:T(8,128)S(1)} %bitcast.16), custom_call_target="tpu_custom_call" | custom-call | tf_op jit(solution)/shard_map/place/pallas_call | solution.py:426
  66.7 2.5 %collective-permute-start.7 = (f32[4,8,32,128]{3,2,1,0:T(8,128)S(1)}, f32[4,8,32,128]{3,2,1,0:T(8,128)S(1)}, u32[]{:S(2)}, u32[]{:S(2)}) collective-permute-start(f32[4,8,32,128]{3,2,1,0:T(8,128)S(1)} %get-tuple-element.48), channel_id=1, source_target_pairs={{0,1},{1,0},{2,3},{3,2},{4,5},{5,4},{6,7},{7,6},{8,9},{9,8},{10,11... | collective-permute-start | bytes 1572872 | tf_op jit(solution)/shard_map/ppermute | solution.py:344
  69.2 1.5 %collective-permute-done.7.got = f32[4,8,32,128]{3,2,1,0:T(8,128)S(1)} collective-permute-done((f32[4,8,32,128]{3,2,1,0:T(8,128)S(1)}, f32[4,8,32,128]{3,2,1,0:T(8,128)S(1)}, u32[]{:S(2)}, u32[]{:S(2)}) %collective-permute-start.7) | collective-permute-done | bytes 524320 | tf_op jit(solution)/shard_map/ppermute | solution.py:344
  70.8 2.7 %collective-permute-start.9 = (f32[8,32,128]{2,1,0:T(8,128)S(1)}, f32[8,32,128]{2,1,0:T(8,128)S(1)}, u32[]{:S(2)}, u32[]{:S(2)}) collective-permute-start(f32[8,32,128]{2,1,0:T(8,128)S(1)} %get-tuple-element.52), channel_id=1, source_target_pairs={{0,2},{1,7},{2,4},{3,1},{4,6},{5,3},{6,0},{7,5},{8,10},{9,15},{10,... | collective-permute-start | bytes 393224 | tf_op jit(solution)/shard_map/ppermute | solution.py:349
  73.6 2.2 %collective-permute-done.9.b = f32[8,32,128]{2,1,0:T(8,128)S(1)} collective-permute-done((f32[8,32,128]{2,1,0:T(8,128)S(1)}, f32[8,32,128]{2,1,0:T(8,128)S(1)}, u32[]{:S(2)}, u32[]{:S(2)}) %collective-permute-start.9) | collective-permute-done | bytes 131104 | tf_op jit(solution)/shard_map/ppermute | solution.py:349
  75.8 3.5 %collective-permute-start.10 = (f32[8,32,128]{2,1,0:T(8,128)S(1)}, f32[8,32,128]{2,1,0:T(8,128)S(1)}, u32[]{:S(2)}, u32[]{:S(2)}) collective-permute-start(f32[8,32,128]{2,1,0:T(8,128)S(1)} %join.1), channel_id=1, source_target_pairs={{0,2},{1,7},{2,4},{3,1},{4,6},{5,3},{6,0},{7,5},{8,10},{9,15},{10,... | collective-permute-start | bytes 393224 | tf_op jit(solution)/shard_map/ppermute | solution.py:349
  79.3 1.9 %collective-permute-done.10.c = f32[8,32,128]{2,1,0:T(8,128)S(1)} collective-permute-done((f32[8,32,128]{2,1,0:T(8,128)S(1)}, f32[8,32,128]{2,1,0:T(8,128)S(1)}, u32[]{:S(2)}, u32[]{:S(2)}) %collective-permute-start.10) | collective-permute-done | bytes 131104 | tf_op jit(solution)/shard_map/ppermute | solution.py:349
  81.2 0.7 last.1
  (36 shorter events, 0.2 us)
Async XLA Ops:
  1.6 12.1 %copy-start.10 = (s32[64]{0:T(128)S(1)}, s32[64]{0:T(128)}, u32[]{:S(2)}) copy-start(s32[64]{0:T(128)} %param.18) | copy-start | bytes 772
  1.6 12.1 %copy-start.11 = (s32[32]{0:T(128)S(1)}, s32[32]{0:T(128)}, u32[]{:S(2)}) copy-start(s32[32]{0:T(128)} %param.20) | copy-start | bytes 388
  1.6 12.5 %copy-start.9 = (s32[64,2]{0,1:T(2,128)S(1)}, s32[64,2]{0,1:T(2,128)}, u32[]{:S(2)}) copy-start(s32[64,2]{0,1:T(2,128)} %param.17) | copy-start | bytes 1540
  1.6 13.1 %copy-start = (f32[2,64,8,128]{3,2,1,0:T(8,128)S(1)}, f32[2,64,8,128]{3,2,1,0:T(8,128)}, u32[]{:S(2)}) copy-start(f32[2,64,8,128]{3,2,1,0:T(8,128)} %vis.1) | copy-start | bytes 1572868
  1.7 13.1 %copy-start.4 = (f32[2,64,128]{2,1,0:T(8,128)S(1)}, f32[2,64,128]{2,1,0:T(8,128)}, u32[]{:S(2)}) copy-start(f32[2,64,128]{2,1,0:T(8,128)} %coord.1) | copy-start | bytes 196612
  1.7 28.3 %all-to-all-start = ((f32[32,1,4096]{2,1,0:T(1,128)}), f32[32,1,4096]{2,1,0:T(1,128)S(1)}, u32[]{:S(2)}, u32[]{:S(2)}) async-start(f32[32,1,4096]{2,1,0:T(1,128)} %bitcast.19), calls=%async_computation | async-start | bytes 1048576 | tf_op jit(solution)/shard_map/all_to_all | solution.py:366
  14.0 0.7 copy-start.8
  14.7 0.7 copy-start.7
  16.0 8.5 %collective-permute-start.1 = (f32[2,17,8,128]{3,2,1,0:T(8,128)S(1)}, f32[2,17,8,128]{3,2,1,0:T(8,128)S(1)}, u32[]{:S(2)}, u32[]{:S(2)}) collective-permute-start(f32[2,17,8,128]{3,2,1,0:T(8,128)S(1)} %get-tuple-element.34), channel_id=1, source_target_pairs={{0,2},{1,3},{2,4},{3,5},{4,6},{5,7},{6,0},{7,1},{8,10},{9,11},{10,... | collective-permute-start | bytes 417800 | tf_op jit(solution)/shard_map/ppermute | solution.py:344
  17.4 7.2 %collective-permute-start.2 = (f32[2,17,8,128]{3,2,1,0:T(8,128)S(1)}, f32[2,17,8,128]{3,2,1,0:T(8,128)S(1)}, u32[]{:S(2)}, u32[]{:S(2)}) collective-permute-start(f32[2,17,8,128]{3,2,1,0:T(8,128)S(1)} %get-tuple-element.35), channel_id=1, source_target_pairs={{0,6},{1,7},{2,0},{3,1},{4,2},{5,3},{6,4},{7,5},{8,14},{9,15},{10,... | collective-permute-start | bytes 417800 | tf_op jit(solution)/shard_map/ppermute | solution.py:344
  18.9 3.1 %collective-permute-start = (f32[17,8,128]{2,1,0:T(8,128)S(1)}, f32[17,8,128]{2,1,0:T(8,128)S(1)}, u32[]{:S(2)}, u32[]{:S(2)}) collective-permute-start(f32[17,8,128]{2,1,0:T(8,128)S(1)} %get-tuple-element.33), channel_id=1, source_target_pairs={{0,1},{1,0},{2,3},{3,2},{4,5},{5,4},{6,7},{7,6},{8,9},{9,8},{10,11... | collective-permute-start | bytes 208904 | tf_op jit(solution)/shard_map/ppermute | solution.py:344
  20.2 7.5 %collective-permute-start.5 = (f32[2,17,8,128]{3,2,1,0:T(8,128)S(1)}, f32[2,17,8,128]{3,2,1,0:T(8,128)S(1)}, u32[]{:S(2)}, u32[]{:S(2)}) collective-permute-start(f32[2,17,8,128]{3,2,1,0:T(8,128)S(1)} %get-tuple-element.39), channel_id=1, source_target_pairs={{0,4},{1,5},{2,6},{3,7},{4,0},{5,1},{6,2},{7,3},{8,12},{9,13},{10,... | collective-permute-start | bytes 417800 | tf_op jit(solution)/shard_map/ppermute | solution.py:344
  24.5 13.8 %collective-permute-start.3 = (f32[2,17,8,128]{3,2,1,0:T(8,128)S(1)}, f32[2,17,8,128]{3,2,1,0:T(8,128)S(1)}, u32[]{:S(2)}, u32[]{:S(2)}) collective-permute-start(f32[2,17,8,128]{3,2,1,0:T(8,128)S(1)} %collective-permute-done.1.refs_0_), channel_id=1, source_target_pairs={{0,1},{1,0},{2,3},{3,2},{4,5},{5,4},{6,7},{7,6},{8,9},{9,8},{10,11... | collective-permute-start | bytes 417800 | tf_op jit(solution)/shard_map/ppermute | solution.py:344
  24.9 13.4 %collective-permute-start.4 = (f32[2,17,8,128]{3,2,1,0:T(8,128)S(1)}, f32[2,17,8,128]{3,2,1,0:T(8,128)S(1)}, u32[]{:S(2)}, u32[]{:S(2)}) collective-permute-start(f32[2,17,8,128]{3,2,1,0:T(8,128)S(1)} %collective-permute-done.2.refs_1_), channel_id=1, source_target_pairs={{0,1},{1,0},{2,3},{3,2},{4,5},{5,4},{6,7},{7,6},{8,9},{9,8},{10,11... | collective-permute-start | bytes 417800 | tf_op jit(solution)/shard_map/ppermute | solution.py:344
  25.1 4.8 %copy-start.6 = (f32[8,128]{1,0:T(8,128)S(1)}, f32[8,128]{1,0:T(8,128)}, u32[]{:S(2)}) copy-start(f32[8,128]{1,0:T(8,128)} %constant.18.clone.taper) | copy-start | bytes 12292
  27.8 10.6 %collective-permute-start.6 = (f32[2,17,8,128]{3,2,1,0:T(8,128)S(1)}, f32[2,17,8,128]{3,2,1,0:T(8,128)S(1)}, u32[]{:S(2)}, u32[]{:S(2)}) collective-permute-start(f32[2,17,8,128]{3,2,1,0:T(8,128)S(1)} %collective-permute-done.5.refs_2_), channel_id=1, source_target_pairs={{0,1},{1,0},{2,3},{3,2},{4,5},{5,4},{6,7},{7,6},{8,9},{9,8},{10,11... | collective-permute-start | bytes 417800 | tf_op jit(solution)/shard_map/ppermute | solution.py:344
  31.4 11.8 %all-to-all-start.1 = ((f32[8,1,2048]{2,1,0:T(1,128)}), f32[8,1,2048]{2,1,0:T(1,128)S(1)}, u32[]{:S(2)}, u32[]{:S(2)}) async-start(f32[8,1,2048]{2,1,0:T(1,128)} %bitcast.7), calls=%async_computation.1 | async-start | bytes 131072 | tf_op jit(solution)/shard_map/all_to_all | solution.py:413
  38.3 4.9 %copy-start.1 = (bf16[384,128]{1,0:T(8,128)(2,1)S(1)}, bf16[384,128]{1,0:T(8,128)(2,1)}, u32[]{:S(2)}) copy-start(bf16[384,128]{1,0:T(8,128)(2,1)} %constant.22.clone.right3) | copy-start | bytes 294916
  38.3 4.9 %copy-start.2 = (bf16[2,128,128]{2,1,0:T(8,128)(2,1)S(1)}, bf16[2,128,128]{2,1,0:T(8,128)(2,1)}, u32[]{:S(2)}) copy-start(bf16[2,128,128]{2,1,0:T(8,128)(2,1)} %constant.20.clone.fold) | copy-start | bytes 196612
  38.3 4.9 %copy-start.3 = (bf16[256,128]{1,0:T(8,128)(2,1)S(1)}, bf16[256,128]{1,0:T(8,128)(2,1)}, u32[]{:S(2)}) copy-start(bf16[256,128]{1,0:T(8,128)(2,1)} %constant.19.clone.to_image) | copy-start | bytes 196612
  38.3 4.9 %copy-start.5 = (bf16[32,192]{1,0:T(8,128)(2,1)S(1)}, bf16[32,192]{1,0:T(8,128)(2,1)}, u32[]{:S(2)}) copy-start(bf16[32,192]{1,0:T(8,128)(2,1)} %constant.21.clone.left3) | copy-start | bytes 36868
  66.7 4.0 %collective-permute-start.7 = (f32[4,8,32,128]{3,2,1,0:T(8,128)S(1)}, f32[4,8,32,128]{3,2,1,0:T(8,128)S(1)}, u32[]{:S(2)}, u32[]{:S(2)}) collective-permute-start(f32[4,8,32,128]{3,2,1,0:T(8,128)S(1)} %get-tuple-element.48), channel_id=1, source_target_pairs={{0,1},{1,0},{2,3},{3,2},{4,5},{5,4},{6,7},{7,6},{8,9},{9,8},{10,11... | collective-permute-start | bytes 1572872 | tf_op jit(solution)/shard_map/ppermute | solution.py:344
  70.8 4.9 %collective-permute-start.9 = (f32[8,32,128]{2,1,0:T(8,128)S(1)}, f32[8,32,128]{2,1,0:T(8,128)S(1)}, u32[]{:S(2)}, u32[]{:S(2)}) collective-permute-start(f32[8,32,128]{2,1,0:T(8,128)S(1)} %get-tuple-element.52), channel_id=1, source_target_pairs={{0,2},{1,7},{2,4},{3,1},{4,6},{5,3},{6,0},{7,5},{8,10},{9,15},{10,... | collective-permute-start | bytes 393224 | tf_op jit(solution)/shard_map/ppermute | solution.py:349
  73.6 5.7 %collective-permute-start.8 = (f32[8,32,128]{2,1,0:T(8,128)S(1)}, f32[8,32,128]{2,1,0:T(8,128)S(1)}, u32[]{:S(2)}, u32[]{:S(2)}) collective-permute-start(f32[8,32,128]{2,1,0:T(8,128)S(1)} %get-tuple-element.50), channel_id=1, source_target_pairs={{0,6},{1,3},{2,0},{3,5},{4,2},{5,7},{6,4},{7,1},{8,14},{9,11},{10,... | collective-permute-start | bytes 393224 | tf_op jit(solution)/shard_map/ppermute | solution.py:349
  75.8 5.4 %collective-permute-start.10 = (f32[8,32,128]{2,1,0:T(8,128)S(1)}, f32[8,32,128]{2,1,0:T(8,128)S(1)}, u32[]{:S(2)}, u32[]{:S(2)}) collective-permute-start(f32[8,32,128]{2,1,0:T(8,128)S(1)} %join.1), channel_id=1, source_target_pairs={{0,2},{1,7},{2,4},{3,1},{4,6},{5,3},{6,0},{7,5},{8,10},{9,15},{10,... | collective-permute-start | bytes 393224 | tf_op jit(solution)/shard_map/ppermute | solution.py:349

commit v7 on v4

--- a/solution.py
+++ b/solution.py
@@ -84,8 +84,8 @@
     )
 
 
-def share_kernel(me_ref, aterms, shared, strip, sems):
-    me = me_ref[0]
+def share_kernel(aterms, shared, strip, sems):
+    me = lax.axis_index("ch")
     copies = []
     for r in range(2):
         at = pl.multiple_of(1024 * r + me * 128, 128)
@@ -313,7 +313,7 @@
             acc[at] = acc[at] + jnp.where(far, moved[m], 0.0)
         return unused
 
-    lax.fori_loop(0, 32, one, 0, unroll=4)
+    lax.fori_loop(0, 32, one, 0, unroll=16)
     for d in range(4):
         block = ((y + d) & 3) << 1
         for k in range(8):
@@ -345,12 +345,12 @@
     shared = pl.pallas_call(
         share_kernel,
         out_shape=jax.ShapeDtypeStruct((32, 32, 128), F32),
-        in_specs=[SM, pl.BlockSpec(memory_space=pltpu.HBM)],
+        in_specs=[pl.BlockSpec(memory_space=pltpu.HBM)],
         out_specs=VM,
         scratch_shapes=[pltpu.VMEM((2, 16, 128), F32), pltpu.SemaphoreType.DMA((2,))],
         compiler_params=grant(60),
         name="share",
-    )(me, aterms)
+    )(aterms)
     sub_tile, tile_of_slot, shared = lax.optimization_barrier((sub_tile, tile_of_slot, shared))
     table = lax.all_to_all(shared.reshape(32, 4096), "bl", 0, 0, tiled=True)
     table = table.reshape(1024, 128)

time: 81.9 us -> 81.5 us (level)
  no operation moved by 1% of the time
where the time goes in v7:
time: 81.5 us; the launch traced here: 81.1 us
  starting transfers between devices  33.4 us (41%)
  blocking collectives  20.9 us (26%)
  Pallas kernels  16.6 us (20%)
  waiting for transfers between devices  8.26 us (10%)
  local copies, waits for them, and re-layouts  1.27 us (2%)
    all_to_all x1, blocking collectives, local(): lax.all_to_all(outgoing.reshape(32, 33 * 128), 'bl', 0, 0, tiled=True)  20.9 us
    ppermute x11, starting transfers between devices, shift(): return lax.ppermute(x, 'ch', pairs)  14.5 us
    all_to_all x1, starting transfers between devices, local(): table = lax.all_to_all(shared.reshape(32, 4096), 'bl', 0, 0, tiled=True)  12 us
    pallas_call x3, Pallas kernels, images(): pl.pallas_call(functools.partial(image_kernel, picks, first), out_shape=j...  9.88 us
    all_to_all x1, starting transfers between devices, local(): lax.all_to_all(pair.reshape(8, 2048), 'ch', 0, 0, tiled=True)  6.9 us
    ppermute x11, waiting for transfers between devices, shift(): return lax.ppermute(x, 'ch', pairs)  6.39 us
    all_to_all x1, waiting for transfers between devices, local(): table = lax.all_to_all(shared.reshape(32, 4096), 'bl', 0, 0, tiled=True)  1.82 us
  transfers between devices with their start and end apart: 13, of which 4 were waited for; matrix products, arithmetic and copies ran while one was open for 1% of the time, Pallas kernels for 15%

profile of v7, /device:TPU:1, one launch (start us, length us, event | category | flops | bytes accessed | tf_op | source)
XLA Modules:
  0.0 81.1 jit_solution(12152832191708580818)
XLA Ops:
  0.0 1.6 %share.1 = f32[32,32,128]{2,1,0:T(8,128)} custom-call(f32[16,2048]{1,0:T(8,128)} %aterms.1), custom_call_target="tpu_custom_call" | custom-call | tf_op jit(solution)/shard_map/share/pallas_call | solution.py:345
  1.7 12.0 %all-to-all-start = ((f32[32,1,4096]{2,1,0:T(1,128)}), f32[32,1,4096]{2,1,0:T(1,128)S(1)}, u32[]{:S(2)}, u32[]{:S(2)}) async-start(f32[32,1,4096]{2,1,0:T(1,128)} %bitcast.19), calls=%async_computation | async-start | bytes 1048576 | tf_op jit(solution)/shard_map/all_to_all | solution.py:355
  13.7 0.1 select_reduce_fusion.1
  13.8 0.2 convert_reduce_fusion
  14.0 0.1 select_reduce_fusion
  14.1 0.6 copy-done.8
  14.7 0.6 copy-done.7
  15.3 0.7 pack.1
  16.0 1.4 %collective-permute-start.1 = (f32[2,17,8,128]{3,2,1,0:T(8,128)S(1)}, f32[2,17,8,128]{3,2,1,0:T(8,128)S(1)}, u32[]{:S(2)}, u32[]{:S(2)}) collective-permute-start(f32[2,17,8,128]{3,2,1,0:T(8,128)S(1)} %get-tuple-element.34), channel_id=1, source_target_pairs={{0,2},{1,3},{2,4},{3,5},{4,6},{5,7},{6,0},{7,1},{8,10},{9,11},{10,... | collective-permute-start | bytes 417800 | tf_op jit(solution)/shard_map/ppermute | solution.py:338
  17.4 1.5 %collective-permute-start.2 = (f32[2,17,8,128]{3,2,1,0:T(8,128)S(1)}, f32[2,17,8,128]{3,2,1,0:T(8,128)S(1)}, u32[]{:S(2)}, u32[]{:S(2)}) collective-permute-start(f32[2,17,8,128]{3,2,1,0:T(8,128)S(1)} %get-tuple-element.35), channel_id=1, source_target_pairs={{0,6},{1,7},{2,0},{3,1},{4,2},{5,3},{6,4},{7,5},{8,14},{9,15},{10,... | collective-permute-start | bytes 417800 | tf_op jit(solution)/shard_map/ppermute | solution.py:338
  18.9 1.4 %collective-permute-start = (f32[17,8,128]{2,1,0:T(8,128)S(1)}, f32[17,8,128]{2,1,0:T(8,128)S(1)}, u32[]{:S(2)}, u32[]{:S(2)}) collective-permute-start(f32[17,8,128]{2,1,0:T(8,128)S(1)} %get-tuple-element.33), channel_id=1, source_target_pairs={{0,1},{1,0},{2,3},{3,2},{4,5},{5,4},{6,7},{7,6},{8,9},{9,8},{10,11... | collective-permute-start | bytes 208904 | tf_op jit(solution)/shard_map/ppermute | solution.py:338
  20.2 1.7 %collective-permute-start.5 = (f32[2,17,8,128]{3,2,1,0:T(8,128)S(1)}, f32[2,17,8,128]{3,2,1,0:T(8,128)S(1)}, u32[]{:S(2)}, u32[]{:S(2)}) collective-permute-start(f32[2,17,8,128]{3,2,1,0:T(8,128)S(1)} %get-tuple-element.39), channel_id=1, source_target_pairs={{0,4},{1,5},{2,6},{3,7},{4,0},{5,1},{6,2},{7,3},{8,12},{9,13},{10,... | collective-permute-start | bytes 417800 | tf_op jit(solution)/shard_map/ppermute | solution.py:338
  22.0 2.5 %shard_map.127.refs_2_ = f32[8,64,128]{2,1,0:T(8,128)S(1)} custom-call(f32[2,8,128]{2,1,0:T(8,128)S(1)} %get-tuple-element.31.uv, f32[17,8,128]{2,1,0:T(8,128)S(1)} %get-tuple-element.32.refs_0_, f32[17,8,128]{2,1,0:T(8,128)S(1)} %collective-permute-done.refs_1_), custom_call_target="tpu_custom_call" | custom-call | flops 400000000 | bytes 200000 | tf_op jit(solution)/shard_map/pallas_call | solution.py:193
  24.5 0.4 collective-permute-start.3
  24.9 0.2 collective-permute-start.4
  25.1 2.6 %shard_map.128.refs_4_ = f32[8,64,128]{2,1,0:T(8,128)S(1)} custom-call(f32[2,8,128]{2,1,0:T(8,128)S(1)} %get-tuple-element.31.uv, f32[2,17,8,128]{3,2,1,0:T(8,128)S(1)} %collective-permute-done.1.refs_0_, f32[2,17,8,128]{3,2,1,0:T(8,128)S(1)} %collective-permute-done.2.refs_1_, f32[8,64,128]{2,1,0:T(8,128)S(1)} %shard_map.127.refs_2_), custom_call_target="tpu_custom_call" | custom-call | flops 400000000 | bytes 200000 | tf_op jit(solution)/shard_map/pallas_call | solution.py:193
  27.7 0.4 collective-permute-start.6
  28.1 1.8 %all-to-all-done = f32[32,1,4096]{2,1,0:T(1,128)S(1)} async-done(((f32[32,1,4096]{2,1,0:T(1,128)}), f32[32,1,4096]{2,1,0:T(1,128)S(1)}, u32[]{:S(2)}, u32[]{:S(2)}) %all-to-all-start) | async-done | bytes 524320 | tf_op jit(solution)/shard_map/all_to_all | solution.py:355
  30.0 1.4 %pair.1 = f32[8,16,128]{2,1,0:T(8,128)} custom-call(s32[385]{0:T(512)S(1)} %concatenate.3.ints, f32[1024,128]{1,0:T(8,128)S(1)} %bitcast.17, f32[8,128]{1,0:T(8,128)S(1)} %copy-done.6), custom_call_target="tpu_custom_call" | custom-call | tf_op jit(solution)/shard_map/pair/pallas_call | solution.py:393
  31.4 6.9 %all-to-all-start.1 = ((f32[8,1,2048]{2,1,0:T(1,128)}), f32[8,1,2048]{2,1,0:T(1,128)S(1)}, u32[]{:S(2)}, u32[]{:S(2)}) async-start(f32[8,1,2048]{2,1,0:T(1,128)} %bitcast.7), calls=%async_computation.1 | async-start | bytes 131072 | tf_op jit(solution)/shard_map/all_to_all | solution.py:402
  38.3 4.7 %shard_map.129.acc = f32[8,64,128]{2,1,0:T(8,128)S(1)} custom-call(f32[2,8,128]{2,1,0:T(8,128)S(1)} %get-tuple-element.31.uv, f32[2,17,8,128]{3,2,1,0:T(8,128)S(1)} %collective-permute-done.3.refs_0_, f32[2,17,8,128]{3,2,1,0:T(8,128)S(1)} %collective-permute-done.4.refs_1_, f32[2,17,8,128]{3,2,1,0:T(8,128)S(1)} %collective-permute-done.5.refs_2_, ...), custom_call_target="tpu_custom_call" | custom-call | flops 800000000 | bytes 400000 | tf_op jit(solution)/shard_map/pallas_call | solution.py:193
  43.2 1.3 %finish.1 = f32[1056,128]{1,0:T(8,128)S(1)} custom-call(s32[385]{0:T(512)S(1)} %concatenate.3.ints, f32[8,64,128]{2,1,0:T(8,128)S(1)} %shard_map.129.acc, f32[8,16,128]{2,1,0:T(8,128)S(1)} %bitcast.18, bf16[256,128]{1,0:T(8,128)(2,1)S(1)} %copy-done.3, bf16[2,128,128]{2,1,0:T(8,128)(2,1)S(1)} %copy-done.2, bf16[32,192]{1,0:T(8,128)(2,1)S(1)} %copy-done.5, ...), custom_call_target="tpu_custom_call" | custom-call | tf_op jit(solution)/shard_map/finish/pallas_call | solution.py:404
  44.5 20.9 %all_to_all.27 = f32[32,1,4224]{2,1,0:T(1,128)S(1)} all-to-all(f32[32,1,4224]{2,1,0:T(1,128)S(1)} %bitcast.15), channel_id=1, replica_groups=mesh['bl'=32,'ch'=8] {'bl'}, dimensions={0} | all-to-all | bytes 1081344 | tf_op jit(solution)/shard_map/all_to_all | solution.py:412
  65.3 1.0 %place.1 = (f32[4,8,32,128]{3,2,1,0:T(8,128)S(1)}, f32[4,8,32,128]{3,2,1,0:T(8,128)S(1)}) custom-call(s32[1]{0:T(128)} %bitcast.me_ref, f32[1056,128]{1,0:T(8,128)S(1)} %bitcast.16), custom_call_target="tpu_custom_call" | custom-call | tf_op jit(solution)/shard_map/place/pallas_call | solution.py:415
  66.3 2.5 %collective-permute-start.7 = (f32[4,8,32,128]{3,2,1,0:T(8,128)S(1)}, f32[4,8,32,128]{3,2,1,0:T(8,128)S(1)}, u32[]{:S(2)}, u32[]{:S(2)}) collective-permute-start(f32[4,8,32,128]{3,2,1,0:T(8,128)S(1)} %get-tuple-element.48), channel_id=1, source_target_pairs={{0,1},{1,0},{2,3},{3,2},{4,5},{5,4},{6,7},{7,6},{8,9},{9,8},{10,11... | collective-permute-start | bytes 1572872 | tf_op jit(solution)/shard_map/ppermute | solution.py:338
  68.8 1.5 %collective-permute-done.7.got = f32[4,8,32,128]{3,2,1,0:T(8,128)S(1)} collective-permute-done((f32[4,8,32,128]{3,2,1,0:T(8,128)S(1)}, f32[4,8,32,128]{3,2,1,0:T(8,128)S(1)}, u32[]{:S(2)}, u32[]{:S(2)}) %collective-permute-start.7) | collective-permute-done | bytes 524320 | tf_op jit(solution)/shard_map/ppermute | solution.py:338
  70.4 1.5 %collective-permute-start.8 = (f32[8,32,128]{2,1,0:T(8,128)S(1)}, f32[8,32,128]{2,1,0:T(8,128)S(1)}, u32[]{:S(2)}, u32[]{:S(2)}) collective-permute-start(f32[8,32,128]{2,1,0:T(8,128)S(1)} %get-tuple-element.50), channel_id=1, source_target_pairs={{0,2},{1,3},{2,4},{3,5},{4,6},{5,7},{6,0},{7,1},{8,10},{9,11},{10,... | collective-permute-start | bytes 393224 | tf_op jit(solution)/shard_map/ppermute | solution.py:338
  71.9 2.4 %collective-permute-start.9 = (f32[8,32,128]{2,1,0:T(8,128)S(1)}, f32[8,32,128]{2,1,0:T(8,128)S(1)}, u32[]{:S(2)}, u32[]{:S(2)}) collective-permute-start(f32[8,32,128]{2,1,0:T(8,128)S(1)} %get-tuple-element.51), channel_id=1, source_target_pairs={{0,4},{1,5},{2,6},{3,7},{4,0},{5,1},{6,2},{7,3},{8,12},{9,13},{10,... | collective-permute-start | bytes 393224 | tf_op jit(solution)/shard_map/ppermute | solution.py:338
  74.3 1.2 %collective-permute-start.10 = (f32[8,32,128]{2,1,0:T(8,128)S(1)}, f32[8,32,128]{2,1,0:T(8,128)S(1)}, u32[]{:S(2)}, u32[]{:S(2)}) collective-permute-start(f32[8,32,128]{2,1,0:T(8,128)S(1)} %get-tuple-element.52), channel_id=1, source_target_pairs={{0,6},{1,7},{2,0},{3,1},{4,2},{5,3},{6,4},{7,5},{8,14},{9,15},{10,... | collective-permute-start | bytes 393224 | tf_op jit(solution)/shard_map/ppermute | solution.py:338
  75.5 0.9 %collective-permute-done.8.b = f32[8,32,128]{2,1,0:T(8,128)S(1)} collective-permute-done((f32[8,32,128]{2,1,0:T(8,128)S(1)}, f32[8,32,128]{2,1,0:T(8,128)S(1)}, u32[]{:S(2)}, u32[]{:S(2)}) %collective-permute-start.8) | collective-permute-done | bytes 131104 | tf_op jit(solution)/shard_map/ppermute | solution.py:338
  76.4 4.0 %collective-permute-done.9.c = f32[8,32,128]{2,1,0:T(8,128)S(1)} collective-permute-done((f32[8,32,128]{2,1,0:T(8,128)S(1)}, f32[8,32,128]{2,1,0:T(8,128)S(1)}, u32[]{:S(2)}, u32[]{:S(2)}) %collective-permute-start.9) | collective-permute-done | bytes 131104 | tf_op jit(solution)/shard_map/ppermute | solution.py:338
  80.3 0.7 last.1
  (35 shorter events, 0.3 us)
Async XLA Ops:
  1.6 12.1 %copy-start.10 = (s32[64]{0:T(128)S(1)}, s32[64]{0:T(128)}, u32[]{:S(2)}) copy-start(s32[64]{0:T(128)} %param.18) | copy-start | bytes 772
  1.6 12.1 %copy-start.11 = (s32[32]{0:T(128)S(1)}, s32[32]{0:T(128)}, u32[]{:S(2)}) copy-start(s32[32]{0:T(128)} %param.20) | copy-start | bytes 388
  1.6 12.5 %copy-start.9 = (s32[64,2]{0,1:T(2,128)S(1)}, s32[64,2]{0,1:T(2,128)}, u32[]{:S(2)}) copy-start(s32[64,2]{0,1:T(2,128)} %param.17) | copy-start | bytes 1540
  1.6 13.1 %copy-start = (f32[2,64,8,128]{3,2,1,0:T(8,128)S(1)}, f32[2,64,8,128]{3,2,1,0:T(8,128)}, u32[]{:S(2)}) copy-start(f32[2,64,8,128]{3,2,1,0:T(8,128)} %vis.1) | copy-start | bytes 1572868
  1.7 13.1 %copy-start.4 = (f32[2,64,128]{2,1,0:T(8,128)S(1)}, f32[2,64,128]{2,1,0:T(8,128)}, u32[]{:S(2)}) copy-start(f32[2,64,128]{2,1,0:T(8,128)} %coord.1) | copy-start | bytes 196612
  1.7 28.3 %all-to-all-start = ((f32[32,1,4096]{2,1,0:T(1,128)}), f32[32,1,4096]{2,1,0:T(1,128)S(1)}, u32[]{:S(2)}, u32[]{:S(2)}) async-start(f32[32,1,4096]{2,1,0:T(1,128)} %bitcast.19), calls=%async_computation | async-start | bytes 1048576 | tf_op jit(solution)/shard_map/all_to_all | solution.py:355
  14.0 0.7 copy-start.8
  14.7 0.7 copy-start.7
  16.0 8.5 %collective-permute-start.1 = (f32[2,17,8,128]{3,2,1,0:T(8,128)S(1)}, f32[2,17,8,128]{3,2,1,0:T(8,128)S(1)}, u32[]{:S(2)}, u32[]{:S(2)}) collective-permute-start(f32[2,17,8,128]{3,2,1,0:T(8,128)S(1)} %get-tuple-element.34), channel_id=1, source_target_pairs={{0,2},{1,3},{2,4},{3,5},{4,6},{5,7},{6,0},{7,1},{8,10},{9,11},{10,... | collective-permute-start | bytes 417800 | tf_op jit(solution)/shard_map/ppermute | solution.py:338
  17.4 7.2 %collective-permute-start.2 = (f32[2,17,8,128]{3,2,1,0:T(8,128)S(1)}, f32[2,17,8,128]{3,2,1,0:T(8,128)S(1)}, u32[]{:S(2)}, u32[]{:S(2)}) collective-permute-start(f32[2,17,8,128]{3,2,1,0:T(8,128)S(1)} %get-tuple-element.35), channel_id=1, source_target_pairs={{0,6},{1,7},{2,0},{3,1},{4,2},{5,3},{6,4},{7,5},{8,14},{9,15},{10,... | collective-permute-start | bytes 417800 | tf_op jit(solution)/shard_map/ppermute | solution.py:338
  18.9 3.1 %collective-permute-start = (f32[17,8,128]{2,1,0:T(8,128)S(1)}, f32[17,8,128]{2,1,0:T(8,128)S(1)}, u32[]{:S(2)}, u32[]{:S(2)}) collective-permute-start(f32[17,8,128]{2,1,0:T(8,128)S(1)} %get-tuple-element.33), channel_id=1, source_target_pairs={{0,1},{1,0},{2,3},{3,2},{4,5},{5,4},{6,7},{7,6},{8,9},{9,8},{10,11... | collective-permute-start | bytes 208904 | tf_op jit(solution)/shard_map/ppermute | solution.py:338
  20.2 7.5 %collective-permute-start.5 = (f32[2,17,8,128]{3,2,1,0:T(8,128)S(1)}, f32[2,17,8,128]{3,2,1,0:T(8,128)S(1)}, u32[]{:S(2)}, u32[]{:S(2)}) collective-permute-start(f32[2,17,8,128]{3,2,1,0:T(8,128)S(1)} %get-tuple-element.39), channel_id=1, source_target_pairs={{0,4},{1,5},{2,6},{3,7},{4,0},{5,1},{6,2},{7,3},{8,12},{9,13},{10,... | collective-permute-start | bytes 417800 | tf_op jit(solution)/shard_map/ppermute | solution.py:338
  24.5 13.8 %collective-permute-start.3 = (f32[2,17,8,128]{3,2,1,0:T(8,128)S(1)}, f32[2,17,8,128]{3,2,1,0:T(8,128)S(1)}, u32[]{:S(2)}, u32[]{:S(2)}) collective-permute-start(f32[2,17,8,128]{3,2,1,0:T(8,128)S(1)} %collective-permute-done.1.refs_0_), channel_id=1, source_target_pairs={{0,1},{1,0},{2,3},{3,2},{4,5},{5,4},{6,7},{7,6},{8,9},{9,8},{10,11... | collective-permute-start | bytes 417800 | tf_op jit(solution)/shard_map/ppermute | solution.py:338
  24.9 13.4 %collective-permute-start.4 = (f32[2,17,8,128]{3,2,1,0:T(8,128)S(1)}, f32[2,17,8,128]{3,2,1,0:T(8,128)S(1)}, u32[]{:S(2)}, u32[]{:S(2)}) collective-permute-start(f32[2,17,8,128]{3,2,1,0:T(8,128)S(1)} %collective-permute-done.2.refs_1_), channel_id=1, source_target_pairs={{0,1},{1,0},{2,3},{3,2},{4,5},{5,4},{6,7},{7,6},{8,9},{9,8},{10,11... | collective-permute-start | bytes 417800 | tf_op jit(solution)/shard_map/ppermute | solution.py:338
  25.1 4.8 %copy-start.6 = (f32[8,128]{1,0:T(8,128)S(1)}, f32[8,128]{1,0:T(8,128)}, u32[]{:S(2)}) copy-start(f32[8,128]{1,0:T(8,128)} %constant.18.clone.taper) | copy-start | bytes 12292
  27.7 10.6 %collective-permute-start.6 = (f32[2,17,8,128]{3,2,1,0:T(8,128)S(1)}, f32[2,17,8,128]{3,2,1,0:T(8,128)S(1)}, u32[]{:S(2)}, u32[]{:S(2)}) collective-permute-start(f32[2,17,8,128]{3,2,1,0:T(8,128)S(1)} %collective-permute-done.5.refs_2_), channel_id=1, source_target_pairs={{0,1},{1,0},{2,3},{3,2},{4,5},{5,4},{6,7},{7,6},{8,9},{9,8},{10,11... | collective-permute-start | bytes 417800 | tf_op jit(solution)/shard_map/ppermute | solution.py:338
  31.4 11.8 %all-to-all-start.1 = ((f32[8,1,2048]{2,1,0:T(1,128)}), f32[8,1,2048]{2,1,0:T(1,128)S(1)}, u32[]{:S(2)}, u32[]{:S(2)}) async-start(f32[8,1,2048]{2,1,0:T(1,128)} %bitcast.7), calls=%async_computation.1 | async-start | bytes 131072 | tf_op jit(solution)/shard_map/all_to_all | solution.py:402
  38.3 4.9 %copy-start.1 = (bf16[384,128]{1,0:T(8,128)(2,1)S(1)}, bf16[384,128]{1,0:T(8,128)(2,1)}, u32[]{:S(2)}) copy-start(bf16[384,128]{1,0:T(8,128)(2,1)} %constant.22.clone.right3) | copy-start | bytes 294916
  38.3 4.9 %copy-start.2 = (bf16[2,128,128]{2,1,0:T(8,128)(2,1)S(1)}, bf16[2,128,128]{2,1,0:T(8,128)(2,1)}, u32[]{:S(2)}) copy-start(bf16[2,128,128]{2,1,0:T(8,128)(2,1)} %constant.20.clone.fold) | copy-start | bytes 196612
  38.3 4.9 %copy-start.3 = (bf16[256,128]{1,0:T(8,128)(2,1)S(1)}, bf16[256,128]{1,0:T(8,128)(2,1)}, u32[]{:S(2)}) copy-start(bf16[256,128]{1,0:T(8,128)(2,1)} %constant.19.clone.to_image) | copy-start | bytes 196612
  38.3 4.9 %copy-start.5 = (bf16[32,192]{1,0:T(8,128)(2,1)S(1)}, bf16[32,192]{1,0:T(8,128)(2,1)}, u32[]{:S(2)}) copy-start(bf16[32,192]{1,0:T(8,128)(2,1)} %constant.21.clone.left3) | copy-start | bytes 36868
  66.3 4.0 %collective-permute-start.7 = (f32[4,8,32,128]{3,2,1,0:T(8,128)S(1)}, f32[4,8,32,128]{3,2,1,0:T(8,128)S(1)}, u32[]{:S(2)}, u32[]{:S(2)}) collective-permute-start(f32[4,8,32,128]{3,2,1,0:T(8,128)S(1)} %get-tuple-element.48), channel_id=1, source_target_pairs={{0,1},{1,0},{2,3},{3,2},{4,5},{5,4},{6,7},{7,6},{8,9},{9,8},{10,11... | collective-permute-start | bytes 1572872 | tf_op jit(solution)/shard_map/ppermute | solution.py:338
  70.4 6.0 %collective-permute-start.8 = (f32[8,32,128]{2,1,0:T(8,128)S(1)}, f32[8,32,128]{2,1,0:T(8,128)S(1)}, u32[]{:S(2)}, u32[]{:S(2)}) collective-permute-start(f32[8,32,128]{2,1,0:T(8,128)S(1)} %get-tuple-element.50), channel_id=1, source_target_pairs={{0,2},{1,3},{2,4},{3,5},{4,6},{5,7},{6,0},{7,1},{8,10},{9,11},{10,... | collective-permute-start | bytes 393224 | tf_op jit(solution)/shard_map/ppermute | solution.py:338
  71.9 8.4 %collective-permute-start.9 = (f32[8,32,128]{2,1,0:T(8,128)S(1)}, f32[8,32,128]{2,1,0:T(8,128)S(1)}, u32[]{:S(2)}, u32[]{:S(2)}) collective-permute-start(f32[8,32,128]{2,1,0:T(8,128)S(1)} %get-tuple-element.51), channel_id=1, source_target_pairs={{0,4},{1,5},{2,6},{3,7},{4,0},{5,1},{6,2},{7,3},{8,12},{9,13},{10,... | collective-permute-start | bytes 393224 | tf_op jit(solution)/shard_map/ppermute | solution.py:338
  74.3 6.0 %collective-permute-start.10 = (f32[8,32,128]{2,1,0:T(8,128)S(1)}, f32[8,32,128]{2,1,0:T(8,128)S(1)}, u32[]{:S(2)}, u32[]{:S(2)}) collective-permute-start(f32[8,32,128]{2,1,0:T(8,128)S(1)} %get-tuple-element.52), channel_id=1, source_target_pairs={{0,6},{1,7},{2,0},{3,1},{4,2},{5,3},{6,4},{7,5},{8,14},{9,15},{10,... | collective-permute-start | bytes 393224 | tf_op jit(solution)/shard_map/ppermute | solution.py:338
